TPU v7x, 32 devices: a whole 2x2x4 slice. The times are simulated.
32 devices in a mesh: kx: 8 (over z, core), ky: 4 (over y, x).
Axes of the slice: x: 2, y: 2, z: 4, core: 2. Of those that a mesh axis runs over, the one named last changes fastest.
Arguments:
- kspace: bfloat16 [64, 16, 64, 256], P(None, 'kx', 'ky'), may hold values from -6 to 6
- kernel: bfloat16 [3, 3, 3, 64, 128], replicated, may hold values from -0.109375 to 0.109375
- mask: int32 [64, 256], P('ky'), may hold values 0 or 1
Outputs:
- updated: bfloat16 [64, 16, 64, 256], P(None, 'kx', 'ky')
- residual: bfloat16 [64, 16, 64, 256], P(None, 'kx', 'ky')
All inputs are finite; a program needn't handle non-finite values. No bound on the sum of `mask` on one device may be relied on, other than what follows from the above.
Results may differ from a plain program's by a relative error of at most 0.0042.
Values may be sent and summed in bfloat16 or wider, within the bound.
No kernel may reach another device: no remote copies, remote signals or barrier semaphores. Data moves between devices by JAX's collectives and lax.ppermute only.
A program may use at most 128 MiB of HBM per device.

v0:
```python
import jax
import jax.numpy as jnp
from jax import lax
from jax.sharding import PartitionSpec as P

step_size = 0.5


def from_partner(value, axis, stride):
    mask = 2**stride
    pairs = [(source, source ^ mask) for source in range(lax.axis_size(axis))]
    return lax.ppermute(value, axis, pairs)


def extended_2(shard, sides, width):
    for axis, dim in sides:
        count, length = (lax.axis_size(axis), shard.shape[dim])
        up = [(i, (i + 1) % count) for i in range(count - 1)]
        down = [(j, i) for i, j in up]
        last = lax.slice_in_dim(shard, length - width, length, axis=dim)
        initial = lax.slice_in_dim(shard, 0, width, axis=dim)
        before = lax.ppermute(last, axis, up)
        after = lax.ppermute(initial, axis, down)
        shard = jnp.concatenate([before, shard, after], axis=dim)
    return shard


def channel_signs(count):
    half = count // 2
    return jnp.concatenate(
        [jnp.ones((half,), jnp.float32), -jnp.ones((count - half,), jnp.float32)]
    )


def flip_cells(block):
    return block[:, ::-1, ::-1, ::-1]


def pad_depth(block):
    return jnp.pad(block, ((0, 0), (0, 0), (0, 0), (1, 1)))


def swap_bits(block):
    result = flip_cells(block)
    for bit in range(lax.axis_size("kx").bit_length() - 1):
        result = from_partner(result, "kx", bit)
    for bit in range(lax.axis_size("ky").bit_length() - 1):
        result = from_partner(result, "ky", bit)
    return result


def return_bits(block):
    result = flip_cells(block)
    for bit in range(lax.axis_size("kx").bit_length() - 1):
        result = from_partner(result, "kx", bit)
    for bit in range(lax.axis_size("ky").bit_length() - 1):
        result = from_partner(result, "ky", bit)
    return result


def forward_terms(padded, weights):
    rows = padded.shape[1] - 2
    cols = padded.shape[2] - 2
    depth = padded.shape[3] - 2
    stacked = jnp.concatenate(
        [padded[:, :, :, third : third + depth] for third in range(3)], axis=0
    )
    total = None
    for first in range(3):
        for second in range(3):
            taps = weights[first, second]
            joined = jnp.transpose(taps, (1, 0, 2)).reshape((taps.shape[1], -1))
            window = stacked[:, first : first + rows, second : second + cols, :]
            term = jnp.einsum("oi,ixyz->oxyz", joined, window, preferred_element_type=jnp.float32)
            total = term if total is None else total + term
    return total


def adjoint_terms(padded, weights):
    rows = padded.shape[1] - 2
    cols = padded.shape[2] - 2
    depth = padded.shape[3] - 2
    stacked = jnp.concatenate(
        [padded[:, :, :, 2 - third : 2 - third + depth] for third in range(3)], axis=0
    )
    total = None
    for first in range(3):
        for second in range(3):
            taps = weights[first, second]
            joined = taps.reshape((-1, taps.shape[2]))
            window = stacked[:, 2 - first : 2 - first + rows, 2 - second : 2 - second + cols, :]
            term = jnp.einsum("ji,jxyz->ixyz", joined, window, preferred_element_type=jnp.float32)
            total = term if total is None else total + term
    return total


def local(kspace, kernel, mask):
    chans = kspace.shape[0]
    signs = channel_signs(chans)[:, None, None, None]
    turned = swap_bits(kspace)
    virtual = (signs * turned.astype(jnp.float32)).astype(jnp.bfloat16)
    extended = jnp.concatenate([kspace, virtual], axis=0)
    padded = pad_depth(extended_2(extended, (("kx", 1), ("ky", 2)), 1))
    residual = (forward_terms(padded, kernel) - kspace.astype(jnp.float32)).astype(jnp.bfloat16)
    beside_all = pad_depth(extended_2(residual, (("kx", 1), ("ky", 2)), 1))
    adjoint = adjoint_terms(beside_all, kernel)
    direct = adjoint[:chans]
    back = adjoint[chans:].astype(jnp.bfloat16)
    mirrored_back = return_bits(back)
    gradient = direct - residual.astype(jnp.float32) + signs * mirrored_back.astype(jnp.float32)
    keep = 1.0 - mask.astype(jnp.float32)
    updated = (kspace.astype(jnp.float32) - step_size * keep[None, None] * gradient).astype(
        jnp.bfloat16
    )
    return (updated, residual)


def solution(mesh):
    return jax.shard_map(
        local,
        mesh=mesh,
        in_specs=(P(None, "kx", "ky", None), P(), P("ky", None)),
        out_specs=(P(None, "kx", "ky", None), P(None, "kx", "ky", None)),
        check_vma=False,
    )
```

profile of v0, /device:TPU:24, one launch (start us, length us, event | category | flops | bytes accessed | tf_op | source)
XLA Modules:
  0.0 435.9 jit_solution(7079194647623524287)
XLA Ops:
  0.6 1.8 copy.19
  3.5 2.6 collective-permute-done
  6.6 24.8 %collective-permute-done.1 = bf16[64,2,16,256]{3,0,2,1:T(8,128)(2,1)S(1)} collective-permute-done((bf16[64,2,16,256]{3,0,2,1:T(8,128)(2,1)S(1)}, bf16[64,2,16,256]{3,0,2,1:T(8,128)(2,1)S(1)}, u32[]{:S(2)}, u32[]{:S(2)}) %collective-permute-start.1) | collective-permute-done | bytes 1048608 | tf_op jit(solution)/shard_map/ppermute | solution.py:12
  31.7 47.3 %collective-permute-done.2 = bf16[64,2,16,256]{3,0,2,1:T(8,128)(2,1)S(1)} collective-permute-done((bf16[64,2,16,256]{3,0,2,1:T(8,128)(2,1)S(1)}, bf16[64,2,16,256]{3,0,2,1:T(8,128)(2,1)S(1)}, u32[]{:S(2)}, u32[]{:S(2)}) %collective-permute-start.2) | collective-permute-done | bytes 1048608 | tf_op jit(solution)/shard_map/ppermute | solution.py:12
  80.4 23.6 %collective-permute-done.3 = bf16[64,2,16,256]{3,0,2,1:T(8,128)(2,1)S(1)} collective-permute-done((bf16[64,2,16,256]{3,0,2,1:T(8,128)(2,1)S(1)}, bf16[64,2,16,256]{3,0,2,1:T(8,128)(2,1)S(1)}, u32[]{:S(2)}, u32[]{:S(2)}) %collective-permute-start.3) | collective-permute-done | bytes 1048608 | tf_op jit(solution)/shard_map/ppermute | solution.py:12
  105.5 22.7 %collective-permute-done.4 = bf16[64,2,16,256]{3,0,2,1:T(8,128)(2,1)S(1)} collective-permute-done((bf16[64,2,16,256]{3,0,2,1:T(8,128)(2,1)S(1)}, bf16[64,2,16,256]{3,0,2,1:T(8,128)(2,1)S(1)}, u32[]{:S(2)}, u32[]{:S(2)}) %collective-permute-start.4) | collective-permute-done | bytes 1048608 | tf_op jit(solution)/shard_map/ppermute | solution.py:12
  129.5 1.9 collective-permute-start.5
  131.5 3.6 collective-permute-start.6
  135.1 10.5 %collective-permute-done.5 = bf16[128,1,16,256]{3,0,2,1:T(8,128)(2,1)S(1)} collective-permute-done((bf16[128,1,16,256]{3,0,2,1:T(8,128)(2,1)S(1)}, bf16[128,1,16,256]{3,0,2,1:T(8,128)(2,1)S(1)}, u32[]{:S(2)}, u32[]{:S(2)}) %collective-permute-start.5) | collective-permute-done | bytes 1048608 | tf_op jit(solution)/shard_map/ppermute | solution.py:22
  145.6 1.8 collective-permute-done.6
  149.2 3.4 collective-permute-start.7
  167.0 13.1 %select_maximum_fusion = bf16[128,4,18,258]{3,0,2,1:T(8,128)(2,1)} fusion(bf16[128,4,1,256]{3,0,2,1:T(8,128)(2,1)} %collective-permute-done.8, bf16[128,4,1,256]{3,0,2,1:T(8,128)(2,1)S(1)} %collective-permute-done.7, bf16[128,1,16,256]{3,0,2,1:T(8,128)(2,1)} %copy-done, bf16[128,1,16,256]{3,0,2,1:T(8,128)(2,1)S(1)} %collective-permute-done.5, ...), kind=kLoop, calls=%fused_computation.6 | loop fusion | flops 49932288 | bytes 9474048 | tf_op jit(solution)/shard_map/concatenate | solution.py:24
  180.1 10.7 %fusion.50 = (bf16[128,4,18,256]{3,0,2,1:T(8,128)(2,1)}, bf16[128,4,18,256]{3,0,2,1:T(8,128)(2,1)}) fusion(bf16[128,4,18,258]{3,0,2,1:T(8,128)(2,1)} %select_maximum_fusion), kind=kLoop, calls=%fused_computation.82 | loop fusion | bytes 18874368 | tf_op jit(solution)/shard_map/slice | solution.py:66
  190.8 16.1 %pad_maximum_fusion = bf16[384,4,18,256]{3,0,2,1:T(8,128)(2,1)S(1)} fusion(bf16[128,4,18,256]{3,0,2,1:T(8,128)(2,1)} %get-tuple-element.7, bf16[128,4,1,256]{3,0,2,1:T(8,128)(2,1)} %collective-permute-done.8, bf16[128,1,16,256]{3,0,2,1:T(8,128)(2,1)S(1)} %copy-done.1, bf16[64,2,16,256]{3,0,2,1:T(8,128)(2,1)S(1)} %multiply_convert_fusion, ...), kind=kLoop, calls=%fused_computation.2 | loop fusion | flops 113246208 | bytes 28311552 | tf_op jit(solution)/shard_map/concatenate | solution.py:65
  209.5 2.6 fusion.15
  212.1 2.6 fusion.17
  214.7 2.6 fusion.19
  217.4 2.7 fusion.21
  220.0 2.6 fusion.23
  222.6 2.6 fusion.25
  225.3 5.9 %fusion.32 = bf16[64,2,16,256]{3,0,2,1:T(8,128)(2,1)S(1)} fusion(f32[2,16,256,64]{2,3,1,0:T(8,128)S(1)} %fusion.11, f32[2,16,256,64]{2,3,1,0:T(8,128)S(1)} %fusion.13, f32[2,16,256,64]{2,3,1,0:T(8,128)} %fusion.15, f32[2,16,256,64]{2,3,1,0:T(8,128)} %fusion.17, f32[2,16,256,64]{2,3,1,0:T(8,128)} %fusion.19, f32[2,16,256,64]{2,3,1,0:T(8,128)} %fusion.21, ...), kind=kOutput, calls=%fused_computation.45 | convolution fusion | flops 408420352 | bytes 25214976 | tf_op jit(solution)/shard_map/oi,ixyz->oxyz/dot_general | solution.py:74
  231.3 3.5 collective-permute-start.10
  234.8 1.9 collective-permute-start.9
  236.8 4.7 %collective-permute-done.10 = bf16[64,1,16,256]{3,0,2,1:T(8,128)(2,1)S(1)} collective-permute-done((bf16[64,1,16,256]{3,0,2,1:T(8,128)(2,1)S(1)}, bf16[64,1,16,256]{3,0,2,1:T(8,128)(2,1)S(1)}, u32[]{:S(2)}, u32[]{:S(2)}) %collective-permute-start.10) | collective-permute-done | bytes 524320 | tf_op jit(solution)/shard_map/ppermute | solution.py:23
  241.5 3.8 collective-permute-done.9
  245.4 4.3 collective-permute-start.11
  252.2 4.7 %collective-permute-done.12 = bf16[64,4,1,256]{3,0,2,1:T(8,128)(2,1)S(1)} collective-permute-done((bf16[64,4,1,256]{3,0,2,1:T(8,128)(2,1)S(1)}, bf16[64,4,1,256]{3,0,2,1:T(8,128)(2,1)S(1)}, u32[]{:S(2)}, u32[]{:S(2)}) %collective-permute-start.12) | collective-permute-done | bytes 131104 | tf_op jit(solution)/shard_map/ppermute | solution.py:23
  256.9 4.1 select_maximum_fusion.2
  262.5 2.7 pad_maximum_fusion.1
  265.2 2.7 fusion.54
  268.0 2.8 fusion.55
  270.8 2.8 fusion.56
  273.6 2.7 fusion.57
  276.3 2.7 fusion.58
  279.0 2.8 fusion.59
  281.8 2.8 fusion.60
  284.6 2.7 fusion.61
  287.3 14.1 %add_bitcast_fusion = f32[128,2,16,256]{3,0,2,1:T(8,128)} fusion(f32[2,16,256,128]{2,3,1,0:T(8,128)} %fusion.61, f32[2,16,256,128]{2,3,1,0:T(8,128)} %fusion.60, f32[2,16,256,128]{2,3,1,0:T(8,128)} %fusion.59, f32[2,16,256,128]{2,3,1,0:T(8,128)} %fusion.58, f32[2,16,256,128]{2,3,1,0:T(8,128)} %fusion.57, f32[2,16,256,128]{2,3,1,0:T(8,128)} %fusion.56, ...), kind=kOutput, calls=%fused_computation.35 | convolution fusion | flops 411041792 | bytes 44875776 | tf_op jit(solution)/shard_map/ji,jxyz->ixyz/dot_general | solution.py:92
  301.4 1.7 slice.238
  303.2 2.0 rev.7
  305.2 2.9 collective-permute-done.13
  308.1 25.2 %collective-permute-done.14 = bf16[64,2,16,256]{3,0,2,1:T(8,128)(2,1)S(1)} collective-permute-done((bf16[64,2,16,256]{3,0,2,1:T(8,128)(2,1)S(1)}, bf16[64,2,16,256]{3,0,2,1:T(8,128)(2,1)S(1)}, u32[]{:S(2)}, u32[]{:S(2)}) %collective-permute-start.14) | collective-permute-done | bytes 1048608 | tf_op jit(solution)/shard_map/ppermute | solution.py:12
  333.3 47.7 %collective-permute-done.15 = bf16[64,2,16,256]{3,0,2,1:T(8,128)(2,1)S(1)} collective-permute-done((bf16[64,2,16,256]{3,0,2,1:T(8,128)(2,1)S(1)}, bf16[64,2,16,256]{3,0,2,1:T(8,128)(2,1)S(1)}, u32[]{:S(2)}, u32[]{:S(2)}) %collective-permute-start.15) | collective-permute-done | bytes 1048608 | tf_op jit(solution)/shard_map/ppermute | solution.py:12
  381.0 2.9 collective-permute-start.16
  383.9 23.3 %collective-permute-done.16 = bf16[64,2,16,256]{3,0,2,1:T(8,128)(2,1)S(1)} collective-permute-done((bf16[64,2,16,256]{3,0,2,1:T(8,128)(2,1)S(1)}, bf16[64,2,16,256]{3,0,2,1:T(8,128)(2,1)S(1)}, u32[]{:S(2)}, u32[]{:S(2)}) %collective-permute-start.16) | collective-permute-done | bytes 1048608 | tf_op jit(solution)/shard_map/ppermute | solution.py:12
  409.5 22.3 %collective-permute-done.17 = bf16[64,2,16,256]{3,0,2,1:T(8,128)(2,1)S(1)} collective-permute-done((bf16[64,2,16,256]{3,0,2,1:T(8,128)(2,1)S(1)}, bf16[64,2,16,256]{3,0,2,1:T(8,128)(2,1)S(1)}, u32[]{:S(2)}, u32[]{:S(2)}) %collective-permute-start.17) | collective-permute-done | bytes 1048608 | tf_op jit(solution)/shard_map/ppermute | solution.py:12
  431.7 2.6 fusion.33
  434.4 1.6 copy.31
  (90 shorter events, 31.2 us)
Async XLA Ops:
  3.4 150.5 %copy-start.3 = (bf16[3,3,3,64,128]{4,3,2,1,0:T(8,128)(2,1)S(1)}, bf16[3,3,3,64,128]{4,3,2,1,0:T(8,128)(2,1)}, u32[]{:S(2)}) copy-start(bf16[3,3,3,64,128]{4,3,2,1,0:T(8,128)(2,1)} %param.4) | copy-start | bytes 1327108
  3.4 2.7 collective-permute-start
  6.1 25.2 %collective-permute-start.1 = (bf16[64,2,16,256]{3,0,2,1:T(8,128)(2,1)S(1)}, bf16[64,2,16,256]{3,0,2,1:T(8,128)(2,1)S(1)}, u32[]{:S(2)}, u32[]{:S(2)}) collective-permute-start(bf16[64,2,16,256]{3,0,2,1:T(8,128)(2,1)S(1)} %collective-permute-done), channel_id=1, source_target_pairs={{0,8},{4,12},{8,0},{12,4},{16,24},{20,28},{24,16},{28,20},{1,9},{5... | collective-permute-start | bytes 3145736 | tf_op jit(solution)/shard_map/ppermute | solution.py:12
  31.3 47.6 %collective-permute-start.2 = (bf16[64,2,16,256]{3,0,2,1:T(8,128)(2,1)S(1)}, bf16[64,2,16,256]{3,0,2,1:T(8,128)(2,1)S(1)}, u32[]{:S(2)}, u32[]{:S(2)}) collective-permute-start(bf16[64,2,16,256]{3,0,2,1:T(8,128)(2,1)S(1)} %collective-permute-done.1), channel_id=1, source_target_pairs={{0,16},{4,20},{8,24},{12,28},{16,0},{20,4},{24,8},{28,12},{1,17},{... | collective-permute-start | bytes 3145736 | tf_op jit(solution)/shard_map/ppermute | solution.py:12
  78.9 25.1 %collective-permute-start.3 = (bf16[64,2,16,256]{3,0,2,1:T(8,128)(2,1)S(1)}, bf16[64,2,16,256]{3,0,2,1:T(8,128)(2,1)S(1)}, u32[]{:S(2)}, u32[]{:S(2)}) collective-permute-start(bf16[64,2,16,256]{3,0,2,1:T(8,128)(2,1)S(1)} %collective-permute-done.2), channel_id=1, source_target_pairs={{0,1},{1,0},{2,3},{3,2},{4,5},{5,4},{6,7},{7,6},{8,9},{9,8},{10,11... | collective-permute-start | bytes 3145736 | tf_op jit(solution)/shard_map/ppermute | solution.py:12
  104.0 24.2 %collective-permute-start.4 = (bf16[64,2,16,256]{3,0,2,1:T(8,128)(2,1)S(1)}, bf16[64,2,16,256]{3,0,2,1:T(8,128)(2,1)S(1)}, u32[]{:S(2)}, u32[]{:S(2)}) collective-permute-start(bf16[64,2,16,256]{3,0,2,1:T(8,128)(2,1)S(1)} %collective-permute-done.3), channel_id=1, source_target_pairs={{0,2},{1,3},{2,0},{3,1},{4,6},{5,7},{6,4},{7,5},{8,10},{9,11},{10,... | collective-permute-start | bytes 3145736 | tf_op jit(solution)/shard_map/ppermute | solution.py:12
  129.5 16.1 %collective-permute-start.5 = (bf16[128,1,16,256]{3,0,2,1:T(8,128)(2,1)S(1)}, bf16[128,1,16,256]{3,0,2,1:T(8,128)(2,1)S(1)}, u32[]{:S(2)}, u32[]{:S(2)}) collective-permute-start(bf16[128,1,16,256]{3,0,2,1:T(8,128)(2,1)S(1)} %get-tuple-element.14), channel_id=1, source_target_pairs={{0,4},{4,8},{8,12},{12,16},{16,20},{20,24},{24,28},{1,5},{5,9},{9,... | collective-permute-start | bytes 3145736 | tf_op jit(solution)/shard_map/ppermute | solution.py:22
  131.5 15.9 %collective-permute-start.6 = (bf16[128,1,16,256]{3,0,2,1:T(8,128)(2,1)S(1)}, bf16[128,1,16,256]{3,0,2,1:T(8,128)(2,1)S(1)}, u32[]{:S(2)}, u32[]{:S(2)}) collective-permute-start(bf16[128,1,16,256]{3,0,2,1:T(8,128)(2,1)S(1)} %get-tuple-element.15), channel_id=1, source_target_pairs={{4,0},{8,4},{12,8},{16,12},{20,16},{24,20},{28,24},{5,1},{9,5},{13... | collective-permute-start | bytes 3145736 | tf_op jit(solution)/shard_map/ppermute | solution.py:23
  147.4 1.0 copy-start
  149.2 17.8 %collective-permute-start.7 = (bf16[128,4,1,256]{3,0,2,1:T(8,128)(2,1)}, bf16[128,4,1,256]{3,0,2,1:T(8,128)(2,1)S(1)}, u32[]{:S(2)}, u32[]{:S(2)}) collective-permute-start(bf16[128,4,1,256]{3,0,2,1:T(8,128)(2,1)} %get-tuple-element.8), channel_id=1, source_target_pairs={{0,1},{1,2},{2,3},{4,5},{5,6},{6,7},{8,9},{9,10},{10,11},{12,13},{... | collective-permute-start | bytes 786440 | tf_op jit(solution)/shard_map/ppermute | solution.py:22
  152.6 14.4 %collective-permute-start.8 = (bf16[128,4,1,256]{3,0,2,1:T(8,128)(2,1)}, bf16[128,4,1,256]{3,0,2,1:T(8,128)(2,1)}, u32[]{:S(2)}, u32[]{:S(2)}) collective-permute-start(bf16[128,4,1,256]{3,0,2,1:T(8,128)(2,1)} %get-tuple-element.9), channel_id=1, source_target_pairs={{1,0},{2,1},{3,2},{5,4},{6,5},{7,6},{9,8},{10,9},{11,10},{13,12},{... | collective-permute-start | bytes 786440 | tf_op jit(solution)/shard_map/ppermute | solution.py:23
  180.1 10.7 %copy-start.1 = (bf16[128,1,16,256]{3,0,2,1:T(8,128)(2,1)S(1)}, bf16[128,1,16,256]{3,0,2,1:T(8,128)(2,1)}, u32[]{:S(2)}) copy-start(bf16[128,1,16,256]{3,0,2,1:T(8,128)(2,1)} %copy-done) | copy-start | bytes 3145732
  206.9 1.3 copy-start.4
  208.2 1.3 copy-start.5
  209.5 2.6 copy-start.6
  212.1 2.6 copy-start.7
  214.7 2.6 copy-start.8
  217.4 2.7 copy-start.9
  220.0 2.6 copy-start.10
  222.6 2.6 copy-start.2
  222.6 2.6 copy-start.19
  231.3 10.2 %collective-permute-start.10 = (bf16[64,1,16,256]{3,0,2,1:T(8,128)(2,1)S(1)}, bf16[64,1,16,256]{3,0,2,1:T(8,128)(2,1)S(1)}, u32[]{:S(2)}, u32[]{:S(2)}) collective-permute-start(bf16[64,1,16,256]{3,0,2,1:T(8,128)(2,1)S(1)} %get-tuple-element.17), channel_id=1, source_target_pairs={{4,0},{8,4},{12,8},{16,12},{20,16},{24,20},{28,24},{5,1},{9,5},{13... | collective-permute-start | bytes 1572872 | tf_op jit(solution)/shard_map/ppermute | solution.py:23
  234.8 10.5 %collective-permute-start.9 = (bf16[64,1,16,256]{3,0,2,1:T(8,128)(2,1)S(1)}, bf16[64,1,16,256]{3,0,2,1:T(8,128)(2,1)S(1)}, u32[]{:S(2)}, u32[]{:S(2)}) collective-permute-start(bf16[64,1,16,256]{3,0,2,1:T(8,128)(2,1)S(1)} %get-tuple-element.16), channel_id=1, source_target_pairs={{0,4},{4,8},{8,12},{12,16},{16,20},{20,24},{24,28},{1,5},{5,9},{9,... | collective-permute-start | bytes 1572872 | tf_op jit(solution)/shard_map/ppermute | solution.py:22
  245.4 6.8 %collective-permute-start.11 = (bf16[64,4,1,256]{3,0,2,1:T(8,128)(2,1)S(1)}, bf16[64,4,1,256]{3,0,2,1:T(8,128)(2,1)S(1)}, u32[]{:S(2)}, u32[]{:S(2)}) collective-permute-start(bf16[64,4,1,256]{3,0,2,1:T(8,128)(2,1)S(1)} %get-tuple-element.12), channel_id=1, source_target_pairs={{0,1},{1,2},{2,3},{4,5},{5,6},{6,7},{8,9},{9,10},{10,11},{12,13},{... | collective-permute-start | bytes 393224 | tf_op jit(solution)/shard_map/ppermute | solution.py:22
  249.7 7.2 %collective-permute-start.12 = (bf16[64,4,1,256]{3,0,2,1:T(8,128)(2,1)S(1)}, bf16[64,4,1,256]{3,0,2,1:T(8,128)(2,1)S(1)}, u32[]{:S(2)}, u32[]{:S(2)}) collective-permute-start(bf16[64,4,1,256]{3,0,2,1:T(8,128)(2,1)S(1)} %get-tuple-element.13), channel_id=1, source_target_pairs={{1,0},{2,1},{3,2},{5,4},{6,5},{7,6},{9,8},{10,9},{11,10},{13,12},{... | collective-permute-start | bytes 393224 | tf_op jit(solution)/shard_map/ppermute | solution.py:23
  262.5 2.7 copy-start.18
  265.2 2.8 copy-start.17
  265.2 5.5 %copy-start.16 = (bf16[1,1,3,64,128]{4,3,2,1,0:T(8,128)(2,1)S(1)}, bf16[1,1,3,64,128]{4,3,2,1,0:T(8,128)(2,1)}, u32[]{:S(2)}) copy-start(bf16[1,1,3,64,128]{4,3,2,1,0:T(8,128)(2,1)} %get-tuple-element.32) | copy-start | bytes 147460
  268.0 5.6 %copy-start.15 = (bf16[1,1,3,64,128]{4,3,2,1,0:T(8,128)(2,1)S(1)}, bf16[1,1,3,64,128]{4,3,2,1,0:T(8,128)(2,1)}, u32[]{:S(2)}) copy-start(bf16[1,1,3,64,128]{4,3,2,1,0:T(8,128)(2,1)} %get-tuple-element.31) | copy-start | bytes 147460
  270.8 5.5 %copy-start.14 = (bf16[1,1,3,64,128]{4,3,2,1,0:T(8,128)(2,1)S(1)}, bf16[1,1,3,64,128]{4,3,2,1,0:T(8,128)(2,1)}, u32[]{:S(2)}) copy-start(bf16[1,1,3,64,128]{4,3,2,1,0:T(8,128)(2,1)} %get-tuple-element.30) | copy-start | bytes 147460
  273.6 5.4 %copy-start.13 = (bf16[1,1,3,64,128]{4,3,2,1,0:T(8,128)(2,1)S(1)}, bf16[1,1,3,64,128]{4,3,2,1,0:T(8,128)(2,1)}, u32[]{:S(2)}) copy-start(bf16[1,1,3,64,128]{4,3,2,1,0:T(8,128)(2,1)} %get-tuple-element.29) | copy-start | bytes 147460
  276.3 5.5 %copy-start.12 = (bf16[1,1,3,64,128]{4,3,2,1,0:T(8,128)(2,1)S(1)}, bf16[1,1,3,64,128]{4,3,2,1,0:T(8,128)(2,1)}, u32[]{:S(2)}) copy-start(bf16[1,1,3,64,128]{4,3,2,1,0:T(8,128)(2,1)} %get-tuple-element.28) | copy-start | bytes 147460
  279.0 5.6 %copy-start.11 = (bf16[1,1,3,64,128]{4,3,2,1,0:T(8,128)(2,1)S(1)}, bf16[1,1,3,64,128]{4,3,2,1,0:T(8,128)(2,1)}, u32[]{:S(2)}) copy-start(bf16[1,1,3,64,128]{4,3,2,1,0:T(8,128)(2,1)} %get-tuple-element.35) | copy-start | bytes 147460
  281.8 5.5 %copy-start.20 = (bf16[1,1,3,64,128]{4,3,2,1,0:T(8,128)(2,1)S(1)}, bf16[1,1,3,64,128]{4,3,2,1,0:T(8,128)(2,1)}, u32[]{:S(2)}) copy-start(bf16[1,1,3,64,128]{4,3,2,1,0:T(8,128)(2,1)} %get-tuple-element.18) | copy-start | bytes 147460
  287.3 120.6 %copy-start.21 = (s32[16,256]{1,0:T(8,128)S(1)}, s32[16,256]{1,0:T(8,128)}, u32[]{:S(2)}) copy-start(s32[16,256]{1,0:T(8,128)} %param.5) | copy-start | bytes 49156
  301.4 130.3 %copy-start.22 = (f32[64]{0:T(128)S(1)}, f32[64]{0:T(128)}, u32[]{:S(2)}) copy-start(f32[64]{0:T(128)} %constant.8.clone.1) | copy-start | bytes 772
  305.2 2.9 collective-permute-start.13
  308.0 25.2 %collective-permute-start.14 = (bf16[64,2,16,256]{3,0,2,1:T(8,128)(2,1)S(1)}, bf16[64,2,16,256]{3,0,2,1:T(8,128)(2,1)S(1)}, u32[]{:S(2)}, u32[]{:S(2)}) collective-permute-start(bf16[64,2,16,256]{3,0,2,1:T(8,128)(2,1)S(1)} %collective-permute-done.13), channel_id=1, source_target_pairs={{0,8},{4,12},{8,0},{12,4},{16,24},{20,28},{24,16},{28,20},{1,9},{5... | collective-permute-start | bytes 3145736 | tf_op jit(solution)/shard_map/ppermute | solution.py:12
  333.3 47.7 %collective-permute-start.15 = (bf16[64,2,16,256]{3,0,2,1:T(8,128)(2,1)S(1)}, bf16[64,2,16,256]{3,0,2,1:T(8,128)(2,1)S(1)}, u32[]{:S(2)}, u32[]{:S(2)}) collective-permute-start(bf16[64,2,16,256]{3,0,2,1:T(8,128)(2,1)S(1)} %collective-permute-done.14), channel_id=1, source_target_pairs={{0,16},{4,20},{8,24},{12,28},{16,0},{20,4},{24,8},{28,12},{1,17},{... | collective-permute-start | bytes 3145736 | tf_op jit(solution)/shard_map/ppermute | solution.py:12
  381.0 26.3 %collective-permute-start.16 = (bf16[64,2,16,256]{3,0,2,1:T(8,128)(2,1)S(1)}, bf16[64,2,16,256]{3,0,2,1:T(8,128)(2,1)S(1)}, u32[]{:S(2)}, u32[]{:S(2)}) collective-permute-start(bf16[64,2,16,256]{3,0,2,1:T(8,128)(2,1)S(1)} %collective-permute-done.15), channel_id=1, source_target_pairs={{0,1},{1,0},{2,3},{3,2},{4,5},{5,4},{6,7},{7,6},{8,9},{9,8},{10,11... | collective-permute-start | bytes 3145736 | tf_op jit(solution)/shard_map/ppermute | solution.py:12
  407.2 24.5 %collective-permute-start.17 = (bf16[64,2,16,256]{3,0,2,1:T(8,128)(2,1)S(1)}, bf16[64,2,16,256]{3,0,2,1:T(8,128)(2,1)S(1)}, u32[]{:S(2)}, u32[]{:S(2)}) collective-permute-start(bf16[64,2,16,256]{3,0,2,1:T(8,128)(2,1)S(1)} %collective-permute-done.16), channel_id=1, source_target_pairs={{0,2},{1,3},{2,0},{3,1},{4,6},{5,7},{6,4},{7,5},{8,10},{9,11},{10,... | collective-permute-start | bytes 3145736 | tf_op jit(solution)/shard_map/ppermute | solution.py:12
where the time goes:
time: 437 us; the launch traced here: 436 us
  waiting for transfers between devices  269 us (62%)
  matrix products  60.3 us (14%)
  other arithmetic  40.8 us (9%)
  local copies, waits for them, and re-layouts  36 us (8%)
  starting transfers between devices  28.7 us (7%)
    ppermute x10, waiting for transfers between devices, from_partner(): return lax.ppermute(value, axis, pairs)  242 us
    dot_general x9, matrix products, adjoint_terms(): jnp.einsum('ji,jxyz->ixyz', joined, window, preferred_element_type=jnp.fl...  36.1 us
    dot_general x9, matrix products, forward_terms(): jnp.einsum('oi,ixyz->oxyz', joined, window, preferred_element_type=jnp.fl...  24.1 us
    concatenate x2, other arithmetic, extended_2(): shard = jnp.concatenate([before, shard, after], axis=dim)  17.2 us
    concatenate x1, other arithmetic, forward_terms(): jnp.concatenate([padded[:, :, :, third:third + depth] for third in range(...  16.1 us
    ppermute x4, waiting for transfers between devices, extended_2(): before = lax.ppermute(last, axis, up)  15.6 us
    ppermute x4, starting transfers between devices, extended_2(): before = lax.ppermute(last, axis, up)  11.5 us
    ppermute x4, waiting for transfers between devices, extended_2(): after = lax.ppermute(initial, axis, down)  11.2 us
  transfers between devices with their start and end apart: 18, of which 16 were waited for; matrix products, arithmetic and copies ran while one was open for 3% of the time, Pallas kernels for 0%

commit v1 on v0

v1 whole, which is shorter than its diff:
```python
import jax
import jax.numpy as jnp
from jax import lax
from jax.experimental import pallas as pl
from jax.experimental.pallas import tpu as pltpu
from jax.sharding import PartitionSpec as P


step_size = 0.5
LANES = 128
AXES = ("kx", "ky")
f32 = jnp.float32
bf16 = jnp.bfloat16


def on_line(a, b, nx, ny):
    inner = min(a, nx - 1 - a)
    return inner if b < ny // 2 else nx - 1 - inner


def line_device(a, b, nx, ny, place):
    near = b if b < ny // 2 else ny - 1 - b
    inner = min(place, nx - 1 - place)
    return (inner if a < nx // 2 else nx - 1 - inner), (near if place < nx // 2 else ny - 1 - near)


def to_mirror(a, b, nx, ny):
    return nx - 1 - a, ny - 1 - b


def to_right(a, b, nx, ny):
    place = on_line(a, b, nx, ny) + 1
    return line_device(a, b, nx, ny, place) if place < nx else None


def to_left(a, b, nx, ny):
    place = on_line(a, b, nx, ny) - 1
    return line_device(a, b, nx, ny, place) if place >= 0 else None


def to_next(a, b, nx, ny):
    return (a, b + 1) if b + 1 < ny else None


def to_previous(a, b, nx, ny):
    return (a, b - 1) if b > 0 else None


def send(value, move):
    nx, ny = lax.axis_size("kx"), lax.axis_size("ky")
    pairs = []
    for a in range(nx):
        for b in range(ny):
            target = move(a, b, nx, ny)
            if target is not None:
                pairs.append((a * ny + b, target[0] * ny + target[1]))
    return lax.ppermute(value, AXES, pairs)


def place_flags():
    a, b = lax.axis_index("kx"), lax.axis_index("ky")
    nx, ny = lax.axis_size("kx"), lax.axis_size("ky")
    near = b < ny // 2
    direct = near == (a < nx // 2)
    fold = (a == nx // 2) | (a == nx // 2 - 1)
    return direct, fold & jnp.logical_not(near), fold & near


def sign_rows(count, chans):
    row = lax.broadcasted_iota(jnp.int32, (count, 1), 0)
    return jnp.where(row % chans < chans // 2, 1.0, -1.0)


def dot(left, right):
    return jnp.dot(left, right, preferred_element_type=f32)


def reversal(depth):
    row = lax.broadcasted_iota(jnp.int32, (depth, depth), 0)
    col = lax.broadcasted_iota(jnp.int32, (depth, depth), 1)
    return jnp.where(row + col == depth - 1, 1.0, 0.0).astype(bf16)


def shifted(rows):
    depth = rows.shape[1]
    lane = lax.broadcasted_iota(jnp.int32, rows.shape, 1)
    before = jnp.where(lane == 0, 0, pltpu.roll(rows, 1, 1)).astype(rows.dtype)
    after = jnp.where(lane == depth - 1, 0, pltpu.roll(rows, depth - 1, 1)).astype(rows.dtype)
    return jnp.concatenate([before, rows, after], axis=0)


def flat(block):
    return block.reshape(-1, block.shape[-1])


def weights_kernel(kernel, early, late, adjoint, blocks):
    chans = kernel.shape[3]
    wide = 2 * chans
    layers = early.shape[0] // (3 * wide)
    direct, fold_first, fold_second = place_flags()
    lane = lax.broadcasted_iota(jnp.int32, (wide, wide), 1)
    lane_sign = jnp.where(lane[:chans] % chans < chans // 2, 1.0, -1.0)
    signs = sign_rows(chans, chans) * lane_sign

    adjoint[...] = jnp.zeros(adjoint.shape, bf16)

    def tap(dx, dy, dz):
        return kernel[dx, dy, dz].astype(f32)

    for dx in range(3):
        for dy in range(3):
            for dz in range(3):
                turned = pltpu.roll(tap(2 - dx, 2 - dy, 2 - dz) * signs, chans, 1)
                block = jnp.concatenate([tap(dx, dy, dz), turned], axis=0)
                blocks[dx, dy, dz] = block
                other = pltpu.roll(tap(dx, dy, dz) * signs, chans, 1)
                column = jnp.concatenate([tap(2 - dx, 2 - dy, 2 - dz), other], axis=0)
                column = jnp.transpose(column)[:chans].astype(bf16)
                for x in range(layers):
                    rows = pl.ds((dy * layers + x) * chans, chans)
                    source = x + dx - 1
                    start = dz * layers * wide
                    if 0 <= source < layers:
                        adjoint[rows, start + source * wide : start + (source + 1) * wide] = column
                    else:
                        start += 3 * layers * wide
                        slot = jnp.where(direct, 0.0, 1.0) if source < 0 else jnp.where(direct, 1.0, 0.0)
                        adjoint[rows, start : start + wide] = (column * (1.0 - slot)).astype(bf16)
                        adjoint[rows, start + wide : start + 2 * wide] = (column * slot).astype(bf16)

    half = lane < chans

    def pair(left, right, left_kind, right_kind):
        left = jnp.where(left_kind, pltpu.roll(left, chans, 1), left)
        right = jnp.where(right_kind, right, pltpu.roll(right, chans, 1))
        return jnp.where(half, left, right).astype(bf16)

    none = jnp.zeros((wide, wide), f32)
    for dy in range(3):
        for x in range(layers):
            rows = pl.ds((dy * layers + x) * wide, wide)
            for dz in range(3):
                get = lambda dx: blocks[dx, dy, dz] if 0 <= dx < 3 else none
                start = dz * layers * chans
                for source in range(0, layers, 2):
                    ahead, next_ahead = get(source - x + 1), get(source + 1 - x + 1)
                    cols = slice(start + source * chans, start + (source + 2) * chans)
                    early[rows, cols] = pair(ahead, next_ahead, False, False)
                    late[rows, cols] = pair(ahead, next_ahead, True, True)
                start = 3 * layers * chans + dz * 2 * chans
                below, above = get(-x), get(layers - x + 1)
                first = jnp.where(direct, below, above)
                second = jnp.where(direct, above, below)
                cols = slice(start, start + 2 * chans)
                early[rows, cols] = pair(first, second, fold_first, fold_second)
                late[rows, cols] = pair(
                    first, second, jnp.logical_not(fold_first), jnp.logical_not(fold_second)
                )


def to_rows(natural, spread, x, rows):
    chans = natural.shape[0]
    whole = natural[:, x].astype(f32).reshape(chans * rows, natural.shape[3])
    for part in range(spread.shape[0]):
        spread[part] = whole[:, part * LANES : (part + 1) * LANES]


def row_from(spread, y, chans, rows):
    return jnp.concatenate(
        [spread[part, pl.ds(y, chans, stride=rows), :] for part in range(spread.shape[0])], axis=1
    )


def prepare_kernel(natural, given, image, spread):
    chans, layers, rows, depth = natural.shape
    flip = reversal(depth)
    signs = sign_rows(chans, chans)
    for x in range(layers):
        to_rows(natural, spread, x, rows)

        def body(y, carry):
            block = row_from(spread, y, chans, rows).astype(bf16)
            given[y, x] = block
            image[rows - 1 - y, layers - 1 - x] = (dot(block, flip) * signs).astype(bf16)
            return carry

        lax.fori_loop(0, rows, body, 0, unroll=4)


def emit_sides(read, rows, chans, layers, depth, signs, right, left):
    direct, fold_first, fold_second = place_flags()
    flip = reversal(depth)

    def write(target, upper, turned):
        @pl.when(turned)
        def _():
            def body(y, carry):
                block = jnp.where(upper, read(y, layers - 1), read(y, 0))
                block = (dot(block, flip) * signs).astype(bf16)
                if block.shape[0] != chans:
                    block = jnp.concatenate([block[chans:], block[:chans]], axis=0)
                target[rows - 1 - y] = block
                return carry

            lax.fori_loop(0, rows, body, 0, unroll=2)

        @pl.when(jnp.logical_not(turned))
        def _():
            def body(y, carry):
                target[y] = jnp.where(upper, read(y, layers - 1), read(y, 0))
                return carry

            lax.fori_loop(0, rows, body, 0, unroll=2)

    write(right, direct, fold_second)
    write(left, jnp.logical_not(direct), fold_first)


def sides_kernel(own, right, left):
    rows, layers, chans, depth = own.shape
    signs = sign_rows(chans, chans)
    emit_sides(lambda y, x: own[y, x], rows, chans, layers, depth, signs, right, left)


def accumulate(weights, own, first, second, total, fresh):
    rows = own.shape[0]
    outs = weights.shape[0] // 3

    def x3(y):
        return jnp.concatenate(
            [shifted(flat(own[y])), shifted(jnp.concatenate([first[y], second[y]], axis=0))], axis=0
        )

    def put(y, part, new):
        total[y] = part if new else total[y] + part

    part = dot(weights[:outs, :], x3(0))
    put(0, part, fresh)
    part = dot(weights[: 2 * outs, :], x3(1))
    put(1, part[:outs], fresh)
    put(0, part[outs:], False)

    def body(y, carry):
        part = dot(weights[...], x3(y))
        put(y, part[:outs], fresh)
        put(y - 1, part[outs : 2 * outs], False)
        put(y - 2, part[2 * outs :], False)
        return carry

    lax.fori_loop(2, rows - 2, body, 0, unroll=4)
    part = dot(weights[outs:, :], x3(rows - 2))
    put(rows - 3, part[:outs], False)
    put(rows - 4, part[outs:], False)
    part = dot(weights[2 * outs :, :], x3(rows - 1))
    put(rows - 3, part, False)


def early_kernel(weights, own, first, second, total):
    accumulate(weights, own, first, second, total, True)


def late_kernel(weights, own, first, second, partial, given, field, right, left, natural, total, spread):
    rows, layers, chans, depth = own.shape
    inner = rows - 2
    total[...] = partial[...]
    accumulate(weights, own, first, second, total, False)
    b, ny = lax.axis_index("ky"), lax.axis_size("ky")

    def body(y, carry):
        inside = ((y > 0) | (b > 0)) & ((y < inner - 1) | (b < ny - 1))
        both = jnp.concatenate([given[y + 1], own[y + 1]], axis=1)
        value = total[y].reshape(layers, 2 * chans, depth) - both.astype(f32)
        field[y] = jnp.where(inside, value, 0.0).astype(bf16)
        return carry

    lax.fori_loop(0, inner, body, 0, unroll=2)
    signs = sign_rows(2 * chans, chans)
    emit_sides(lambda y, x: field[y, x], inner, chans, layers, depth, signs, right, left)
    from_rows(lambda y, x: field[y + 1, x, :chans].astype(f32), natural, spread)


def from_rows(read, natural, spread):
    chans, layers, rows, _ = natural.shape
    for x in range(layers):

        def body(y, carry):
            row = read(y, x)
            for part in range(spread.shape[0]):
                spread[part, pl.ds(y, chans, stride=rows), :] = row[:, part * LANES : (part + 1) * LANES]
            return carry

        lax.fori_loop(0, rows, body, 0, unroll=4)
        for part in range(spread.shape[0]):
            natural[:, x, :, part * LANES : (part + 1) * LANES] = (
                spread[part].reshape(chans, rows, LANES).astype(bf16)
            )


def gradient_kernel(weights, field, first, second, given, mask, natural, total, spread):
    chans, _, _, _ = natural.shape
    accumulate(weights, field, first, second, total, True)

    def value(y, x):
        gradient = total[y, x * chans : (x + 1) * chans] - field[y + 1, x, :chans].astype(f32)
        keep = 1.0 - mask[pl.ds(y, 1)].astype(f32)
        return given[y + 2, x].astype(f32) - step_size * keep * gradient

    from_rows(value, natural, spread)


def call(kernel, shape, scratch, *args):
    return pl.pallas_call(
        kernel,
        out_shape=shape,
        scratch_shapes=scratch,
        compiler_params=pltpu.CompilerParams(vmem_limit_bytes=56 << 20),
    )(*args)


def like(*shape, dtype=bf16):
    return jax.ShapeDtypeStruct(shape, dtype)


def around_y(own):
    before, after = send(own[-2:], to_next), send(own[:2], to_previous)
    return jnp.concatenate([before, own, after], axis=0)


def around_x(own):
    rows, _, chans, depth = own.shape
    side = like(rows, chans, depth)
    right, left = call(sides_kernel, (side, side), [], own)
    return send(right, to_right), send(left, to_left)


def step(kspace, kernel, mask):
    chans, layers, rows, depth = kspace.shape
    wide = layers * 2 * chans
    block = like(rows, layers, chans, depth)
    spread = pltpu.VMEM((depth // LANES, chans * rows, LANES), f32)
    given, image = call(prepare_kernel, (block, block), [spread], kspace)
    virtual = send(image, to_mirror)

    square = like(3 * wide, 3 * (layers + 2) * chans)
    early, late, adjoint = call(
        weights_kernel,
        (square, square, like(3 * layers * chans, 3 * (layers + 2) * 2 * chans)),
        [pltpu.VMEM((3, 3, 3, 2 * chans, 2 * chans), f32)],
        kernel,
    )

    given = around_y(given)
    first, second = around_x(given)
    partial = call(
        early_kernel, like(rows + 2, wide, depth, dtype=f32), [], early, given, first, second
    )

    virtual = around_y(virtual)
    first, second = around_x(virtual)
    side = like(rows + 2, 2 * chans, depth)
    field, right, left, residual = call(
        late_kernel,
        (like(rows + 2, layers, 2 * chans, depth), side, side, like(chans, layers, rows, depth)),
        [pltpu.VMEM((rows + 2, wide, depth), f32), spread],
        late, virtual, first, second, partial, given,
    )
    first, second = send(right, to_right), send(left, to_left)
    updated = call(
        gradient_kernel,
        like(chans, layers, rows, depth),
        [pltpu.VMEM((rows, layers * chans, depth), f32), spread],
        adjoint, field, first, second, given, mask,
    )
    return updated, residual


def solution(mesh):
    spec = P(None, "kx", "ky", None)
    return jax.shard_map(
        step,
        mesh=mesh,
        in_specs=(spec, P(), P("ky", None)),
        out_specs=(spec, spec),
        check_vma=False,
    )
```

time: 437 us -> 166 us (0.38)
  the two profiles are of different devices: /device:TPU:24 before, /device:TPU:18 now
where the time goes in v1:
time: 166 us
  waiting for transfers between devices  71.7 us (43%)
  Pallas kernels  58.6 us (35%)
  starting transfers between devices  27.8 us (17%)
  local copies, waits for them, and re-layouts  6.74 us (4%)
    ppermute x11, waiting for transfers between devices, send(): return lax.ppermute(value, AXES, pairs)  71.7 us
    pallas_call x7, Pallas kernels, call(): pl.pallas_call(kernel, out_shape=shape, scratch_shapes=scratch, compiler_...  58.6 us
    ppermute x11, starting transfers between devices, send(): return lax.ppermute(value, AXES, pairs)  27.8 us
    unnamed x22, local copies, waits for them, and re-layouts  5.72 us
  transfers between devices with their start and end apart: 11, of which 5 were waited for; matrix products, arithmetic and copies ran while one was open for 1% of the time, Pallas kernels for 15%

profile of v1, /device:TPU:18, one launch (start us, length us, event | category | flops | bytes accessed | tf_op | source)
XLA Modules:
  0.0 165.7 jit_solution(7389747161222873865)
XLA Ops:
  0.6 4.4 %shard_map.51 = (bf16[16,2,64,256]{3,2,1,0:T(8,128)(2,1)}, bf16[16,2,64,256]{3,2,1,0:T(8,128)(2,1)}) custom-call(bf16[64,2,16,256]{3,2,1,0:T(8,128)(2,1)} %natural.1), custom_call_target="tpu_custom_call" | custom-call | tf_op jit(solution)/shard_map/pallas_call | solution.py:312
  5.0 0.0 copy-start.2
  5.0 0.8 collective-permute-start
  5.9 1.0 fusion
  6.8 3.3 %collective-permute-start.5 = (bf16[2,2,64,256]{3,2,1,0:T(8,128)(2,1)S(1)}, bf16[2,2,64,256]{3,2,1,0:T(8,128)(2,1)S(1)}, u32[]{:S(2)}, u32[]{:S(2)}) collective-permute-start(bf16[2,2,64,256]{3,2,1,0:T(8,128)(2,1)S(1)} %get-tuple-element.29), channel_id=1, source_target_pairs={{0,1},{1,2},{2,3},{4,5},{5,6},{6,7},{8,9},{9,10},{10,11},{12,13},{... | collective-permute-start | bytes 393224 | tf_op jit(solution)/shard_map/ppermute | solution.py:57
  10.2 2.5 %collective-permute-start.6 = (bf16[2,2,64,256]{3,2,1,0:T(8,128)(2,1)S(1)}, bf16[2,2,64,256]{3,2,1,0:T(8,128)(2,1)S(1)}, u32[]{:S(2)}, u32[]{:S(2)}) collective-permute-start(bf16[2,2,64,256]{3,2,1,0:T(8,128)(2,1)S(1)} %get-tuple-element.28), channel_id=1, source_target_pairs={{1,0},{2,1},{3,2},{5,4},{6,5},{7,6},{9,8},{10,9},{11,10},{13,12},{... | collective-permute-start | bytes 393224 | tf_op jit(solution)/shard_map/ppermute | solution.py:57
  12.7 2.2 %collective-permute-done.5 = bf16[2,2,64,256]{3,2,1,0:T(8,128)(2,1)S(1)} collective-permute-done((bf16[2,2,64,256]{3,2,1,0:T(8,128)(2,1)S(1)}, bf16[2,2,64,256]{3,2,1,0:T(8,128)(2,1)S(1)}, u32[]{:S(2)}, u32[]{:S(2)}) %collective-permute-start.5) | collective-permute-done | bytes 131104 | tf_op jit(solution)/shard_map/ppermute | solution.py:57
  14.9 40.0 %collective-permute-done = bf16[16,2,64,256]{3,2,1,0:T(8,128)(2,1)S(1)} collective-permute-done((bf16[16,2,64,256]{3,2,1,0:T(8,128)(2,1)}, bf16[16,2,64,256]{3,2,1,0:T(8,128)(2,1)S(1)}, u32[]{:S(2)}, u32[]{:S(2)}) %collective-permute-start) | collective-permute-done | bytes 1048608 | tf_op jit(solution)/shard_map/ppermute | solution.py:57
  55.0 3.4 %collective-permute-start.1 = (bf16[2,2,64,256]{3,2,1,0:T(8,128)(2,1)S(1)}, bf16[2,2,64,256]{3,2,1,0:T(8,128)(2,1)S(1)}, u32[]{:S(2)}, u32[]{:S(2)}) collective-permute-start(bf16[2,2,64,256]{3,2,1,0:T(8,128)(2,1)S(1)} %get-tuple-element.31), channel_id=1, source_target_pairs={{0,1},{1,2},{2,3},{4,5},{5,6},{6,7},{8,9},{9,10},{10,11},{12,13},{... | collective-permute-start | bytes 393224 | tf_op jit(solution)/shard_map/ppermute | solution.py:57
  58.4 0.0 copy-done.2
  58.4 0.1 constant_dynamic-update-slice_fusion.4
  58.5 0.0 collective-permute-done.6
  58.5 0.0 copy-start
  58.5 1.2 copy-done
  59.7 4.2 %shard_map.53 = (bf16[20,64,256]{2,1,0:T(8,128)(2,1)}, bf16[20,64,256]{2,1,0:T(8,128)(2,1)}) custom-call(bf16[20,2,64,256]{3,2,1,0:T(8,128)(2,1)} %copy-done), custom_call_target="tpu_custom_call" | custom-call | tf_op jit(solution)/shard_map/pallas_call | solution.py:312
  63.9 3.4 %collective-permute-start.7 = (bf16[20,64,256]{2,1,0:T(8,128)(2,1)}, bf16[20,64,256]{2,1,0:T(8,128)(2,1)S(1)}, u32[]{:S(2)}, u32[]{:S(2)}) collective-permute-start(bf16[20,64,256]{2,1,0:T(8,128)(2,1)} %get-tuple-element.22), channel_id=1, source_target_pairs={{0,4},{1,5},{4,8},{5,9},{6,2},{7,3},{8,12},{9,13},{10,6},{11,7},{1... | collective-permute-start | bytes 1966088 | tf_op jit(solution)/shard_map/ppermute | solution.py:57
  67.3 1.9 %collective-permute-start.8 = (bf16[20,64,256]{2,1,0:T(8,128)(2,1)}, bf16[20,64,256]{2,1,0:T(8,128)(2,1)S(1)}, u32[]{:S(2)}, u32[]{:S(2)}) collective-permute-start(bf16[20,64,256]{2,1,0:T(8,128)(2,1)} %get-tuple-element.23), channel_id=1, source_target_pairs={{2,6},{3,7},{4,0},{5,1},{6,10},{7,11},{8,4},{9,5},{10,14},{11,15},... | collective-permute-start | bytes 1966088 | tf_op jit(solution)/shard_map/ppermute | solution.py:57
  69.2 1.9 %collective-permute-start.2 = (bf16[2,2,64,256]{3,2,1,0:T(8,128)(2,1)S(1)}, bf16[2,2,64,256]{3,2,1,0:T(8,128)(2,1)S(1)}, u32[]{:S(2)}, u32[]{:S(2)}) collective-permute-start(bf16[2,2,64,256]{3,2,1,0:T(8,128)(2,1)S(1)} %get-tuple-element.30), channel_id=1, source_target_pairs={{1,0},{2,1},{3,2},{5,4},{6,5},{7,6},{9,8},{10,9},{11,10},{13,12},{... | collective-permute-start | bytes 393224 | tf_op jit(solution)/shard_map/ppermute | solution.py:57
  71.1 0.0 collective-permute-done.1
  71.1 0.1 constant_dynamic-update-slice_fusion.1
  71.3 12.2 %collective-permute-done.2 = bf16[2,2,64,256]{3,2,1,0:T(8,128)(2,1)S(1)} collective-permute-done((bf16[2,2,64,256]{3,2,1,0:T(8,128)(2,1)S(1)}, bf16[2,2,64,256]{3,2,1,0:T(8,128)(2,1)S(1)}, u32[]{:S(2)}, u32[]{:S(2)}) %collective-permute-start.2) | collective-permute-done | bytes 131104 | tf_op jit(solution)/shard_map/ppermute | solution.py:57
  83.4 0.0 copy-start.1
  83.5 1.1 copy-done.1
  84.6 4.2 %shard_map.52 = (bf16[20,64,256]{2,1,0:T(8,128)(2,1)}, bf16[20,64,256]{2,1,0:T(8,128)(2,1)}) custom-call(bf16[20,2,64,256]{3,2,1,0:T(8,128)(2,1)} %copy-done.1), custom_call_target="tpu_custom_call" | custom-call | tf_op jit(solution)/shard_map/pallas_call | solution.py:312
  88.7 1.9 %collective-permute-start.3 = (bf16[20,64,256]{2,1,0:T(8,128)(2,1)}, bf16[20,64,256]{2,1,0:T(8,128)(2,1)S(1)}, u32[]{:S(2)}, u32[]{:S(2)}) collective-permute-start(bf16[20,64,256]{2,1,0:T(8,128)(2,1)} %get-tuple-element.18), channel_id=1, source_target_pairs={{0,4},{1,5},{4,8},{5,9},{6,2},{7,3},{8,12},{9,13},{10,6},{11,7},{1... | collective-permute-start | bytes 1966088 | tf_op jit(solution)/shard_map/ppermute | solution.py:57
  90.6 2.4 %collective-permute-start.4 = (bf16[20,64,256]{2,1,0:T(8,128)(2,1)}, bf16[20,64,256]{2,1,0:T(8,128)(2,1)S(1)}, u32[]{:S(2)}, u32[]{:S(2)}) collective-permute-start(bf16[20,64,256]{2,1,0:T(8,128)(2,1)} %get-tuple-element.19), channel_id=1, source_target_pairs={{2,6},{3,7},{4,0},{5,1},{6,10},{7,11},{8,4},{9,5},{10,14},{11,15},... | collective-permute-start | bytes 1966088 | tf_op jit(solution)/shard_map/ppermute | solution.py:57
  93.0 4.5 %shard_map.50 = (bf16[768,768]{1,0:T(8,128)(2,1)}, bf16[768,768]{1,0:T(8,128)(2,1)}, bf16[384,1536]{1,0:T(8,128)(2,1)}) custom-call(bf16[3,3,3,64,128]{4,3,2,1,0:T(8,128)(2,1)} %kernel.1), custom_call_target="tpu_custom_call" | custom-call | tf_op jit(solution)/shard_map/pallas_call | solution.py:312
  97.5 0.0 collective-permute-done.7.first
  97.5 0.0 copy-start.5
  97.5 0.0 collective-permute-done.8.second
  97.5 0.0 copy-start.6
  97.5 0.8 copy-done.5
  98.4 0.3 copy-done.6
  98.6 11.5 %shard_map.54.partial = f32[18,256,256]{2,1,0:T(8,128)} custom-call(bf16[768,768]{1,0:T(8,128)(2,1)} %get-tuple-element.20.weights, bf16[20,2,64,256]{3,2,1,0:T(8,128)(2,1)} %copy-done, bf16[20,64,256]{2,1,0:T(8,128)(2,1)} %copy-done.5, bf16[20,64,256]{2,1,0:T(8,128)(2,1)} %copy-done.6), custom_call_target="tpu_custom_call" | custom-call | tf_op jit(solution)/shard_map/pallas_call | solution.py:312
  110.2 0.0 collective-permute-done.3.first
  110.2 0.0 copy-start.7
  110.2 0.0 collective-permute-done.4.second
  110.2 0.0 copy-start.8
  110.2 0.8 copy-done.7
  111.0 0.2 copy-done.8
  111.2 17.6 %shard_map.55 = (bf16[18,2,128,256]{3,2,1,0:T(8,128)(2,1)}, bf16[18,128,256]{2,1,0:T(8,128)(2,1)}, bf16[18,128,256]{2,1,0:T(8,128)(2,1)}, bf16[64,2,16,256]{3,2,1,0:T(8,128)(2,1)}) custom-call(bf16[768,768]{1,0:T(8,128)(2,1)} %get-tuple-element.16.weights, bf16[20,2,64,256]{3,2,1,0:T(8,128)(2,1)} %copy-done.1, bf16[20,64,256]{2,1,0:T(8,128)(2,1)} %copy-done.7, ...), custom_call_target="tpu_custom_call" | custom-call | tf_op jit(solution)/shard_map/pallas_call | solution.py:312
  128.8 4.3 %collective-permute-start.9 = (bf16[18,128,256]{2,1,0:T(8,128)(2,1)}, bf16[18,128,256]{2,1,0:T(8,128)(2,1)S(1)}, u32[]{:S(2)}, u32[]{:S(2)}) collective-permute-start(bf16[18,128,256]{2,1,0:T(8,128)(2,1)} %get-tuple-element.25), channel_id=1, source_target_pairs={{0,4},{1,5},{4,8},{5,9},{6,2},{7,3},{8,12},{9,13},{10,6},{11,7},{1... | collective-permute-start | bytes 3538952 | tf_op jit(solution)/shard_map/ppermute | solution.py:57
  133.1 1.9 %collective-permute-start.10 = (bf16[18,128,256]{2,1,0:T(8,128)(2,1)}, bf16[18,128,256]{2,1,0:T(8,128)(2,1)S(1)}, u32[]{:S(2)}, u32[]{:S(2)}) collective-permute-start(bf16[18,128,256]{2,1,0:T(8,128)(2,1)} %get-tuple-element.26), channel_id=1, source_target_pairs={{2,6},{3,7},{4,0},{5,1},{6,10},{7,11},{8,4},{9,5},{10,14},{11,15},... | collective-permute-start | bytes 3538952 | tf_op jit(solution)/shard_map/ppermute | solution.py:57
  135.0 12.1 %collective-permute-done.9.first = bf16[18,128,256]{2,1,0:T(8,128)(2,1)S(1)} collective-permute-done((bf16[18,128,256]{2,1,0:T(8,128)(2,1)}, bf16[18,128,256]{2,1,0:T(8,128)(2,1)S(1)}, u32[]{:S(2)}, u32[]{:S(2)}) %collective-permute-start.9) | collective-permute-done | bytes 1179680 | tf_op jit(solution)/shard_map/ppermute | solution.py:57
  147.1 5.2 %collective-permute-done.10.second = bf16[18,128,256]{2,1,0:T(8,128)(2,1)S(1)} collective-permute-done((bf16[18,128,256]{2,1,0:T(8,128)(2,1)}, bf16[18,128,256]{2,1,0:T(8,128)(2,1)S(1)}, u32[]{:S(2)}, u32[]{:S(2)}) %collective-permute-start.10) | collective-permute-done | bytes 1179680 | tf_op jit(solution)/shard_map/ppermute | solution.py:57
  152.3 0.0 copy-done.3
  152.3 1.1 copy-done.4
  153.4 12.2 %shard_map.56 = bf16[64,2,16,256]{3,2,1,0:T(8,128)(2,1)} custom-call(bf16[384,1536]{1,0:T(8,128)(2,1)} %get-tuple-element.15.weights, bf16[18,2,128,256]{3,2,1,0:T(8,128)(2,1)} %get-tuple-element.24.field, bf16[18,128,256]{2,1,0:T(8,128)(2,1)} %copy-done.3, bf16[18,128,256]{2,1,0:T(8,128)(2,1)} %copy-done.4, bf16[20,2,64,256]{3,2,1,0:T(8,128)(2,1)} %copy-done, ...), custom_call_target="tpu_custom_call" | custom-call | tf_op jit(solution)/shard_map/pallas_call | solution.py:312
  (7 shorter events, 0.1 us)
Async XLA Ops:
  5.0 53.4 %copy-start.2 = (bf16[16,2,64,256]{3,2,1,0:T(8,128)(2,1)S(1)}, bf16[16,2,64,256]{3,2,1,0:T(8,128)(2,1)}, u32[]{:S(2)}) copy-start(bf16[16,2,64,256]{3,2,1,0:T(8,128)(2,1)} %get-tuple-element.21) | copy-start | bytes 3145732
  5.0 49.9 %collective-permute-start = (bf16[16,2,64,256]{3,2,1,0:T(8,128)(2,1)}, bf16[16,2,64,256]{3,2,1,0:T(8,128)(2,1)S(1)}, u32[]{:S(2)}, u32[]{:S(2)}) collective-permute-start(bf16[16,2,64,256]{3,2,1,0:T(8,128)(2,1)} %get-tuple-element.17), channel_id=1, source_target_pairs={{0,31},{1,30},{2,29},{3,28},{4,27},{5,26},{6,25},{7,24},{8,23},{9,... | collective-permute-start | bytes 3145736 | tf_op jit(solution)/shard_map/ppermute | solution.py:57
  6.8 8.1 %collective-permute-start.5 = (bf16[2,2,64,256]{3,2,1,0:T(8,128)(2,1)S(1)}, bf16[2,2,64,256]{3,2,1,0:T(8,128)(2,1)S(1)}, u32[]{:S(2)}, u32[]{:S(2)}) collective-permute-start(bf16[2,2,64,256]{3,2,1,0:T(8,128)(2,1)S(1)} %get-tuple-element.29), channel_id=1, source_target_pairs={{0,1},{1,2},{2,3},{4,5},{5,6},{6,7},{8,9},{9,10},{10,11},{12,13},{... | collective-permute-start | bytes 393224 | tf_op jit(solution)/shard_map/ppermute | solution.py:57
  10.2 48.3 %collective-permute-start.6 = (bf16[2,2,64,256]{3,2,1,0:T(8,128)(2,1)S(1)}, bf16[2,2,64,256]{3,2,1,0:T(8,128)(2,1)S(1)}, u32[]{:S(2)}, u32[]{:S(2)}) collective-permute-start(bf16[2,2,64,256]{3,2,1,0:T(8,128)(2,1)S(1)} %get-tuple-element.28), channel_id=1, source_target_pairs={{1,0},{2,1},{3,2},{5,4},{6,5},{7,6},{9,8},{10,9},{11,10},{13,12},{... | collective-permute-start | bytes 393224 | tf_op jit(solution)/shard_map/ppermute | solution.py:57
  55.0 16.1 %collective-permute-start.1 = (bf16[2,2,64,256]{3,2,1,0:T(8,128)(2,1)S(1)}, bf16[2,2,64,256]{3,2,1,0:T(8,128)(2,1)S(1)}, u32[]{:S(2)}, u32[]{:S(2)}) collective-permute-start(bf16[2,2,64,256]{3,2,1,0:T(8,128)(2,1)S(1)} %get-tuple-element.31), channel_id=1, source_target_pairs={{0,1},{1,2},{2,3},{4,5},{5,6},{6,7},{8,9},{9,10},{10,11},{12,13},{... | collective-permute-start | bytes 393224 | tf_op jit(solution)/shard_map/ppermute | solution.py:57
  58.5 1.2 copy-start
  63.9 33.6 %collective-permute-start.7 = (bf16[20,64,256]{2,1,0:T(8,128)(2,1)}, bf16[20,64,256]{2,1,0:T(8,128)(2,1)S(1)}, u32[]{:S(2)}, u32[]{:S(2)}) collective-permute-start(bf16[20,64,256]{2,1,0:T(8,128)(2,1)} %get-tuple-element.22), channel_id=1, source_target_pairs={{0,4},{1,5},{4,8},{5,9},{6,2},{7,3},{8,12},{9,13},{10,6},{11,7},{1... | collective-permute-start | bytes 1966088 | tf_op jit(solution)/shard_map/ppermute | solution.py:57
  67.3 30.2 %collective-permute-start.8 = (bf16[20,64,256]{2,1,0:T(8,128)(2,1)}, bf16[20,64,256]{2,1,0:T(8,128)(2,1)S(1)}, u32[]{:S(2)}, u32[]{:S(2)}) collective-permute-start(bf16[20,64,256]{2,1,0:T(8,128)(2,1)} %get-tuple-element.23), channel_id=1, source_target_pairs={{2,6},{3,7},{4,0},{5,1},{6,10},{7,11},{8,4},{9,5},{10,14},{11,15},... | collective-permute-start | bytes 1966088 | tf_op jit(solution)/shard_map/ppermute | solution.py:57
  69.2 14.2 %collective-permute-start.2 = (bf16[2,2,64,256]{3,2,1,0:T(8,128)(2,1)S(1)}, bf16[2,2,64,256]{3,2,1,0:T(8,128)(2,1)S(1)}, u32[]{:S(2)}, u32[]{:S(2)}) collective-permute-start(bf16[2,2,64,256]{3,2,1,0:T(8,128)(2,1)S(1)} %get-tuple-element.30), channel_id=1, source_target_pairs={{1,0},{2,1},{3,2},{5,4},{6,5},{7,6},{9,8},{10,9},{11,10},{13,12},{... | collective-permute-start | bytes 393224 | tf_op jit(solution)/shard_map/ppermute | solution.py:57
  83.4 1.1 copy-start.1
  88.7 21.5 %collective-permute-start.3 = (bf16[20,64,256]{2,1,0:T(8,128)(2,1)}, bf16[20,64,256]{2,1,0:T(8,128)(2,1)S(1)}, u32[]{:S(2)}, u32[]{:S(2)}) collective-permute-start(bf16[20,64,256]{2,1,0:T(8,128)(2,1)} %get-tuple-element.18), channel_id=1, source_target_pairs={{0,4},{1,5},{4,8},{5,9},{6,2},{7,3},{8,12},{9,13},{10,6},{11,7},{1... | collective-permute-start | bytes 1966088 | tf_op jit(solution)/shard_map/ppermute | solution.py:57
  90.6 19.5 %collective-permute-start.4 = (bf16[20,64,256]{2,1,0:T(8,128)(2,1)}, bf16[20,64,256]{2,1,0:T(8,128)(2,1)S(1)}, u32[]{:S(2)}, u32[]{:S(2)}) collective-permute-start(bf16[20,64,256]{2,1,0:T(8,128)(2,1)} %get-tuple-element.19), channel_id=1, source_target_pairs={{2,6},{3,7},{4,0},{5,1},{6,10},{7,11},{8,4},{9,5},{10,14},{11,15},... | collective-permute-start | bytes 1966088 | tf_op jit(solution)/shard_map/ppermute | solution.py:57
  97.5 0.9 copy-start.5
  97.5 1.1 copy-start.6
  110.2 0.8 copy-start.7
  110.2 1.0 copy-start.8
  128.8 18.3 %collective-permute-start.9 = (bf16[18,128,256]{2,1,0:T(8,128)(2,1)}, bf16[18,128,256]{2,1,0:T(8,128)(2,1)S(1)}, u32[]{:S(2)}, u32[]{:S(2)}) collective-permute-start(bf16[18,128,256]{2,1,0:T(8,128)(2,1)} %get-tuple-element.25), channel_id=1, source_target_pairs={{0,4},{1,5},{4,8},{5,9},{6,2},{7,3},{8,12},{9,13},{10,6},{11,7},{1... | collective-permute-start | bytes 3538952 | tf_op jit(solution)/shard_map/ppermute | solution.py:57
  133.1 19.2 %collective-permute-start.10 = (bf16[18,128,256]{2,1,0:T(8,128)(2,1)}, bf16[18,128,256]{2,1,0:T(8,128)(2,1)S(1)}, u32[]{:S(2)}, u32[]{:S(2)}) collective-permute-start(bf16[18,128,256]{2,1,0:T(8,128)(2,1)} %get-tuple-element.26), channel_id=1, source_target_pairs={{2,6},{3,7},{4,0},{5,1},{6,10},{7,11},{8,4},{9,5},{10,14},{11,15},... | collective-permute-start | bytes 3538952 | tf_op jit(solution)/shard_map/ppermute | solution.py:57
  147.1 5.2 %copy-start.3 = (bf16[18,128,256]{2,1,0:T(8,128)(2,1)}, bf16[18,128,256]{2,1,0:T(8,128)(2,1)S(1)}, u32[]{:S(2)}) copy-start(bf16[18,128,256]{2,1,0:T(8,128)(2,1)S(1)} %collective-permute-done.9.first) | copy-start | bytes 3538948
  152.3 1.1 copy-start.4

commit v2 on v1

v2 whole, which is shorter than its diff:
```python
import functools

import jax
import jax.numpy as jnp
from jax import lax
from jax.experimental import pallas as pl
from jax.experimental.pallas import tpu as pltpu
from jax.sharding import PartitionSpec as P


step_size = 0.5
LANES = 128
OUTER = 4
VMEM_LIMIT = 40 << 20
AXES = ("kx", "ky")
f32 = jnp.float32
bf16 = jnp.bfloat16


def on_line(a, b, nx, ny):
    inner = min(a, nx - 1 - a)
    return inner if b < ny // 2 else nx - 1 - inner


def line_device(a, b, nx, ny, place):
    near = b if b < ny // 2 else ny - 1 - b
    inner = min(place, nx - 1 - place)
    return (inner if a < nx // 2 else nx - 1 - inner), (near if place < nx // 2 else ny - 1 - near)


def to_mirror(a, b, nx, ny):
    return nx - 1 - a, ny - 1 - b


def to_right(a, b, nx, ny):
    place = on_line(a, b, nx, ny) + 1
    return line_device(a, b, nx, ny, place) if place < nx else None


def to_left(a, b, nx, ny):
    place = on_line(a, b, nx, ny) - 1
    return line_device(a, b, nx, ny, place) if place >= 0 else None


def to_next(a, b, nx, ny):
    return (a, b + 1) if b + 1 < ny else None


def to_previous(a, b, nx, ny):
    return (a, b - 1) if b > 0 else None


def send(value, move):
    nx, ny = lax.axis_size("kx"), lax.axis_size("ky")
    pairs = []
    for a in range(nx):
        for b in range(ny):
            target = move(a, b, nx, ny)
            if target is not None:
                pairs.append((a * ny + b, target[0] * ny + target[1]))
    return lax.ppermute(value, AXES, pairs)


def place_flags():
    a, b = lax.axis_index("kx"), lax.axis_index("ky")
    nx, ny = lax.axis_size("kx"), lax.axis_size("ky")
    near = b < ny // 2
    direct = near == (a < nx // 2)
    fold = (a == nx // 2) | (a == nx // 2 - 1)
    return direct, fold & jnp.logical_not(near), fold & near


def sign_rows(count, chans):
    row = lax.broadcasted_iota(jnp.int32, (count, 1), 0)
    return jnp.where(row % chans < chans // 2, 1.0, -1.0)


def dot(left, right):
    return jnp.dot(left, right, preferred_element_type=f32)


def reversal(depth):
    row = lax.broadcasted_iota(jnp.int32, (depth, depth), 0)
    col = lax.broadcasted_iota(jnp.int32, (depth, depth), 1)
    return jnp.where(row + col == depth - 1, 1.0, 0.0).astype(bf16)


def shifted(rows):
    depth = rows.shape[1]
    lane = lax.broadcasted_iota(jnp.int32, rows.shape, 1)
    before = jnp.where(lane == 0, 0, pltpu.roll(rows, 1, 1)).astype(rows.dtype)
    after = jnp.where(lane == depth - 1, 0, pltpu.roll(rows, depth - 1, 1)).astype(rows.dtype)
    return jnp.concatenate([before, rows, after], axis=0)


def flat(block):
    return block.reshape(-1, block.shape[-1])


def inside_y(y, count):
    b, ny = lax.axis_index("ky"), lax.axis_size("ky")
    return ((y > 0) | (b > 0)) & ((y < count - 1) | (b < ny - 1))


def weights_kernel(kernel, early, early_sides, late, late_sides, adjoint, outward, blocks, columns):
    chans = kernel.shape[3]
    wide = 2 * chans
    layers = early.shape[0] // (3 * wide)
    direct, fold_first, fold_second = place_flags()
    lane = lax.broadcasted_iota(jnp.int32, (wide, wide), 1)
    lane_sign = jnp.where(lane[:chans] % chans < chans // 2, 1.0, -1.0)
    signs = sign_rows(chans, chans) * lane_sign

    for dx in range(3):
        for dy in range(3):
            for dz in range(3):
                plain = kernel[dx, dy, dz].astype(f32)
                opposite = kernel[2 - dx, 2 - dy, 2 - dz].astype(f32)
                blocks[dx, dy, dz] = jnp.concatenate(
                    [plain, pltpu.roll(opposite * signs, chans, 1)], axis=0
                )
                column = jnp.concatenate([opposite, pltpu.roll(plain * signs, chans, 1)], axis=0)
                columns[dx, dy, dz] = jnp.transpose(column)[:chans]

    none = jnp.zeros((chans, wide), bf16)
    for dy in range(3):
        for x in range(layers):
            rows = pl.ds((dy * layers + x) * chans, chans)
            for dz in range(3):
                for source in range(layers):
                    dx = source - x + 1
                    start = (dz * layers + source) * wide
                    block = columns[dx, dy, dz].astype(bf16) if 0 <= dx < 3 else none
                    adjoint[rows, start : start + wide] = block
        for dz in range(3):
            rows, cols = pl.ds(dy * chans, chans), slice(dz * wide, (dz + 1) * wide)
            low, high = columns[0, dy, dz], columns[2, dy, dz]
            turn = lambda block: pltpu.roll(block, chans, 1) * lane_sign
            low_turned, high_turned = turn(columns[0, 2 - dy, 2 - dz]), turn(columns[2, 2 - dy, 2 - dz])
            right = jnp.where(direct, low, high)
            right = jnp.where(fold_second, jnp.where(direct, high_turned, low_turned), right)
            left = jnp.where(direct, high, low)
            left = jnp.where(fold_first, jnp.where(direct, low_turned, high_turned), left)
            outward[0, rows, cols] = right.astype(bf16)
            outward[1, rows, cols] = left.astype(bf16)

    half = lane < chans

    def pair(left, right, kind):
        left = jnp.where(kind, pltpu.roll(left, chans, 1), left)
        right = jnp.where(kind, right, pltpu.roll(right, chans, 1))
        return jnp.where(half, left, right).astype(bf16)

    empty = jnp.zeros((wide, wide), f32)
    for dy in range(3):
        for x in range(layers):
            rows = pl.ds((dy * layers + x) * wide, wide)
            for dz in range(3):
                get = lambda dx: blocks[dx, dy, dz] if 0 <= dx < 3 else empty
                start = dz * layers * chans
                for source in range(0, layers, 2):
                    ahead, behind = get(source - x + 1), get(source - x + 2)
                    cols = slice(start + source * chans, start + (source + 2) * chans)
                    early[rows, cols] = pair(ahead, behind, False)
                    late[rows, cols] = pair(ahead, behind, True)
        rows = pl.ds(dy * wide, wide)
        for slot, fold in ((0, fold_first), (1, fold_second)):
            lower = direct if slot == 0 else jnp.logical_not(direct)
            taps = [jnp.where(lower, blocks[0, dy, dz], blocks[2, dy, dz]) for dz in range(3)]
            for target, kind in ((early_sides, fold), (late_sides, jnp.logical_not(fold))):
                target[slot, rows, 0:wide] = pair(taps[0], taps[1], kind)
                target[slot, rows, wide : wide + chans] = pair(taps[2], taps[2], kind)[:, :chans]


def row_from(spread, y, chans, rows):
    return jnp.concatenate(
        [spread[part, pl.ds(y, chans, stride=rows), :] for part in range(spread.shape[0])], axis=1
    )


def prepare_kernel(natural, given, first_rows, last_rows, outer, inner, spread, turned):
    chans, layers, rows, depth = natural.shape
    flip = reversal(depth)
    signs = sign_rows(chans, chans)
    edge = outer.shape[0] // 2
    for x in range(layers):
        whole = natural[:, x].reshape(chans * rows, depth)
        mirrored = dot(whole, flip)
        whole = whole.astype(f32)
        for part in range(spread.shape[0]):
            spread[part] = whole[:, part * LANES : (part + 1) * LANES]
            turned[part] = mirrored[:, part * LANES : (part + 1) * LANES]
        for y in range(rows):
            block = row_from(spread, y, chans, rows).astype(bf16)
            given[y, x] = block
            if y < 2:
                first_rows[y, x] = block
            if y >= rows - 2:
                last_rows[y - rows + 2, x] = block
            target = rows - 1 - y
            block = (row_from(turned, y, chans, rows) * signs).astype(bf16)
            if target < edge:
                outer[target, layers - 1 - x] = block
            elif target < rows - edge:
                inner[target - edge, layers - 1 - x] = block
            else:
                outer[target - rows + 2 * edge, layers - 1 - x] = block


def emit_sides(read, rows, group, chans, depth, layers, signs, right, left):
    direct, fold_first, fold_second = place_flags()
    flip = reversal(depth)

    def write(target, upper, turned):
        def pick(y):
            return jnp.where(upper, read(y, layers - 1), read(y, 0))

        @pl.when(turned)
        def _():
            def body(j, carry):
                block = jnp.concatenate([pick(j * group + i).astype(bf16) for i in range(group)], axis=0)
                block = dot(block, flip)
                for i in range(group):
                    part = block[i * chans : (i + 1) * chans]
                    target[rows - 1 - j * group - i] = (part * signs).astype(bf16)
                return carry

            lax.fori_loop(0, rows // group, body, 0)

        @pl.when(jnp.logical_not(turned))
        def _():
            def body(y, carry):
                target[y] = pick(y).astype(bf16)
                return carry

            lax.fori_loop(0, rows, body, 0, unroll=2)

    write(right, direct, fold_second)
    write(left, jnp.logical_not(direct), fold_first)


def sides_kernel(layout, *refs):
    *segments, right, left, joined = refs
    rows, layers, chans, depth = joined.shape
    start = 0
    for index, offset, count in layout:
        joined[start : start + count] = segments[index][offset : offset + count]
        start += count
    signs = sign_rows(chans, chans)
    emit_sides(lambda y, x: joined[y, x], rows, 4, chans, depth, layers, signs, right, left)


def add_part(total, part, place, columns):
    outs = part.shape[0] // 3
    for third in range(3):
        target = place - third
        if isinstance(target, int) and not 0 <= target < total.shape[0]:
            continue
        total[target, columns] = total[target, columns] + part[third * outs : (third + 1) * outs]


def add_rows(weights, read, count, place, total, columns, static):
    def one(y, place):
        add_part(total, dot(weights[...], shifted(flat(read(y)))), place, columns)

    if static:
        for y in range(count):
            one(y, place + y)
    else:

        def body(y, carry):
            one(y, place + y)
            return carry

        lax.fori_loop(0, count, body, 0, unroll=4)


def side_columns(total, layers):
    direct, _, _ = place_flags()
    wide = total.shape[1] // layers
    upper = (layers - 1) * wide
    first = pl.multiple_of(jnp.where(direct, 0, upper), wide)
    second = pl.multiple_of(jnp.where(direct, upper, 0), wide)
    return pl.ds(first, wide), pl.ds(second, wide)


def add_own(weights, segments, total):
    for ref, count, offset, place, static in segments:
        add_rows(
            weights, lambda y, ref=ref, offset=offset: ref[y + offset], count, place, total,
            slice(None), static,
        )


def add_sides(weights, first, second, offset, count, place, total, columns, static):
    for slot, ref in ((0, first), (1, second)):
        add_rows(
            weights.at[slot], lambda y, ref=ref: ref[y + offset], count, place, total,
            columns[slot], static,
        )


def early_kernel(weights, top, own, bottom, total):
    rows = own.shape[0]
    total[...] = jnp.zeros(total.shape, f32)
    add_own(
        weights,
        ((top, 2, 0, 0, True), (own, rows, 0, 2, False), (bottom, 2, 0, rows + 2, True)),
        total,
    )


def middle_kernel(sides, first, second, partial, total):
    rows = total.shape[0] - 2
    layers = 3 * total.shape[1] // sides.shape[1]
    total[...] = partial[...]
    add_all_sides(sides, first, second, rows, total, side_columns(total, layers))


def add_all_sides(sides, first, second, rows, total, columns):
    for offset, count, static in ((0, 2, True), (2, rows, False), (rows + 2, 2, True)):
        add_sides(sides, first, second, offset, count, offset, total, columns, static)


def inner_kernel(weights, top, outer, inner, bottom, partial, total):
    rows = total.shape[0] - 2
    edge = outer.shape[0] // 2
    total[...] = partial[...]
    add_own(
        weights,
        (
            (top, 2, 0, 0, True),
            (outer, edge, 0, 2, True),
            (inner, rows - 2 * edge, 0, 2 + edge, False),
            (outer, edge, edge, rows + 2 - edge, True),
            (bottom, 2, 0, rows + 2, True),
        ),
        total,
    )


def residual_kernel(
    sides, outward, first, second, partial,
    top, given, bottom, virtual_top, virtual_outer, virtual_bottom, virtual_inner,
    field, right, left, total, reach,
):
    rows, layers, chans, depth = given.shape
    span = rows + 2
    edge = virtual_outer.shape[0] // 2
    total[...] = partial[...]
    columns = side_columns(total, layers)
    add_all_sides(sides, first, second, rows, total, columns)

    def finish(target, k, t):
        both = jnp.concatenate([k, t], axis=1).astype(f32)
        value = total[target].reshape(layers, 2 * chans, depth) - both
        field[target] = jnp.where(inside_y(target, span), value, 0.0).astype(bf16)

    def loop(count, first_target, k, t):
        def body(y, carry):
            finish(first_target + y, k(y), t(y))
            return carry

        lax.fori_loop(0, count, body, 0, unroll=2)

    finish(0, top[1], virtual_top[1])
    loop(edge, 1, lambda y: given[y], lambda y: virtual_outer[y])
    loop(rows - 2 * edge, 1 + edge, lambda y: given[y + edge], lambda y: virtual_inner[y])
    loop(edge, 1 + rows - edge, lambda y: given[y + rows - edge], lambda y: virtual_outer[y + edge])
    finish(span - 1, bottom[0], virtual_bottom[0])

    direct, _, _ = place_flags()
    reach[...] = jnp.zeros(reach.shape, f32)
    for slot, upper in ((0, direct), (1, jnp.logical_not(direct))):
        target, weights = reach.at[slot], outward.at[slot]

        def read(y, upper=upper):
            return jnp.where(upper, field[y, layers - 1], field[y, 0])

        add_rows(weights, read, 1, 0, target, slice(None), True)
        add_rows(weights, lambda y, read=read: read(y + 1), 1, 1, target, slice(None), True)
        add_rows(weights, lambda y, read=read: read(y + 2), rows - 2, 2, target, slice(None), False)
        add_rows(weights, lambda y, read=read: read(y + rows), 1, rows, target, slice(None), True)
        add_rows(weights, lambda y, read=read: read(y + rows + 1), 1, rows + 1, target, slice(None), True)
    ones = jnp.ones((chans, 1), f32)

    upper_reach = lambda y: jnp.where(direct, reach[0, y], reach[1, y])
    lower_reach = lambda y: jnp.where(direct, reach[1, y], reach[0, y])
    emit_sides(
        lambda y, x: upper_reach(y) if x == layers - 1 else lower_reach(y),
        rows, 4, chans, depth, layers, ones, right, left,
    )


def from_rows(read, natural, spread):
    chans, layers, rows, _ = natural.shape
    for x in range(layers):

        def body(y, carry):
            row = read(y, x)
            for part in range(spread.shape[0]):
                spread[part, pl.ds(y, chans, stride=rows), :] = row[:, part * LANES : (part + 1) * LANES]
            return carry

        lax.fori_loop(0, rows, body, 0, unroll=4)
        for part in range(spread.shape[0]):
            natural[:, x, :, part * LANES : (part + 1) * LANES] = (
                spread[part].reshape(chans, rows, LANES).astype(bf16)
            )


def own_gradient_kernel(weights, field, total, natural, spread):
    chans, _, rows, _ = natural.shape
    total[...] = jnp.zeros(total.shape, f32)
    add_own(
        weights,
        (
            (field, 1, 0, 0, True),
            (field, 1, 1, 1, True),
            (field, rows - 2, 2, 2, False),
            (field, 1, rows, rows, True),
            (field, 1, rows + 1, rows + 1, True),
        ),
        total,
    )
    from_rows(lambda y, x: field[y + 1, x, :chans].astype(f32), natural, spread)


def update_kernel(partial, first, second, field, given, mask, natural, spread):
    chans, layers, _, _ = natural.shape
    direct, _, _ = place_flags()

    def value(y, x):
        gradient = partial[y, x * chans : (x + 1) * chans] - field[y + 1, x, :chans].astype(f32)
        if x == 0:
            gradient += jnp.where(direct, first[y], second[y]).astype(f32)
        if x == layers - 1:
            gradient += jnp.where(direct, second[y], first[y]).astype(f32)
        keep = 1.0 - mask[pl.ds(y, 1)].astype(f32)
        return given[y, x].astype(f32) - step_size * keep * gradient

    from_rows(value, natural, spread)


def call(kernel, shape, scratch, *args):
    return pl.pallas_call(
        kernel,
        out_shape=shape,
        scratch_shapes=scratch,
        compiler_params=pltpu.CompilerParams(vmem_limit_bytes=VMEM_LIMIT),
    )(*args)


def like(*shape, dtype=bf16):
    return jax.ShapeDtypeStruct(shape, dtype)


def around_x(layout, *segments):
    rows = sum(count for _, _, count in layout)
    layers, chans, depth = segments[0].shape[1:]
    side = like(rows, chans, depth)
    joined = pltpu.VMEM((rows, layers, chans, depth), bf16)
    kernel = functools.partial(sides_kernel, layout)
    right, left = call(kernel, (side, side), [joined], *segments)
    return send(right, to_right), send(left, to_left)


def step(kspace, kernel, mask):
    chans, layers, rows, depth = kspace.shape
    wide = layers * 2 * chans
    edge = max(2, rows * OUTER // 32)
    block = lambda count: like(count, layers, chans, depth)
    spread = pltpu.VMEM((depth // LANES, chans * rows, LANES), f32)
    total = like(rows + 2, wide, depth, dtype=f32)

    given, head, tail, outer, inner = call(
        prepare_kernel,
        (block(rows), block(2), block(2), block(2 * edge), block(rows - 2 * edge)),
        [spread, spread],
        kspace,
    )
    top, bottom = send(tail, to_next), send(head, to_previous)
    outer = send(outer, to_mirror)
    inner = send(inner, to_mirror)
    layout = ((0, 0, 2), (1, 0, rows), (2, 0, 2))
    first, second = around_x(layout, top, given, bottom)

    early, early_sides, late, late_sides, adjoint, outward = call(
        weights_kernel,
        (
            like(3 * wide, 3 * layers * chans),
            like(2, 6 * chans, 3 * chans),
            like(3 * wide, 3 * layers * chans),
            like(2, 6 * chans, 3 * chans),
            like(3 * layers * chans, 3 * wide),
            like(2, 3 * chans, 6 * chans),
        ),
        [pltpu.VMEM((3, 3, 3, 2 * chans, 2 * chans), f32), pltpu.VMEM((3, 3, 3, chans, 2 * chans), f32)],
        kernel,
    )
    partial = call(early_kernel, total, [], early, top, given, bottom)

    virtual_top = send(outer[-2:], to_next)
    virtual_bottom = send(outer[:2], to_previous)
    partial = call(middle_kernel, total, [], early_sides, first, second, partial)

    layout = ((0, 0, 2), (1, 0, edge), (2, 0, rows - 2 * edge), (1, edge, edge), (3, 0, 2))
    first, second = around_x(layout, virtual_top, outer, inner, virtual_bottom)
    partial = call(
        inner_kernel, total, [], late, virtual_top, outer, inner, virtual_bottom, partial
    )
    side = like(rows, chans, depth)
    field, right, left = call(
        residual_kernel,
        (like(rows + 2, layers, 2 * chans, depth), side, side),
        [pltpu.VMEM(total.shape, f32), pltpu.VMEM((2, rows, chans, depth), f32)],
        late_sides, outward, first, second, partial,
        top, given, bottom, virtual_top, outer, virtual_bottom, inner,
    )
    first, second = send(right, to_right), send(left, to_left)
    natural = like(chans, layers, rows, depth)
    partial, residual = call(
        own_gradient_kernel,
        (like(rows, layers * chans, depth, dtype=f32), natural),
        [spread],
        adjoint, field,
    )
    updated = call(update_kernel, natural, [spread], partial, first, second, field, given, mask)
    return updated, residual


def solution(mesh):
    spec = P(None, "kx", "ky", None)
    return jax.shard_map(
        step,
        mesh=mesh,
        in_specs=(spec, P(), P("ky", None)),
        out_specs=(spec, spec),
        check_vma=False,
    )
```

time: 166 us -> 124 us (0.75)
  the two profiles are of different devices: /device:TPU:18 before, /device:TPU:16 now
where the time goes in v2:
time: 124 us
  waiting for transfers between devices  44.8 us (36%)
  Pallas kernels  42.1 us (34%)
  starting transfers between devices  34.1 us (28%)
  local copies, waits for them, and re-layouts  2.25 us (2%)
    ppermute x12, waiting for transfers between devices, send(): return lax.ppermute(value, AXES, pairs)  44.8 us
    pallas_call x10, Pallas kernels, call(): pl.pallas_call(kernel, out_shape=shape, scratch_shapes=scratch, compiler_...  42.1 us
    ppermute x12, starting transfers between devices, send(): return lax.ppermute(value, AXES, pairs)  34.1 us
  transfers between devices with their start and end apart: 12, of which 2 were waited for; matrix products, arithmetic and copies ran while one was open for 0% of the time, Pallas kernels for 21%

profile of v2, /device:TPU:16, one launch (start us, length us, event | category | flops | bytes accessed | tf_op | source)
XLA Modules:
  0.0 124.0 jit_solution(7475832182611941003)
XLA Ops:
  0.6 0.0 copy-start
  0.6 1.2 copy-done
  1.9 1.9 %shard_map.51 = (bf16[16,2,64,256]{3,2,1,0:T(8,128)(2,1)S(1)}, bf16[2,2,64,256]{3,2,1,0:T(8,128)(2,1)S(1)}, bf16[2,2,64,256]{3,2,1,0:T(8,128)(2,1)S(1)}, bf16[4,...) custom-call(bf16[64,2,16,256]{3,2,1,0:T(8,128)(2,1)S(1)} %copy-done), custom_call_target="tpu_custom_call" | custom-call | tf_op jit(solution)/shard_map/pallas_call | solution.py:446
  3.8 1.8 %collective-permute-start.2 = (bf16[12,2,64,256]{3,2,1,0:T(8,128)(2,1)S(1)}, bf16[12,2,64,256]{3,2,1,0:T(8,128)(2,1)S(1)}, u32[]{:S(2)}, u32[]{:S(2)}) collective-permute-start(bf16[12,2,64,256]{3,2,1,0:T(8,128)(2,1)S(1)} %get-tuple-element.26), channel_id=1, source_target_pairs={{0,31},{1,30},{2,29},{3,28},{4,27},{5,26},{6,25},{7,24},{8,23},{9,... | collective-permute-start | bytes 2359304 | tf_op jit(solution)/shard_map/ppermute | solution.py:61
  5.6 1.8 %collective-permute-start = (bf16[4,2,64,256]{3,2,1,0:T(8,128)(2,1)S(1)}, bf16[4,2,64,256]{3,2,1,0:T(8,128)(2,1)S(1)}, u32[]{:S(2)}, u32[]{:S(2)}) collective-permute-start(bf16[4,2,64,256]{3,2,1,0:T(8,128)(2,1)S(1)} %get-tuple-element.25), channel_id=1, source_target_pairs={{0,31},{1,30},{2,29},{3,28},{4,27},{5,26},{6,25},{7,24},{8,23},{9,... | collective-permute-start | bytes 786440 | tf_op jit(solution)/shard_map/ppermute | solution.py:61
  7.4 3.4 %collective-permute-start.6 = (bf16[2,2,64,256]{3,2,1,0:T(8,128)(2,1)S(1)}, bf16[2,2,64,256]{3,2,1,0:T(8,128)(2,1)S(1)}, u32[]{:S(2)}, u32[]{:S(2)}) collective-permute-start(bf16[2,2,64,256]{3,2,1,0:T(8,128)(2,1)S(1)} %get-tuple-element.31), channel_id=1, source_target_pairs={{0,1},{1,2},{2,3},{4,5},{5,6},{6,7},{8,9},{9,10},{10,11},{12,13},{... | collective-permute-start | bytes 393224 | tf_op jit(solution)/shard_map/ppermute | solution.py:61
  10.8 1.3 %collective-permute-start.7 = (bf16[2,2,64,256]{3,2,1,0:T(8,128)(2,1)S(1)}, bf16[2,2,64,256]{3,2,1,0:T(8,128)(2,1)S(1)}, u32[]{:S(2)}, u32[]{:S(2)}) collective-permute-start(bf16[2,2,64,256]{3,2,1,0:T(8,128)(2,1)S(1)} %get-tuple-element.33), channel_id=1, source_target_pairs={{1,0},{2,1},{3,2},{5,4},{6,5},{7,6},{9,8},{10,9},{11,10},{13,12},{... | collective-permute-start | bytes 393224 | tf_op jit(solution)/shard_map/ppermute | solution.py:61
  12.1 41.5 %collective-permute-done.refs_1_.outer.virtual_outer = bf16[4,2,64,256]{3,2,1,0:T(8,128)(2,1)S(1)} collective-permute-done((bf16[4,2,64,256]{3,2,1,0:T(8,128)(2,1)S(1)}, bf16[4,2,64,256]{3,2,1,0:T(8,128)(2,1)S(1)}, u32[]{:S(2)}, u32[]{:S(2)}) %collective-permute-start) | collective-permute-done | bytes 262176 | tf_op jit(solution)/shard_map/ppermute | solution.py:61
  53.6 3.4 %collective-permute-start.1 = (bf16[2,2,64,256]{3,2,1,0:T(8,128)(2,1)S(1)}, bf16[2,2,64,256]{3,2,1,0:T(8,128)(2,1)S(1)}, u32[]{:S(2)}, u32[]{:S(2)}) collective-permute-start(bf16[2,2,64,256]{3,2,1,0:T(8,128)(2,1)S(1)} %get-tuple-element.43), channel_id=1, source_target_pairs={{0,1},{1,2},{2,3},{4,5},{5,6},{6,7},{8,9},{9,10},{10,11},{12,13},{... | collective-permute-start | bytes 393224 | tf_op jit(solution)/shard_map/ppermute | solution.py:61
  57.0 1.3 %collective-permute-start.3 = (bf16[2,2,64,256]{3,2,1,0:T(8,128)(2,1)S(1)}, bf16[2,2,64,256]{3,2,1,0:T(8,128)(2,1)S(1)}, u32[]{:S(2)}, u32[]{:S(2)}) collective-permute-start(bf16[2,2,64,256]{3,2,1,0:T(8,128)(2,1)S(1)} %get-tuple-element.42), channel_id=1, source_target_pairs={{1,0},{2,1},{3,2},{5,4},{6,5},{7,6},{9,8},{10,9},{11,10},{13,12},{... | collective-permute-start | bytes 393224 | tf_op jit(solution)/shard_map/ppermute | solution.py:61
  58.3 0.0 collective-permute-done.6.refs_0_.top
  58.3 0.0 collective-permute-done.7.refs_2_.bottom
  58.3 1.2 shard_map.53
  59.5 5.5 %collective-permute-start.8 = (bf16[20,64,256]{2,1,0:T(8,128)(2,1)S(1)}, bf16[20,64,256]{2,1,0:T(8,128)(2,1)S(1)}, u32[]{:S(2)}, u32[]{:S(2)}) collective-permute-start(bf16[20,64,256]{2,1,0:T(8,128)(2,1)S(1)} %get-tuple-element.34), channel_id=1, source_target_pairs={{0,4},{1,5},{4,8},{5,9},{6,2},{7,3},{8,12},{9,13},{10,6},{11,7},{1... | collective-permute-start | bytes 1966088 | tf_op jit(solution)/shard_map/ppermute | solution.py:61
  65.0 1.9 %collective-permute-start.9 = (bf16[20,64,256]{2,1,0:T(8,128)(2,1)S(1)}, bf16[20,64,256]{2,1,0:T(8,128)(2,1)S(1)}, u32[]{:S(2)}, u32[]{:S(2)}) collective-permute-start(bf16[20,64,256]{2,1,0:T(8,128)(2,1)S(1)} %get-tuple-element.35), channel_id=1, source_target_pairs={{2,6},{3,7},{4,0},{5,1},{6,10},{7,11},{8,4},{9,5},{10,14},{11,15},... | collective-permute-start | bytes 1966088 | tf_op jit(solution)/shard_map/ppermute | solution.py:61
  66.9 0.0 collective-permute-done.1.refs_0_.top.virtual_top
  66.9 0.0 collective-permute-done.3.refs_3_.bottom.virtual_bottom
  67.0 0.0 collective-permute-done.2.refs_2_.inner.virtual_inner
  67.0 1.1 shard_map.52
  68.1 4.8 %collective-permute-start.4 = (bf16[20,64,256]{2,1,0:T(8,128)(2,1)S(1)}, bf16[20,64,256]{2,1,0:T(8,128)(2,1)S(1)}, u32[]{:S(2)}, u32[]{:S(2)}) collective-permute-start(bf16[20,64,256]{2,1,0:T(8,128)(2,1)S(1)} %get-tuple-element.27), channel_id=1, source_target_pairs={{0,4},{1,5},{4,8},{5,9},{6,2},{7,3},{8,12},{9,13},{10,6},{11,7},{1... | collective-permute-start | bytes 1966088 | tf_op jit(solution)/shard_map/ppermute | solution.py:61
  73.0 2.1 %collective-permute-start.5 = (bf16[20,64,256]{2,1,0:T(8,128)(2,1)S(1)}, bf16[20,64,256]{2,1,0:T(8,128)(2,1)S(1)}, u32[]{:S(2)}, u32[]{:S(2)}) collective-permute-start(bf16[20,64,256]{2,1,0:T(8,128)(2,1)S(1)} %get-tuple-element.28), channel_id=1, source_target_pairs={{2,6},{3,7},{4,0},{5,1},{6,10},{7,11},{8,4},{9,5},{10,14},{11,15},... | collective-permute-start | bytes 1966088 | tf_op jit(solution)/shard_map/ppermute | solution.py:61
  75.1 0.0 copy-start.1
  75.1 1.0 copy-done.1
  76.1 1.6 %shard_map.50 = (bf16[768,384]{1,0:T(8,128)(2,1)S(1)}, bf16[2,384,192]{2,1,0:T(8,128)(2,1)S(1)}, bf16[768,384]{1,0:T(8,128)(2,1)S(1)}, bf16[2,384,192]{2,1,0:T(8...) custom-call(bf16[3,3,3,64,128]{4,3,2,1,0:T(8,128)(2,1)S(1)} %copy-done.1), custom_call_target="tpu_custom_call" | custom-call | tf_op jit(solution)/shard_map/pallas_call | solution.py:446
  77.7 5.7 %shard_map.54.partial = f32[18,256,256]{2,1,0:T(8,128)S(1)} custom-call(bf16[768,384]{1,0:T(8,128)(2,1)S(1)} %get-tuple-element.36.weights, bf16[2,2,64,256]{3,2,1,0:T(8,128)(2,1)S(1)} %collective-permute-done.6.refs_0_.top, bf16[16,2,64,256]{3,2,1,0:T(8,128)(2,1)S(1)} %get-tuple-element.32.refs_1_.own.given, ...), custom_call_target="tpu_custom_call" | custom-call | tf_op jit(solution)/shard_map/pallas_call | solution.py:446
  83.4 0.0 collective-permute-done.8.first
  83.4 0.0 collective-permute-done.9.second
  83.4 4.6 %shard_map.55.partial = f32[18,256,256]{2,1,0:T(8,128)S(1)} custom-call(bf16[2,384,192]{2,1,0:T(8,128)(2,1)S(1)} %get-tuple-element.30.sides, bf16[20,64,256]{2,1,0:T(8,128)(2,1)S(1)} %collective-permute-done.8.first, bf16[20,64,256]{2,1,0:T(8,128)(2,1)S(1)} %collective-permute-done.9.second, f32[18,256,256]{2,1,0:T(8,128)S(1)} %shard_map.54.partial), custom_call_target="tpu_custom_call" | custom-call | tf_op jit(solution)/shard_map/pallas_call | solution.py:446
  88.0 5.4 %shard_map.56.partial = f32[18,256,256]{2,1,0:T(8,128)S(1)} custom-call(bf16[768,384]{1,0:T(8,128)(2,1)S(1)} %get-tuple-element.29.weights, bf16[2,2,64,256]{3,2,1,0:T(8,128)(2,1)S(1)} %collective-permute-done.1.refs_0_.top.virtual_top, bf16[4,2,64,256]{3,2,1,0:T(8,128)(2,1)S(1)} %collective-permute-done.refs_1_.outer.virtual_outer, ...), custom_call_target="tpu_custom_call" | custom-call | tf_op jit(solution)/shard_map/pallas_call | solution.py:446
  93.4 0.0 collective-permute-done.4.first
  93.5 0.0 collective-permute-done.5.second
  93.5 0.0 copy-start.2
  93.5 11.4 %shard_map.57 = (bf16[18,2,128,256]{3,2,1,0:T(8,128)(2,1)S(1)}, bf16[16,64,256]{2,1,0:T(8,128)(2,1)S(1)}, bf16[16,64,256]{2,1,0:T(8,128)(2,1)S(1)}) custom-call(bf16[2,384,192]{2,1,0:T(8,128)(2,1)S(1)} %get-tuple-element.23.sides, bf16[2,192,384]{2,1,0:T(8,128)(2,1)S(1)} %get-tuple-element.24.outward, bf16[20,64,256]{2,1,0:T(8,128)(2,1)S(1)} %collective-permute-done.4.first, ...), custom_call_target="tpu_custom_call" | custom-call | tf_op jit(solution)/shard_map/pallas_call | solution.py:446
  104.8 4.8 %collective-permute-start.10 = (bf16[16,64,256]{2,1,0:T(8,128)(2,1)S(1)}, bf16[16,64,256]{2,1,0:T(8,128)(2,1)S(1)}, u32[]{:S(2)}, u32[]{:S(2)}) collective-permute-start(bf16[16,64,256]{2,1,0:T(8,128)(2,1)S(1)} %get-tuple-element.39), channel_id=1, source_target_pairs={{0,4},{1,5},{4,8},{5,9},{6,2},{7,3},{8,12},{9,13},{10,6},{11,7},{1... | collective-permute-start | bytes 1572872 | tf_op jit(solution)/shard_map/ppermute | solution.py:61
  109.7 1.9 %collective-permute-start.11 = (bf16[16,64,256]{2,1,0:T(8,128)(2,1)S(1)}, bf16[16,64,256]{2,1,0:T(8,128)(2,1)S(1)}, u32[]{:S(2)}, u32[]{:S(2)}) collective-permute-start(bf16[16,64,256]{2,1,0:T(8,128)(2,1)S(1)} %get-tuple-element.40), channel_id=1, source_target_pairs={{2,6},{3,7},{4,0},{5,1},{6,10},{7,11},{8,4},{9,5},{10,14},{11,15},... | collective-permute-start | bytes 1572872 | tf_op jit(solution)/shard_map/ppermute | solution.py:61
  111.6 6.8 %shard_map.58 = (f32[16,128,256]{2,1,0:T(8,128)S(1)}, bf16[64,2,16,256]{3,2,1,0:T(8,128)(2,1)}) custom-call(bf16[384,768]{1,0:T(8,128)(2,1)S(1)} %get-tuple-element.22.weights, bf16[18,2,128,256]{3,2,1,0:T(8,128)(2,1)S(1)} %get-tuple-element.37.field), custom_call_target="tpu_custom_call" | custom-call | tf_op jit(solution)/shard_map/pallas_call | solution.py:446
  118.4 0.0 collective-permute-done.10.first
  118.4 3.3 %collective-permute-done.11.second = bf16[16,64,256]{2,1,0:T(8,128)(2,1)S(1)} collective-permute-done((bf16[16,64,256]{2,1,0:T(8,128)(2,1)S(1)}, bf16[16,64,256]{2,1,0:T(8,128)(2,1)S(1)}, u32[]{:S(2)}, u32[]{:S(2)}) %collective-permute-start.11) | collective-permute-done | bytes 524320 | tf_op jit(solution)/shard_map/ppermute | solution.py:61
  121.6 0.0 copy-done.2
  121.6 2.4 %shard_map.59 = bf16[64,2,16,256]{3,2,1,0:T(8,128)(2,1)} custom-call(f32[16,128,256]{2,1,0:T(8,128)S(1)} %get-tuple-element.38.partial, bf16[16,64,256]{2,1,0:T(8,128)(2,1)S(1)} %collective-permute-done.10.first, bf16[16,64,256]{2,1,0:T(8,128)(2,1)S(1)} %collective-permute-done.11.second, bf16[18,2,128,256]{3,2,1,0:T(8,128)(2,1)S(1)} %get-tuple-element.37.field, ...), custom_call_target="tpu_custom_call" | custom-call | tf_op jit(solution)/shard_map/pallas_call | solution.py:446
  (1 shorter events, 0.0 us)
Async XLA Ops:
  0.6 1.2 copy-start
  3.8 63.2 %collective-permute-start.2 = (bf16[12,2,64,256]{3,2,1,0:T(8,128)(2,1)S(1)}, bf16[12,2,64,256]{3,2,1,0:T(8,128)(2,1)S(1)}, u32[]{:S(2)}, u32[]{:S(2)}) collective-permute-start(bf16[12,2,64,256]{3,2,1,0:T(8,128)(2,1)S(1)} %get-tuple-element.26), channel_id=1, source_target_pairs={{0,31},{1,30},{2,29},{3,28},{4,27},{5,26},{6,25},{7,24},{8,23},{9,... | collective-permute-start | bytes 2359304 | tf_op jit(solution)/shard_map/ppermute | solution.py:61
  5.6 47.9 %collective-permute-start = (bf16[4,2,64,256]{3,2,1,0:T(8,128)(2,1)S(1)}, bf16[4,2,64,256]{3,2,1,0:T(8,128)(2,1)S(1)}, u32[]{:S(2)}, u32[]{:S(2)}) collective-permute-start(bf16[4,2,64,256]{3,2,1,0:T(8,128)(2,1)S(1)} %get-tuple-element.25), channel_id=1, source_target_pairs={{0,31},{1,30},{2,29},{3,28},{4,27},{5,26},{6,25},{7,24},{8,23},{9,... | collective-permute-start | bytes 786440 | tf_op jit(solution)/shard_map/ppermute | solution.py:61
  7.4 50.9 %collective-permute-start.6 = (bf16[2,2,64,256]{3,2,1,0:T(8,128)(2,1)S(1)}, bf16[2,2,64,256]{3,2,1,0:T(8,128)(2,1)S(1)}, u32[]{:S(2)}, u32[]{:S(2)}) collective-permute-start(bf16[2,2,64,256]{3,2,1,0:T(8,128)(2,1)S(1)} %get-tuple-element.31), channel_id=1, source_target_pairs={{0,1},{1,2},{2,3},{4,5},{5,6},{6,7},{8,9},{9,10},{10,11},{12,13},{... | collective-permute-start | bytes 393224 | tf_op jit(solution)/shard_map/ppermute | solution.py:61
  10.8 47.5 %collective-permute-start.7 = (bf16[2,2,64,256]{3,2,1,0:T(8,128)(2,1)S(1)}, bf16[2,2,64,256]{3,2,1,0:T(8,128)(2,1)S(1)}, u32[]{:S(2)}, u32[]{:S(2)}) collective-permute-start(bf16[2,2,64,256]{3,2,1,0:T(8,128)(2,1)S(1)} %get-tuple-element.33), channel_id=1, source_target_pairs={{1,0},{2,1},{3,2},{5,4},{6,5},{7,6},{9,8},{10,9},{11,10},{13,12},{... | collective-permute-start | bytes 393224 | tf_op jit(solution)/shard_map/ppermute | solution.py:61
  53.6 13.3 %collective-permute-start.1 = (bf16[2,2,64,256]{3,2,1,0:T(8,128)(2,1)S(1)}, bf16[2,2,64,256]{3,2,1,0:T(8,128)(2,1)S(1)}, u32[]{:S(2)}, u32[]{:S(2)}) collective-permute-start(bf16[2,2,64,256]{3,2,1,0:T(8,128)(2,1)S(1)} %get-tuple-element.43), channel_id=1, source_target_pairs={{0,1},{1,2},{2,3},{4,5},{5,6},{6,7},{8,9},{9,10},{10,11},{12,13},{... | collective-permute-start | bytes 393224 | tf_op jit(solution)/shard_map/ppermute | solution.py:61
  57.0 9.9 %collective-permute-start.3 = (bf16[2,2,64,256]{3,2,1,0:T(8,128)(2,1)S(1)}, bf16[2,2,64,256]{3,2,1,0:T(8,128)(2,1)S(1)}, u32[]{:S(2)}, u32[]{:S(2)}) collective-permute-start(bf16[2,2,64,256]{3,2,1,0:T(8,128)(2,1)S(1)} %get-tuple-element.42), channel_id=1, source_target_pairs={{1,0},{2,1},{3,2},{5,4},{6,5},{7,6},{9,8},{10,9},{11,10},{13,12},{... | collective-permute-start | bytes 393224 | tf_op jit(solution)/shard_map/ppermute | solution.py:61
  59.5 23.9 %collective-permute-start.8 = (bf16[20,64,256]{2,1,0:T(8,128)(2,1)S(1)}, bf16[20,64,256]{2,1,0:T(8,128)(2,1)S(1)}, u32[]{:S(2)}, u32[]{:S(2)}) collective-permute-start(bf16[20,64,256]{2,1,0:T(8,128)(2,1)S(1)} %get-tuple-element.34), channel_id=1, source_target_pairs={{0,4},{1,5},{4,8},{5,9},{6,2},{7,3},{8,12},{9,13},{10,6},{11,7},{1... | collective-permute-start | bytes 1966088 | tf_op jit(solution)/shard_map/ppermute | solution.py:61
  65.0 18.4 %collective-permute-start.9 = (bf16[20,64,256]{2,1,0:T(8,128)(2,1)S(1)}, bf16[20,64,256]{2,1,0:T(8,128)(2,1)S(1)}, u32[]{:S(2)}, u32[]{:S(2)}) collective-permute-start(bf16[20,64,256]{2,1,0:T(8,128)(2,1)S(1)} %get-tuple-element.35), channel_id=1, source_target_pairs={{2,6},{3,7},{4,0},{5,1},{6,10},{7,11},{8,4},{9,5},{10,14},{11,15},... | collective-permute-start | bytes 1966088 | tf_op jit(solution)/shard_map/ppermute | solution.py:61
  68.1 25.3 %collective-permute-start.4 = (bf16[20,64,256]{2,1,0:T(8,128)(2,1)S(1)}, bf16[20,64,256]{2,1,0:T(8,128)(2,1)S(1)}, u32[]{:S(2)}, u32[]{:S(2)}) collective-permute-start(bf16[20,64,256]{2,1,0:T(8,128)(2,1)S(1)} %get-tuple-element.27), channel_id=1, source_target_pairs={{0,4},{1,5},{4,8},{5,9},{6,2},{7,3},{8,12},{9,13},{10,6},{11,7},{1... | collective-permute-start | bytes 1966088 | tf_op jit(solution)/shard_map/ppermute | solution.py:61
  73.0 20.5 %collective-permute-start.5 = (bf16[20,64,256]{2,1,0:T(8,128)(2,1)S(1)}, bf16[20,64,256]{2,1,0:T(8,128)(2,1)S(1)}, u32[]{:S(2)}, u32[]{:S(2)}) collective-permute-start(bf16[20,64,256]{2,1,0:T(8,128)(2,1)S(1)} %get-tuple-element.28), channel_id=1, source_target_pairs={{2,6},{3,7},{4,0},{5,1},{6,10},{7,11},{8,4},{9,5},{10,14},{11,15},... | collective-permute-start | bytes 1966088 | tf_op jit(solution)/shard_map/ppermute | solution.py:61
  75.1 1.0 copy-start.1
  93.5 28.2 %copy-start.2 = (s32[16,256]{1,0:T(8,128)S(1)}, s32[16,256]{1,0:T(8,128)}, u32[]{:S(2)}) copy-start(s32[16,256]{1,0:T(8,128)} %mask.1) | copy-start | bytes 49156
  104.8 13.5 %collective-permute-start.10 = (bf16[16,64,256]{2,1,0:T(8,128)(2,1)S(1)}, bf16[16,64,256]{2,1,0:T(8,128)(2,1)S(1)}, u32[]{:S(2)}, u32[]{:S(2)}) collective-permute-start(bf16[16,64,256]{2,1,0:T(8,128)(2,1)S(1)} %get-tuple-element.39), channel_id=1, source_target_pairs={{0,4},{1,5},{4,8},{5,9},{6,2},{7,3},{8,12},{9,13},{10,6},{11,7},{1... | collective-permute-start | bytes 1572872 | tf_op jit(solution)/shard_map/ppermute | solution.py:61
  109.7 12.0 %collective-permute-start.11 = (bf16[16,64,256]{2,1,0:T(8,128)(2,1)S(1)}, bf16[16,64,256]{2,1,0:T(8,128)(2,1)S(1)}, u32[]{:S(2)}, u32[]{:S(2)}) collective-permute-start(bf16[16,64,256]{2,1,0:T(8,128)(2,1)S(1)} %get-tuple-element.40), channel_id=1, source_target_pairs={{2,6},{3,7},{4,0},{5,1},{6,10},{7,11},{8,4},{9,5},{10,14},{11,15},... | collective-permute-start | bytes 1572872 | tf_op jit(solution)/shard_map/ppermute | solution.py:61

commit v3 on v2

--- a/solution.py
+++ b/solution.py
@@ -11,6 +11,7 @@
 step_size = 0.5
 LANES = 128
 OUTER = 4
+MIDDLE = 6
 VMEM_LIMIT = 40 << 20
 AXES = ("kx", "ky")
 f32 = jnp.float32
@@ -178,11 +179,14 @@
     )
 
 
-def prepare_kernel(natural, given, first_rows, last_rows, outer, inner, spread, turned):
+def prepare_kernel(natural, given, first_rows, last_rows, outer, middle, inner, spread, turned):
     chans, layers, rows, depth = natural.shape
     flip = reversal(depth)
     signs = sign_rows(chans, chans)
-    edge = outer.shape[0] // 2
+    groups, start = [], 0
+    for ref in (outer, middle):
+        groups.append((ref, start, ref.shape[0] // 2))
+        start += ref.shape[0] // 2
     for x in range(layers):
         whole = natural[:, x].reshape(chans * rows, depth)
         mirrored = dot(whole, flip)
@@ -199,12 +203,14 @@
                 last_rows[y - rows + 2, x] = block
             target = rows - 1 - y
             block = (row_from(turned, y, chans, rows) * signs).astype(bf16)
-            if target < edge:
-                outer[target, layers - 1 - x] = block
-            elif target < rows - edge:
-                inner[target - edge, layers - 1 - x] = block
-            else:
-                outer[target - rows + 2 * edge, layers - 1 - x] = block
+            for ref, start, half in groups:
+                if start <= target < start + half:
+                    ref[target - start, layers - 1 - x] = block
+                if start <= rows - 1 - target < start + half:
+                    ref[target - rows + start + 2 * half, layers - 1 - x] = block
+            first_inner = (rows - inner.shape[0]) // 2
+            if first_inner <= target < first_inner + inner.shape[0]:
+                inner[target - first_inner, layers - 1 - x] = block
 
 
 def emit_sides(read, rows, group, chans, depth, layers, signs, right, left):
@@ -247,7 +253,7 @@
         joined[start : start + count] = segments[index][offset : offset + count]
         start += count
     signs = sign_rows(chans, chans)
-    emit_sides(lambda y, x: joined[y, x], rows, 4, chans, depth, layers, signs, right, left)
+    emit_sides(lambda y, x: joined[y, x], rows, 2, chans, depth, layers, signs, right, left)
 
 
 def add_part(total, part, place, columns):
@@ -300,39 +306,55 @@
         )
 
 
-def early_kernel(weights, top, own, bottom, total):
-    rows = own.shape[0]
+def early_kernel(weights, own, total):
     total[...] = jnp.zeros(total.shape, f32)
-    add_own(
-        weights,
-        ((top, 2, 0, 0, True), (own, rows, 0, 2, False), (bottom, 2, 0, rows + 2, True)),
-        total,
-    )
-
-
-def middle_kernel(sides, first, second, partial, total):
+    add_own(weights, ((own, own.shape[0], 0, 2, False),), total)
+
+
+def given_kernel(sides, first, second, partial, total):
     rows = total.shape[0] - 2
     layers = 3 * total.shape[1] // sides.shape[1]
     total[...] = partial[...]
-    add_all_sides(sides, first, second, rows, total, side_columns(total, layers))
-
-
-def add_all_sides(sides, first, second, rows, total, columns):
-    for offset, count, static in ((0, 2, True), (2, rows, False), (rows + 2, 2, True)):
-        add_sides(sides, first, second, offset, count, offset, total, columns, static)
-
-
-def inner_kernel(weights, top, outer, inner, bottom, partial, total):
+    add_sides(sides, first, second, 0, rows, 2, total, side_columns(total, layers), False)
+
+
+def outer_kernel(early, late, top, bottom, outer, middle, partial, total):
     rows = total.shape[0] - 2
-    edge = outer.shape[0] // 2
+    edge, half = outer.shape[0] // 2, middle.shape[0] // 2
+    total[...] = partial[...]
+    add_own(early, ((top, 2, 0, 0, True), (bottom, 2, 0, rows + 2, True)), total)
+    add_own(
+        late,
+        (
+            (outer, edge, 0, 2, True),
+            (middle, half, 0, 2 + edge, True),
+            (middle, half, half, rows + 2 - edge - half, True),
+            (outer, edge, edge, rows + 2 - edge, True),
+        ),
+        total,
+    )
+
+
+def middle_kernel(early_sides, late_sides, first, second, partial, total):
+    rows = total.shape[0] - 2
+    half = (first.shape[0] - 4) // 2
+    columns = side_columns(total, 3 * total.shape[1] // early_sides.shape[1])
+    total[...] = partial[...]
+    for offset, place in ((0, 0), (2 + 2 * half, rows + 2)):
+        add_sides(early_sides, first, second, offset, 2, place, total, columns, True)
+    for offset, place in ((2, 2), (2 + half, rows + 2 - half)):
+        add_sides(late_sides, first, second, offset, half, place, total, columns, True)
+
+
+def inner_kernel(weights, top, inner, bottom, partial, total):
+    rows = total.shape[0] - 2
+    count = inner.shape[0]
     total[...] = partial[...]
     add_own(
         weights,
         (
             (top, 2, 0, 0, True),
-            (outer, edge, 0, 2, True),
-            (inner, rows - 2 * edge, 0, 2 + edge, False),
-            (outer, edge, edge, rows + 2 - edge, True),
+            (inner, count, 0, 2 + (rows - count) // 2, True),
             (bottom, 2, 0, rows + 2, True),
         ),
         total,
@@ -341,15 +363,17 @@
 
 def residual_kernel(
     sides, outward, first, second, partial,
-    top, given, bottom, virtual_top, virtual_outer, virtual_bottom, virtual_inner,
+    top, given, bottom, virtual_top, virtual_outer, virtual_middle, virtual_bottom, virtual_inner,
     field, right, left, total, reach,
 ):
     rows, layers, chans, depth = given.shape
     span = rows + 2
-    edge = virtual_outer.shape[0] // 2
+    edge, half = virtual_outer.shape[0] // 2, virtual_middle.shape[0] // 2
+    inner = rows - 2 * edge - 2 * half
     total[...] = partial[...]
     columns = side_columns(total, layers)
-    add_all_sides(sides, first, second, rows, total, columns)
+    for offset, count, place in ((0, 2, 0), (2, inner, 2 + edge + half), (2 + inner, 2, rows + 2)):
+        add_sides(sides, first, second, offset, count, place, total, columns, True)
 
     def finish(target, k, t):
         both = jnp.concatenate([k, t], axis=1).astype(f32)
@@ -364,9 +388,16 @@
         lax.fori_loop(0, count, body, 0, unroll=2)
 
     finish(0, top[1], virtual_top[1])
-    loop(edge, 1, lambda y: given[y], lambda y: virtual_outer[y])
-    loop(rows - 2 * edge, 1 + edge, lambda y: given[y + edge], lambda y: virtual_inner[y])
-    loop(edge, 1 + rows - edge, lambda y: given[y + rows - edge], lambda y: virtual_outer[y + edge])
+    y = 0
+    for ref, offset, count in (
+        (virtual_outer, 0, edge), (virtual_middle, 0, half), (virtual_inner, 0, inner),
+        (virtual_middle, half, half), (virtual_outer, edge, edge),
+    ):
+        loop(
+            count, 1 + y, lambda j, y=y: given[j + y],
+            lambda j, ref=ref, offset=offset: ref[j + offset],
+        )
+        y += count
     finish(span - 1, bottom[0], virtual_bottom[0])
 
     direct, _, _ = place_flags()
@@ -469,21 +500,23 @@
     chans, layers, rows, depth = kspace.shape
     wide = layers * 2 * chans
     edge = max(2, rows * OUTER // 32)
-    block = lambda count: like(count, layers, chans, depth)
+    half = max(1, rows * MIDDLE // 32)
+    count = rows - 2 * edge - 2 * half
+    block = lambda size: like(size, layers, chans, depth)
     spread = pltpu.VMEM((depth // LANES, chans * rows, LANES), f32)
     total = like(rows + 2, wide, depth, dtype=f32)
 
-    given, head, tail, outer, inner = call(
+    given, head, tail, outer, middle, inner = call(
         prepare_kernel,
-        (block(rows), block(2), block(2), block(2 * edge), block(rows - 2 * edge)),
+        (block(rows), block(2), block(2), block(2 * edge), block(2 * half), block(count)),
         [spread, spread],
         kspace,
     )
+    outer = send(outer, to_mirror)
+    given_sides = around_x(((0, 0, rows),), given)
+    middle = send(middle, to_mirror)
     top, bottom = send(tail, to_next), send(head, to_previous)
-    outer = send(outer, to_mirror)
     inner = send(inner, to_mirror)
-    layout = ((0, 0, 2), (1, 0, rows), (2, 0, 2))
-    first, second = around_x(layout, top, given, bottom)
 
     early, early_sides, late, late_sides, adjoint, outward = call(
         weights_kernel,
@@ -498,24 +531,29 @@
         [pltpu.VMEM((3, 3, 3, 2 * chans, 2 * chans), f32), pltpu.VMEM((3, 3, 3, chans, 2 * chans), f32)],
         kernel,
     )
-    partial = call(early_kernel, total, [], early, top, given, bottom)
+    partial = call(early_kernel, total, [], early, given)
+    partial = call(given_kernel, total, [], early_sides, *given_sides, partial)
 
     virtual_top = send(outer[-2:], to_next)
     virtual_bottom = send(outer[:2], to_previous)
-    partial = call(middle_kernel, total, [], early_sides, first, second, partial)
-
-    layout = ((0, 0, 2), (1, 0, edge), (2, 0, rows - 2 * edge), (1, edge, edge), (3, 0, 2))
-    first, second = around_x(layout, virtual_top, outer, inner, virtual_bottom)
-    partial = call(
-        inner_kernel, total, [], late, virtual_top, outer, inner, virtual_bottom, partial
-    )
+    layout = (
+        (0, 0, 2), (1, 0, edge), (2, 0, half), (2, half, half), (1, edge, edge), (3, 0, 2)
+    )
+    first, second = around_x(layout, top, outer, middle, bottom)
+    partial = call(outer_kernel, total, [], early, late, top, bottom, outer, middle, partial)
+    middle_sides = first, second
+
+    layout = ((0, 0, 2), (1, 0, count), (2, 0, 2))
+    first, second = around_x(layout, virtual_top, inner, virtual_bottom)
+    partial = call(inner_kernel, total, [], late, virtual_top, inner, virtual_bottom, partial)
+    partial = call(middle_kernel, total, [], early_sides, late_sides, *middle_sides, partial)
     side = like(rows, chans, depth)
     field, right, left = call(
         residual_kernel,
         (like(rows + 2, layers, 2 * chans, depth), side, side),
         [pltpu.VMEM(total.shape, f32), pltpu.VMEM((2, rows, chans, depth), f32)],
         late_sides, outward, first, second, partial,
-        top, given, bottom, virtual_top, outer, virtual_bottom, inner,
+        top, given, bottom, virtual_top, outer, middle, virtual_bottom, inner,
     )
     first, second = send(right, to_right), send(left, to_left)
     natural = like(chans, layers, rows, depth)

time: 124 us -> 116 us (0.935)
  the two profiles are of different devices: /device:TPU:16 before, /device:TPU:18 now
where the time goes in v3:
time: 116 us; the launch traced here: 115 us
  Pallas kernels  41.6 us (36%)
  starting transfers between devices  37.7 us (33%)
  waiting for transfers between devices  32.6 us (28%)
  local copies, waits for them, and re-layouts  2.25 us (2%)
    pallas_call x13, Pallas kernels, call(): pl.pallas_call(kernel, out_shape=shape, scratch_shapes=scratch, compiler_...  41.6 us
    ppermute x15, starting transfers between devices, send(): return lax.ppermute(value, AXES, pairs)  37.7 us
    ppermute x15, waiting for transfers between devices, send(): return lax.ppermute(value, AXES, pairs)  32.6 us
  transfers between devices with their start and end apart: 15, of which 5 were waited for; matrix products, arithmetic and copies ran while one was open for 0% of the time, Pallas kernels for 25%

profile of v3, /device:TPU:18, one launch (start us, length us, event | category | flops | bytes accessed | tf_op | source)
XLA Modules:
  0.0 115.1 jit_solution(10005761535037072786)
XLA Ops:
  0.6 1.2 %copy-done = bf16[64,2,16,256]{3,2,1,0:T(8,128)(2,1)S(1)} copy-done((bf16[64,2,16,256]{3,2,1,0:T(8,128)(2,1)S(1)}, bf16[64,2,16,256]{3,2,1,0:T(8,128)(2,1)}, u32[]{:S(2)}) %copy-start) | copy-done | bytes 1048600
  1.9 1.9 %shard_map.51 = (bf16[16,2,64,256]{3,2,1,0:T(8,128)(2,1)S(1)}, bf16[2,2,64,256]{3,2,1,0:T(8,128)(2,1)S(1)}, bf16[2,2,64,256]{3,2,1,0:T(8,128)(2,1)S(1)}, bf16[4,...) custom-call(bf16[64,2,16,256]{3,2,1,0:T(8,128)(2,1)S(1)} %copy-done), custom_call_target="tpu_custom_call" | custom-call | tf_op jit(solution)/shard_map/pallas_call | solution.py:477
  3.8 0.9 collective-permute-start
  4.7 2.7 %collective-permute-start.7 = (bf16[6,2,64,256]{3,2,1,0:T(8,128)(2,1)S(1)}, bf16[6,2,64,256]{3,2,1,0:T(8,128)(2,1)S(1)}, u32[]{:S(2)}, u32[]{:S(2)}) collective-permute-start(bf16[6,2,64,256]{3,2,1,0:T(8,128)(2,1)S(1)} %get-tuple-element.34), channel_id=1, source_target_pairs={{0,31},{1,30},{2,29},{3,28},{4,27},{5,26},{6,25},{7,24},{8,23},{9,... | collective-permute-start | bytes 1179656 | tf_op jit(solution)/shard_map/ppermute | solution.py:62
  7.4 1.5 %shard_map.54 = (bf16[16,64,256]{2,1,0:T(8,128)(2,1)S(1)}, bf16[16,64,256]{2,1,0:T(8,128)(2,1)S(1)}) custom-call(bf16[16,2,64,256]{3,2,1,0:T(8,128)(2,1)S(1)} %get-tuple-element.40.refs_0_.own.given), custom_call_target="tpu_custom_call" | custom-call | tf_op jit(solution)/shard_map/pallas_call | solution.py:477
  8.9 3.4 %collective-permute-start.11 = (bf16[16,64,256]{2,1,0:T(8,128)(2,1)S(1)}, bf16[16,64,256]{2,1,0:T(8,128)(2,1)S(1)}, u32[]{:S(2)}, u32[]{:S(2)}) collective-permute-start(bf16[16,64,256]{2,1,0:T(8,128)(2,1)S(1)} %get-tuple-element.41), channel_id=1, source_target_pairs={{0,4},{1,5},{4,8},{5,9},{6,2},{7,3},{8,12},{9,13},{10,6},{11,7},{1... | collective-permute-start | bytes 1572872 | tf_op jit(solution)/shard_map/ppermute | solution.py:62
  12.3 1.9 %collective-permute-start.6 = (bf16[2,2,64,256]{3,2,1,0:T(8,128)(2,1)S(1)}, bf16[2,2,64,256]{3,2,1,0:T(8,128)(2,1)S(1)}, u32[]{:S(2)}, u32[]{:S(2)}) collective-permute-start(bf16[2,2,64,256]{3,2,1,0:T(8,128)(2,1)S(1)} %get-tuple-element.33), channel_id=1, source_target_pairs={{0,1},{1,2},{2,3},{4,5},{5,6},{6,7},{8,9},{9,10},{10,11},{12,13},{... | collective-permute-start | bytes 393224 | tf_op jit(solution)/shard_map/ppermute | solution.py:62
  14.2 3.9 %collective-permute-start.8 = (bf16[2,2,64,256]{3,2,1,0:T(8,128)(2,1)S(1)}, bf16[2,2,64,256]{3,2,1,0:T(8,128)(2,1)S(1)}, u32[]{:S(2)}, u32[]{:S(2)}) collective-permute-start(bf16[2,2,64,256]{3,2,1,0:T(8,128)(2,1)S(1)} %get-tuple-element.35), channel_id=1, source_target_pairs={{1,0},{2,1},{3,2},{5,4},{6,5},{7,6},{9,8},{10,9},{11,10},{13,12},{... | collective-permute-start | bytes 393224 | tf_op jit(solution)/shard_map/ppermute | solution.py:62
  18.2 18.6 %collective-permute-done.refs_1_.outer.virtual_outer = bf16[4,2,64,256]{3,2,1,0:T(8,128)(2,1)S(1)} collective-permute-done((bf16[4,2,64,256]{3,2,1,0:T(8,128)(2,1)S(1)}, bf16[4,2,64,256]{3,2,1,0:T(8,128)(2,1)S(1)}, u32[]{:S(2)}, u32[]{:S(2)}) %collective-permute-start) | collective-permute-done | bytes 262176 | tf_op jit(solution)/shard_map/ppermute | solution.py:62
  36.7 0.0 collective-permute-start.2
  36.7 0.0 collective-permute-done.6.refs_0_.top
  36.8 4.5 %collective-permute-start.1 = (bf16[2,2,64,256]{3,2,1,0:T(8,128)(2,1)S(1)}, bf16[2,2,64,256]{3,2,1,0:T(8,128)(2,1)S(1)}, u32[]{:S(2)}, u32[]{:S(2)}) collective-permute-start(bf16[2,2,64,256]{3,2,1,0:T(8,128)(2,1)S(1)} %get-tuple-element.49), channel_id=1, source_target_pairs={{0,1},{1,2},{2,3},{4,5},{5,6},{6,7},{8,9},{9,10},{10,11},{12,13},{... | collective-permute-start | bytes 393224 | tf_op jit(solution)/shard_map/ppermute | solution.py:62
  41.2 0.0 collective-permute-done.8.refs_3_.bottom
  41.2 1.9 %collective-permute-start.3 = (bf16[2,2,64,256]{3,2,1,0:T(8,128)(2,1)S(1)}, bf16[2,2,64,256]{3,2,1,0:T(8,128)(2,1)S(1)}, u32[]{:S(2)}, u32[]{:S(2)}) collective-permute-start(bf16[2,2,64,256]{3,2,1,0:T(8,128)(2,1)S(1)} %get-tuple-element.48), channel_id=1, source_target_pairs={{1,0},{2,1},{3,2},{5,4},{6,5},{7,6},{9,8},{10,9},{11,10},{13,12},{... | collective-permute-start | bytes 393224 | tf_op jit(solution)/shard_map/ppermute | solution.py:62
  43.2 2.1 %collective-permute-done.7.refs_2_.middle.virtual_middle = bf16[6,2,64,256]{3,2,1,0:T(8,128)(2,1)S(1)} collective-permute-done((bf16[6,2,64,256]{3,2,1,0:T(8,128)(2,1)S(1)}, bf16[6,2,64,256]{3,2,1,0:T(8,128)(2,1)S(1)}, u32[]{:S(2)}, u32[]{:S(2)}) %collective-permute-start.7) | collective-permute-done | bytes 393248 | tf_op jit(solution)/shard_map/ppermute | solution.py:62
  45.2 2.0 %collective-permute-start.12 = (bf16[16,64,256]{2,1,0:T(8,128)(2,1)S(1)}, bf16[16,64,256]{2,1,0:T(8,128)(2,1)S(1)}, u32[]{:S(2)}, u32[]{:S(2)}) collective-permute-start(bf16[16,64,256]{2,1,0:T(8,128)(2,1)S(1)} %get-tuple-element.42), channel_id=1, source_target_pairs={{2,6},{3,7},{4,0},{5,1},{6,10},{7,11},{8,4},{9,5},{10,14},{11,15},... | collective-permute-start | bytes 1572872 | tf_op jit(solution)/shard_map/ppermute | solution.py:62
  47.2 1.3 %shard_map.53 = (bf16[14,64,256]{2,1,0:T(8,128)(2,1)S(1)}, bf16[14,64,256]{2,1,0:T(8,128)(2,1)S(1)}) custom-call(bf16[2,2,64,256]{3,2,1,0:T(8,128)(2,1)S(1)} %collective-permute-done.6.refs_0_.top, bf16[4,2,64,256]{3,2,1,0:T(8,128)(2,1)S(1)} %collective-permute-done.refs_1_.outer.virtual_outer, ...), custom_call_target="tpu_custom_call" | custom-call | tf_op jit(solution)/shard_map/pallas_call | solution.py:477
  48.6 7.9 %collective-permute-done.1.refs_0_.top.virtual_top = bf16[2,2,64,256]{3,2,1,0:T(8,128)(2,1)S(1)} collective-permute-done((bf16[2,2,64,256]{3,2,1,0:T(8,128)(2,1)S(1)}, bf16[2,2,64,256]{3,2,1,0:T(8,128)(2,1)S(1)}, u32[]{:S(2)}, u32[]{:S(2)}) %collective-permute-start.1) | collective-permute-done | bytes 131104 | tf_op jit(solution)/shard_map/ppermute | solution.py:62
  56.5 1.9 %collective-permute-start.10 = (bf16[14,64,256]{2,1,0:T(8,128)(2,1)S(1)}, bf16[14,64,256]{2,1,0:T(8,128)(2,1)S(1)}, u32[]{:S(2)}, u32[]{:S(2)}) collective-permute-start(bf16[14,64,256]{2,1,0:T(8,128)(2,1)S(1)} %get-tuple-element.37), channel_id=1, source_target_pairs={{2,6},{3,7},{4,0},{5,1},{6,10},{7,11},{8,4},{9,5},{10,14},{11,15},... | collective-permute-start | bytes 1376264 | tf_op jit(solution)/shard_map/ppermute | solution.py:62
  58.4 0.8 collective-permute-done.3.refs_2_.bottom.virtual_bottom
  59.2 4.0 %collective-permute-start.9 = (bf16[14,64,256]{2,1,0:T(8,128)(2,1)S(1)}, bf16[14,64,256]{2,1,0:T(8,128)(2,1)S(1)}, u32[]{:S(2)}, u32[]{:S(2)}) collective-permute-start(bf16[14,64,256]{2,1,0:T(8,128)(2,1)S(1)} %get-tuple-element.36), channel_id=1, source_target_pairs={{0,4},{1,5},{4,8},{5,9},{6,2},{7,3},{8,12},{9,13},{10,6},{11,7},{1... | collective-permute-start | bytes 1376264 | tf_op jit(solution)/shard_map/ppermute | solution.py:62
  63.2 0.0 collective-permute-done.2.refs_1_.inner.virtual_inner
  63.2 0.9 shard_map.52
  64.2 1.9 %collective-permute-start.4 = (bf16[10,64,256]{2,1,0:T(8,128)(2,1)S(1)}, bf16[10,64,256]{2,1,0:T(8,128)(2,1)S(1)}, u32[]{:S(2)}, u32[]{:S(2)}) collective-permute-start(bf16[10,64,256]{2,1,0:T(8,128)(2,1)S(1)} %get-tuple-element.30), channel_id=1, source_target_pairs={{0,4},{1,5},{4,8},{5,9},{6,2},{7,3},{8,12},{9,13},{10,6},{11,7},{1... | collective-permute-start | bytes 983048 | tf_op jit(solution)/shard_map/ppermute | solution.py:62
  66.1 0.0 collective-permute-done.11.first
  66.1 2.4 %collective-permute-start.5 = (bf16[10,64,256]{2,1,0:T(8,128)(2,1)S(1)}, bf16[10,64,256]{2,1,0:T(8,128)(2,1)S(1)}, u32[]{:S(2)}, u32[]{:S(2)}) collective-permute-start(bf16[10,64,256]{2,1,0:T(8,128)(2,1)S(1)} %get-tuple-element.31), channel_id=1, source_target_pairs={{2,6},{3,7},{4,0},{5,1},{6,10},{7,11},{8,4},{9,5},{10,14},{11,15},... | collective-permute-start | bytes 983048 | tf_op jit(solution)/shard_map/ppermute | solution.py:62
  68.5 0.0 copy-start.1
  68.5 1.0 copy-done.1
  69.5 1.6 %shard_map.50 = (bf16[768,384]{1,0:T(8,128)(2,1)S(1)}, bf16[2,384,192]{2,1,0:T(8,128)(2,1)S(1)}, bf16[768,384]{1,0:T(8,128)(2,1)S(1)}, bf16[2,384,192]{2,1,0:T(8...) custom-call(bf16[3,3,3,64,128]{4,3,2,1,0:T(8,128)(2,1)S(1)} %copy-done.1), custom_call_target="tpu_custom_call" | custom-call | tf_op jit(solution)/shard_map/pallas_call | solution.py:477
  71.1 4.7 %shard_map.55.partial = f32[18,256,256]{2,1,0:T(8,128)S(1)} custom-call(bf16[768,384]{1,0:T(8,128)(2,1)S(1)} %get-tuple-element.39.weights.early, bf16[16,2,64,256]{3,2,1,0:T(8,128)(2,1)S(1)} %get-tuple-element.40.refs_0_.own.given), custom_call_target="tpu_custom_call" | custom-call | tf_op jit(solution)/shard_map/pallas_call | solution.py:477
  75.8 0.0 collective-permute-done.12.second
  75.9 3.8 %shard_map.56.partial = f32[18,256,256]{2,1,0:T(8,128)S(1)} custom-call(bf16[2,384,192]{2,1,0:T(8,128)(2,1)S(1)} %get-tuple-element.32.sides.early_sides, bf16[16,64,256]{2,1,0:T(8,128)(2,1)S(1)} %collective-permute-done.11.first, bf16[16,64,256]{2,1,0:T(8,128)(2,1)S(1)} %collective-permute-done.12.second, f32[18,256,256]{2,1,0:T(8,128)S(1)} %shard_map.55.partial), custom_call_target="tpu_custom_call" | custom-call | tf_op jit(solution)/shard_map/pallas_call | solution.py:477
  79.7 3.1 %shard_map.57.partial = f32[18,256,256]{2,1,0:T(8,128)S(1)} custom-call(bf16[768,384]{1,0:T(8,128)(2,1)S(1)} %get-tuple-element.39.weights.early, bf16[768,384]{1,0:T(8,128)(2,1)S(1)} %get-tuple-element.38.late.weights, bf16[2,2,64,256]{3,2,1,0:T(8,128)(2,1)S(1)} %collective-permute-done.6.refs_0_.top, ...), custom_call_target="tpu_custom_call" | custom-call | tf_op jit(solution)/shard_map/pallas_call | solution.py:477
  82.8 2.3 %shard_map.58.partial = f32[18,256,256]{2,1,0:T(8,128)S(1)} custom-call(bf16[768,384]{1,0:T(8,128)(2,1)S(1)} %get-tuple-element.38.late.weights, bf16[2,2,64,256]{3,2,1,0:T(8,128)(2,1)S(1)} %collective-permute-done.1.refs_0_.top.virtual_top, bf16[6,2,64,256]{3,2,1,0:T(8,128)(2,1)S(1)} %collective-permute-done.2.refs_1_.inner.virtual_inner, ...), custom_call_target="tpu_custom_call" | custom-call | tf_op jit(solution)/shard_map/pallas_call | solution.py:477
  85.1 0.0 collective-permute-done.10.second
  85.1 0.0 collective-permute-done.9.first
  85.1 2.8 %shard_map.59.partial = f32[18,256,256]{2,1,0:T(8,128)S(1)} custom-call(bf16[2,384,192]{2,1,0:T(8,128)(2,1)S(1)} %get-tuple-element.32.sides.early_sides, bf16[2,384,192]{2,1,0:T(8,128)(2,1)S(1)} %get-tuple-element.26.late_sides.sides, bf16[14,64,256]{2,1,0:T(8,128)(2,1)S(1)} %collective-permute-done.9.first, ...), custom_call_target="tpu_custom_call" | custom-call | tf_op jit(solution)/shard_map/pallas_call | solution.py:477
  87.9 0.0 collective-permute-done.4.first
  87.9 0.0 collective-permute-done.5.second
  87.9 0.0 copy-start.2
  87.9 8.5 %shard_map.60 = (bf16[18,2,128,256]{3,2,1,0:T(8,128)(2,1)S(1)}, bf16[16,64,256]{2,1,0:T(8,128)(2,1)S(1)}, bf16[16,64,256]{2,1,0:T(8,128)(2,1)S(1)}) custom-call(bf16[2,384,192]{2,1,0:T(8,128)(2,1)S(1)} %get-tuple-element.26.late_sides.sides, bf16[2,192,384]{2,1,0:T(8,128)(2,1)S(1)} %get-tuple-element.27.outward, ...), custom_call_target="tpu_custom_call" | custom-call | tf_op jit(solution)/shard_map/pallas_call | solution.py:477
  96.4 4.3 %collective-permute-start.13 = (bf16[16,64,256]{2,1,0:T(8,128)(2,1)S(1)}, bf16[16,64,256]{2,1,0:T(8,128)(2,1)S(1)}, u32[]{:S(2)}, u32[]{:S(2)}) collective-permute-start(bf16[16,64,256]{2,1,0:T(8,128)(2,1)S(1)} %get-tuple-element.45), channel_id=1, source_target_pairs={{0,4},{1,5},{4,8},{5,9},{6,2},{7,3},{8,12},{9,13},{10,6},{11,7},{1... | collective-permute-start | bytes 1572872 | tf_op jit(solution)/shard_map/ppermute | solution.py:62
  100.7 1.9 %collective-permute-start.14 = (bf16[16,64,256]{2,1,0:T(8,128)(2,1)S(1)}, bf16[16,64,256]{2,1,0:T(8,128)(2,1)S(1)}, u32[]{:S(2)}, u32[]{:S(2)}) collective-permute-start(bf16[16,64,256]{2,1,0:T(8,128)(2,1)S(1)} %get-tuple-element.46), channel_id=1, source_target_pairs={{2,6},{3,7},{4,0},{5,1},{6,10},{7,11},{8,4},{9,5},{10,14},{11,15},... | collective-permute-start | bytes 1572872 | tf_op jit(solution)/shard_map/ppermute | solution.py:62
  102.7 6.8 %shard_map.61 = (f32[16,128,256]{2,1,0:T(8,128)S(1)}, bf16[64,2,16,256]{3,2,1,0:T(8,128)(2,1)}) custom-call(bf16[384,768]{1,0:T(8,128)(2,1)S(1)} %get-tuple-element.25.weights, bf16[18,2,128,256]{3,2,1,0:T(8,128)(2,1)S(1)} %get-tuple-element.43.field), custom_call_target="tpu_custom_call" | custom-call | tf_op jit(solution)/shard_map/pallas_call | solution.py:477
  109.4 0.0 collective-permute-done.13.first
  109.4 3.3 %collective-permute-done.14.second = bf16[16,64,256]{2,1,0:T(8,128)(2,1)S(1)} collective-permute-done((bf16[16,64,256]{2,1,0:T(8,128)(2,1)S(1)}, bf16[16,64,256]{2,1,0:T(8,128)(2,1)S(1)}, u32[]{:S(2)}, u32[]{:S(2)}) %collective-permute-start.14) | collective-permute-done | bytes 524320 | tf_op jit(solution)/shard_map/ppermute | solution.py:62
  112.7 0.0 copy-done.2
  112.7 2.4 %shard_map.62 = bf16[64,2,16,256]{3,2,1,0:T(8,128)(2,1)} custom-call(f32[16,128,256]{2,1,0:T(8,128)S(1)} %get-tuple-element.44.partial, bf16[16,64,256]{2,1,0:T(8,128)(2,1)S(1)} %collective-permute-done.13.first, bf16[16,64,256]{2,1,0:T(8,128)(2,1)S(1)} %collective-permute-done.14.second, bf16[18,2,128,256]{3,2,1,0:T(8,128)(2,1)S(1)} %get-tuple-element.43.field, ...), custom_call_target="tpu_custom_call" | custom-call | tf_op jit(solution)/shard_map/pallas_call | solution.py:477
  (2 shorter events, 0.0 us)
Async XLA Ops:
  0.6 1.2 %copy-start = (bf16[64,2,16,256]{3,2,1,0:T(8,128)(2,1)S(1)}, bf16[64,2,16,256]{3,2,1,0:T(8,128)(2,1)}, u32[]{:S(2)}) copy-start(bf16[64,2,16,256]{3,2,1,0:T(8,128)(2,1)} %natural.1) | copy-start | bytes 3145732
  3.8 32.9 %collective-permute-start = (bf16[4,2,64,256]{3,2,1,0:T(8,128)(2,1)S(1)}, bf16[4,2,64,256]{3,2,1,0:T(8,128)(2,1)S(1)}, u32[]{:S(2)}, u32[]{:S(2)}) collective-permute-start(bf16[4,2,64,256]{3,2,1,0:T(8,128)(2,1)S(1)} %get-tuple-element.28), channel_id=1, source_target_pairs={{0,31},{1,30},{2,29},{3,28},{4,27},{5,26},{6,25},{7,24},{8,23},{9,... | collective-permute-start | bytes 786440 | tf_op jit(solution)/shard_map/ppermute | solution.py:62
  4.7 40.6 %collective-permute-start.7 = (bf16[6,2,64,256]{3,2,1,0:T(8,128)(2,1)S(1)}, bf16[6,2,64,256]{3,2,1,0:T(8,128)(2,1)S(1)}, u32[]{:S(2)}, u32[]{:S(2)}) collective-permute-start(bf16[6,2,64,256]{3,2,1,0:T(8,128)(2,1)S(1)} %get-tuple-element.34), channel_id=1, source_target_pairs={{0,31},{1,30},{2,29},{3,28},{4,27},{5,26},{6,25},{7,24},{8,23},{9,... | collective-permute-start | bytes 1179656 | tf_op jit(solution)/shard_map/ppermute | solution.py:62
  8.9 57.2 %collective-permute-start.11 = (bf16[16,64,256]{2,1,0:T(8,128)(2,1)S(1)}, bf16[16,64,256]{2,1,0:T(8,128)(2,1)S(1)}, u32[]{:S(2)}, u32[]{:S(2)}) collective-permute-start(bf16[16,64,256]{2,1,0:T(8,128)(2,1)S(1)} %get-tuple-element.41), channel_id=1, source_target_pairs={{0,4},{1,5},{4,8},{5,9},{6,2},{7,3},{8,12},{9,13},{10,6},{11,7},{1... | collective-permute-start | bytes 1572872 | tf_op jit(solution)/shard_map/ppermute | solution.py:62
  12.3 24.4 %collective-permute-start.6 = (bf16[2,2,64,256]{3,2,1,0:T(8,128)(2,1)S(1)}, bf16[2,2,64,256]{3,2,1,0:T(8,128)(2,1)S(1)}, u32[]{:S(2)}, u32[]{:S(2)}) collective-permute-start(bf16[2,2,64,256]{3,2,1,0:T(8,128)(2,1)S(1)} %get-tuple-element.33), channel_id=1, source_target_pairs={{0,1},{1,2},{2,3},{4,5},{5,6},{6,7},{8,9},{9,10},{10,11},{12,13},{... | collective-permute-start | bytes 393224 | tf_op jit(solution)/shard_map/ppermute | solution.py:62
  14.2 27.0 %collective-permute-start.8 = (bf16[2,2,64,256]{3,2,1,0:T(8,128)(2,1)S(1)}, bf16[2,2,64,256]{3,2,1,0:T(8,128)(2,1)S(1)}, u32[]{:S(2)}, u32[]{:S(2)}) collective-permute-start(bf16[2,2,64,256]{3,2,1,0:T(8,128)(2,1)S(1)} %get-tuple-element.35), channel_id=1, source_target_pairs={{1,0},{2,1},{3,2},{5,4},{6,5},{7,6},{9,8},{10,9},{11,10},{13,12},{... | collective-permute-start | bytes 393224 | tf_op jit(solution)/shard_map/ppermute | solution.py:62
  36.7 26.5 %collective-permute-start.2 = (bf16[6,2,64,256]{3,2,1,0:T(8,128)(2,1)S(1)}, bf16[6,2,64,256]{3,2,1,0:T(8,128)(2,1)S(1)}, u32[]{:S(2)}, u32[]{:S(2)}) collective-permute-start(bf16[6,2,64,256]{3,2,1,0:T(8,128)(2,1)S(1)} %get-tuple-element.29), channel_id=1, source_target_pairs={{0,31},{1,30},{2,29},{3,28},{4,27},{5,26},{6,25},{7,24},{8,23},{9,... | collective-permute-start | bytes 1179656 | tf_op jit(solution)/shard_map/ppermute | solution.py:62
  36.8 19.7 %collective-permute-start.1 = (bf16[2,2,64,256]{3,2,1,0:T(8,128)(2,1)S(1)}, bf16[2,2,64,256]{3,2,1,0:T(8,128)(2,1)S(1)}, u32[]{:S(2)}, u32[]{:S(2)}) collective-permute-start(bf16[2,2,64,256]{3,2,1,0:T(8,128)(2,1)S(1)} %get-tuple-element.49), channel_id=1, source_target_pairs={{0,1},{1,2},{2,3},{4,5},{5,6},{6,7},{8,9},{9,10},{10,11},{12,13},{... | collective-permute-start | bytes 393224 | tf_op jit(solution)/shard_map/ppermute | solution.py:62
  41.2 18.0 %collective-permute-start.3 = (bf16[2,2,64,256]{3,2,1,0:T(8,128)(2,1)S(1)}, bf16[2,2,64,256]{3,2,1,0:T(8,128)(2,1)S(1)}, u32[]{:S(2)}, u32[]{:S(2)}) collective-permute-start(bf16[2,2,64,256]{3,2,1,0:T(8,128)(2,1)S(1)} %get-tuple-element.48), channel_id=1, source_target_pairs={{1,0},{2,1},{3,2},{5,4},{6,5},{7,6},{9,8},{10,9},{11,10},{13,12},{... | collective-permute-start | bytes 393224 | tf_op jit(solution)/shard_map/ppermute | solution.py:62
  45.2 30.6 %collective-permute-start.12 = (bf16[16,64,256]{2,1,0:T(8,128)(2,1)S(1)}, bf16[16,64,256]{2,1,0:T(8,128)(2,1)S(1)}, u32[]{:S(2)}, u32[]{:S(2)}) collective-permute-start(bf16[16,64,256]{2,1,0:T(8,128)(2,1)S(1)} %get-tuple-element.42), channel_id=1, source_target_pairs={{2,6},{3,7},{4,0},{5,1},{6,10},{7,11},{8,4},{9,5},{10,14},{11,15},... | collective-permute-start | bytes 1572872 | tf_op jit(solution)/shard_map/ppermute | solution.py:62
  56.5 28.6 %collective-permute-start.10 = (bf16[14,64,256]{2,1,0:T(8,128)(2,1)S(1)}, bf16[14,64,256]{2,1,0:T(8,128)(2,1)S(1)}, u32[]{:S(2)}, u32[]{:S(2)}) collective-permute-start(bf16[14,64,256]{2,1,0:T(8,128)(2,1)S(1)} %get-tuple-element.37), channel_id=1, source_target_pairs={{2,6},{3,7},{4,0},{5,1},{6,10},{7,11},{8,4},{9,5},{10,14},{11,15},... | collective-permute-start | bytes 1376264 | tf_op jit(solution)/shard_map/ppermute | solution.py:62
  59.2 25.9 %collective-permute-start.9 = (bf16[14,64,256]{2,1,0:T(8,128)(2,1)S(1)}, bf16[14,64,256]{2,1,0:T(8,128)(2,1)S(1)}, u32[]{:S(2)}, u32[]{:S(2)}) collective-permute-start(bf16[14,64,256]{2,1,0:T(8,128)(2,1)S(1)} %get-tuple-element.36), channel_id=1, source_target_pairs={{0,4},{1,5},{4,8},{5,9},{6,2},{7,3},{8,12},{9,13},{10,6},{11,7},{1... | collective-permute-start | bytes 1376264 | tf_op jit(solution)/shard_map/ppermute | solution.py:62
  64.2 23.7 %collective-permute-start.4 = (bf16[10,64,256]{2,1,0:T(8,128)(2,1)S(1)}, bf16[10,64,256]{2,1,0:T(8,128)(2,1)S(1)}, u32[]{:S(2)}, u32[]{:S(2)}) collective-permute-start(bf16[10,64,256]{2,1,0:T(8,128)(2,1)S(1)} %get-tuple-element.30), channel_id=1, source_target_pairs={{0,4},{1,5},{4,8},{5,9},{6,2},{7,3},{8,12},{9,13},{10,6},{11,7},{1... | collective-permute-start | bytes 983048 | tf_op jit(solution)/shard_map/ppermute | solution.py:62
  66.1 21.8 %collective-permute-start.5 = (bf16[10,64,256]{2,1,0:T(8,128)(2,1)S(1)}, bf16[10,64,256]{2,1,0:T(8,128)(2,1)S(1)}, u32[]{:S(2)}, u32[]{:S(2)}) collective-permute-start(bf16[10,64,256]{2,1,0:T(8,128)(2,1)S(1)} %get-tuple-element.31), channel_id=1, source_target_pairs={{2,6},{3,7},{4,0},{5,1},{6,10},{7,11},{8,4},{9,5},{10,14},{11,15},... | collective-permute-start | bytes 983048 | tf_op jit(solution)/shard_map/ppermute | solution.py:62
  68.5 1.0 copy-start.1
  87.9 24.8 %copy-start.2 = (s32[16,256]{1,0:T(8,128)S(1)}, s32[16,256]{1,0:T(8,128)}, u32[]{:S(2)}) copy-start(s32[16,256]{1,0:T(8,128)} %mask.1) | copy-start | bytes 49156
  96.4 13.1 %collective-permute-start.13 = (bf16[16,64,256]{2,1,0:T(8,128)(2,1)S(1)}, bf16[16,64,256]{2,1,0:T(8,128)(2,1)S(1)}, u32[]{:S(2)}, u32[]{:S(2)}) collective-permute-start(bf16[16,64,256]{2,1,0:T(8,128)(2,1)S(1)} %get-tuple-element.45), channel_id=1, source_target_pairs={{0,4},{1,5},{4,8},{5,9},{6,2},{7,3},{8,12},{9,13},{10,6},{11,7},{1... | collective-permute-start | bytes 1572872 | tf_op jit(solution)/shard_map/ppermute | solution.py:62
  100.7 12.0 %collective-permute-start.14 = (bf16[16,64,256]{2,1,0:T(8,128)(2,1)S(1)}, bf16[16,64,256]{2,1,0:T(8,128)(2,1)S(1)}, u32[]{:S(2)}, u32[]{:S(2)}) collective-permute-start(bf16[16,64,256]{2,1,0:T(8,128)(2,1)S(1)} %get-tuple-element.46), channel_id=1, source_target_pairs={{2,6},{3,7},{4,0},{5,1},{6,10},{7,11},{8,4},{9,5},{10,14},{11,15},... | collective-permute-start | bytes 1572872 | tf_op jit(solution)/shard_map/ppermute | solution.py:62

commit v4 on v3

--- a/solution.py
+++ b/solution.py
@@ -10,8 +10,9 @@
 
 step_size = 0.5
 LANES = 128
+IN_VMEM = pl.BlockSpec(memory_space=pltpu.VMEM)
 OUTER = 4
-MIDDLE = 6
+MIDDLE = 8
 VMEM_LIMIT = 40 << 20
 AXES = ("kx", "ky")
 f32 = jnp.float32
@@ -253,7 +254,7 @@
         joined[start : start + count] = segments[index][offset : offset + count]
         start += count
     signs = sign_rows(chans, chans)
-    emit_sides(lambda y, x: joined[y, x], rows, 2, chans, depth, layers, signs, right, left)
+    emit_sides(lambda y, x: joined[y, x], rows, 2 if rows % 4 else 4, chans, depth, layers, signs, right, left)
 
 
 def add_part(total, part, place, columns):
@@ -299,11 +300,21 @@
 
 
 def add_sides(weights, first, second, offset, count, place, total, columns, static):
-    for slot, ref in ((0, first), (1, second)):
-        add_rows(
-            weights.at[slot], lambda y, ref=ref: ref[y + offset], count, place, total,
-            columns[slot], static,
-        )
+    def one(y, place):
+        for slot, ref in ((0, first), (1, second)):
+            part = dot(weights[slot], shifted(flat(ref[y + offset])))
+            add_part(total, part, place, columns[slot])
+
+    if static:
+        for y in range(count):
+            one(y, place + y)
+    else:
+
+        def body(y, carry):
+            one(y, place + y)
+            return carry
+
+        lax.fori_loop(0, count, body, 0, unroll=4)
 
 
 def early_kernel(weights, own, total):
@@ -314,63 +325,68 @@
 def given_kernel(sides, first, second, partial, total):
     rows = total.shape[0] - 2
     layers = 3 * total.shape[1] // sides.shape[1]
-    total[...] = partial[...]
     add_sides(sides, first, second, 0, rows, 2, total, side_columns(total, layers), False)
 
 
-def outer_kernel(early, late, top, bottom, outer, middle, partial, total):
-    rows = total.shape[0] - 2
-    edge, half = outer.shape[0] // 2, middle.shape[0] // 2
-    total[...] = partial[...]
-    add_own(early, ((top, 2, 0, 0, True), (bottom, 2, 0, rows + 2, True)), total)
+def outer_kernel(early, late, top, bottom, outer, partial, total):
+    end, edge = total.shape[0], outer.shape[0] // 2
+    add_own(early, ((top, 2, 0, 0, True), (bottom, 2, 0, end, True)), total)
     add_own(
         late,
         (
             (outer, edge, 0, 2, True),
-            (middle, half, 0, 2 + edge, True),
-            (middle, half, half, rows + 2 - edge - half, True),
-            (outer, edge, edge, rows + 2 - edge, True),
+            (outer, edge, edge, end - edge, True),
         ),
         total,
     )
 
 
-def middle_kernel(early_sides, late_sides, first, second, partial, total):
-    rows = total.shape[0] - 2
-    half = (first.shape[0] - 4) // 2
-    columns = side_columns(total, 3 * total.shape[1] // early_sides.shape[1])
-    total[...] = partial[...]
-    for offset, place in ((0, 0), (2 + 2 * half, rows + 2)):
-        add_sides(early_sides, first, second, offset, 2, place, total, columns, True)
-    for offset, place in ((2, 2), (2 + half, rows + 2 - half)):
-        add_sides(late_sides, first, second, offset, half, place, total, columns, True)
-
-
-def inner_kernel(weights, top, inner, bottom, partial, total):
-    rows = total.shape[0] - 2
-    count = inner.shape[0]
-    total[...] = partial[...]
+def outer_rows(rows):
+    return max(2, rows * OUTER // 32)
+
+
+def own_kernel(late, virtual_top, middle, virtual_bottom, partial, total):
+    end, half = total.shape[0], middle.shape[0] // 2
+    edge = outer_rows(end - 2)
     add_own(
-        weights,
+        late,
         (
-            (top, 2, 0, 0, True),
-            (inner, count, 0, 2 + (rows - count) // 2, True),
-            (bottom, 2, 0, rows + 2, True),
+            (virtual_top, 2, 0, 0, True),
+            (middle, half, 0, 2 + edge, True),
+            (middle, half, half, end - edge - half, True),
+            (virtual_bottom, 2, 0, end, True),
         ),
         total,
     )
+
+
+def inner_kernel(
+    late, early_sides, late_sides, inner,
+    first_outer, second_outer, first_middle, second_middle, partial, total,
+):
+    end, edge, half = total.shape[0], first_outer.shape[0] // 2 - 2, first_middle.shape[0] // 2
+    add_own(late, ((inner, inner.shape[0], 0, 2 + edge + half, True),), total)
+    columns = side_columns(total, 3 * total.shape[1] // early_sides.shape[1])
+    for weights, first, second, offset, size, place in (
+        (early_sides, first_outer, second_outer, 0, 2, 0),
+        (late_sides, first_outer, second_outer, 2, edge, 2),
+        (late_sides, first_outer, second_outer, 2 + edge, edge, end - edge),
+        (early_sides, first_outer, second_outer, 2 + 2 * edge, 2, end),
+        (late_sides, first_middle, second_middle, 0, half, 2 + edge),
+        (late_sides, first_middle, second_middle, half, half, end - edge - half),
+    ):
+        add_sides(weights, first, second, offset, size, place, total, columns, True)
 
 
 def residual_kernel(
     sides, outward, first, second, partial,
     top, given, bottom, virtual_top, virtual_outer, virtual_middle, virtual_bottom, virtual_inner,
-    field, right, left, total, reach,
+    total, field, right, left, reach,
 ):
     rows, layers, chans, depth = given.shape
     span = rows + 2
     edge, half = virtual_outer.shape[0] // 2, virtual_middle.shape[0] // 2
     inner = rows - 2 * edge - 2 * half
-    total[...] = partial[...]
     columns = side_columns(total, layers)
     for offset, count, place in ((0, 2, 0), (2, inner, 2 + edge + half), (2 + inner, 2, rows + 2)):
         add_sides(sides, first, second, offset, count, place, total, columns, True)
@@ -402,17 +418,23 @@
 
     direct, _, _ = place_flags()
     reach[...] = jnp.zeros(reach.shape, f32)
-    for slot, upper in ((0, direct), (1, jnp.logical_not(direct))):
-        target, weights = reach.at[slot], outward.at[slot]
-
-        def read(y, upper=upper):
-            return jnp.where(upper, field[y, layers - 1], field[y, 0])
-
-        add_rows(weights, read, 1, 0, target, slice(None), True)
-        add_rows(weights, lambda y, read=read: read(y + 1), 1, 1, target, slice(None), True)
-        add_rows(weights, lambda y, read=read: read(y + 2), rows - 2, 2, target, slice(None), False)
-        add_rows(weights, lambda y, read=read: read(y + rows), 1, rows, target, slice(None), True)
-        add_rows(weights, lambda y, read=read: read(y + rows + 1), 1, rows + 1, target, slice(None), True)
+
+    def add_reach(y, place):
+        upper, lower = field[y, layers - 1], field[y, 0]
+        for slot, row in (
+            (0, jnp.where(direct, upper, lower)), (1, jnp.where(direct, lower, upper))
+        ):
+            add_part(reach.at[slot], dot(outward[slot], shifted(row)), place, slice(None))
+
+    def body(y, carry):
+        add_reach(y, y)
+        return carry
+
+    for y in (0, 1):
+        add_reach(y, y)
+    lax.fori_loop(2, rows, body, 0, unroll=7 if (rows - 2) % 7 == 0 else 2)
+    for y in (rows, rows + 1):
+        add_reach(y, y)
     ones = jnp.ones((chans, 1), f32)
 
     upper_reach = lambda y: jnp.where(direct, reach[0, y], reach[1, y])
@@ -473,10 +495,13 @@
     from_rows(value, natural, spread)
 
 
-def call(kernel, shape, scratch, *args):
+def call(kernel, shape, scratch, *args, reuse=None):
     return pl.pallas_call(
         kernel,
         out_shape=shape,
+        in_specs=[IN_VMEM] * len(args),
+        out_specs=jax.tree.map(lambda _: IN_VMEM, shape),
+        input_output_aliases={} if reuse is None else {reuse: 0},
         scratch_shapes=scratch,
         compiler_params=pltpu.CompilerParams(vmem_limit_bytes=VMEM_LIMIT),
     )(*args)
@@ -499,7 +524,7 @@
 def step(kspace, kernel, mask):
     chans, layers, rows, depth = kspace.shape
     wide = layers * 2 * chans
-    edge = max(2, rows * OUTER // 32)
+    edge = outer_rows(rows)
     half = max(1, rows * MIDDLE // 32)
     count = rows - 2 * edge - 2 * half
     block = lambda size: like(size, layers, chans, depth)
@@ -516,7 +541,6 @@
     given_sides = around_x(((0, 0, rows),), given)
     middle = send(middle, to_mirror)
     top, bottom = send(tail, to_next), send(head, to_previous)
-    inner = send(inner, to_mirror)
 
     early, early_sides, late, late_sides, adjoint, outward = call(
         weights_kernel,
@@ -532,28 +556,34 @@
         kernel,
     )
     partial = call(early_kernel, total, [], early, given)
-    partial = call(given_kernel, total, [], early_sides, *given_sides, partial)
-
     virtual_top = send(outer[-2:], to_next)
     virtual_bottom = send(outer[:2], to_previous)
-    layout = (
-        (0, 0, 2), (1, 0, edge), (2, 0, half), (2, half, half), (1, edge, edge), (3, 0, 2)
-    )
-    first, second = around_x(layout, top, outer, middle, bottom)
-    partial = call(outer_kernel, total, [], early, late, top, bottom, outer, middle, partial)
-    middle_sides = first, second
-
+    inner = send(inner, to_mirror)
+    layout = ((0, 0, 2), (1, 0, edge), (1, edge, edge), (2, 0, 2))
+    outer_sides = around_x(layout, top, outer, bottom)
+    partial = call(given_kernel, total, [], early_sides, *given_sides, partial, reuse=3)
+    partial = call(
+        outer_kernel, total, [],
+        early, late, top, bottom, outer, partial, reuse=5,
+    )
+
+    middle_sides = around_x(((0, 0, 2 * half),), middle)
+    partial = call(
+        own_kernel, total, [], late, virtual_top, middle, virtual_bottom, partial, reuse=4
+    )
     layout = ((0, 0, 2), (1, 0, count), (2, 0, 2))
     first, second = around_x(layout, virtual_top, inner, virtual_bottom)
-    partial = call(inner_kernel, total, [], late, virtual_top, inner, virtual_bottom, partial)
-    partial = call(middle_kernel, total, [], early_sides, late_sides, *middle_sides, partial)
+    partial = call(
+        inner_kernel, total, [],
+        late, early_sides, late_sides, inner, *outer_sides, *middle_sides, partial, reuse=8,
+    )
     side = like(rows, chans, depth)
-    field, right, left = call(
+    _, field, right, left = call(
         residual_kernel,
-        (like(rows + 2, layers, 2 * chans, depth), side, side),
-        [pltpu.VMEM(total.shape, f32), pltpu.VMEM((2, rows, chans, depth), f32)],
+        (total, like(rows + 2, layers, 2 * chans, depth), side, side),
+        [pltpu.VMEM((2, rows, chans, depth), f32)],
         late_sides, outward, first, second, partial,
-        top, given, bottom, virtual_top, outer, middle, virtual_bottom, inner,
+        top, given, bottom, virtual_top, outer, middle, virtual_bottom, inner, reuse=4,
     )
     first, second = send(right, to_right), send(left, to_left)
     natural = like(chans, layers, rows, depth)

time: 116 us -> 127 us (1.095)
  the two profiles are of different devices: /device:TPU:18 before, /device:TPU:16 now
where the time goes in v4:
time: 127 us
  starting transfers between devices  46.3 us (36%)
  waiting for transfers between devices  39.5 us (31%)
  Pallas kernels  37.6 us (30%)
  local copies, waits for them, and re-layouts  2.25 us (2%)
    ppermute x17, starting transfers between devices, send(): return lax.ppermute(value, AXES, pairs)  46.3 us
    ppermute x17, waiting for transfers between devices, send(): return lax.ppermute(value, AXES, pairs)  39.5 us
    pallas_call x14, Pallas kernels, call(): pl.pallas_call(kernel, out_shape=shape, in_specs=[IN_VMEM] * len(args), o...  37.6 us
  transfers between devices with their start and end apart: 17, of which 5 were waited for; matrix products, arithmetic and copies ran while one was open for 0% of the time, Pallas kernels for 21%

profile of v4, /device:TPU:16, one launch (start us, length us, event | category | flops | bytes accessed | tf_op | source)
XLA Modules:
  0.0 126.6 jit_solution(134365440587191524)
XLA Ops:
  0.6 1.2 copy-done
  1.9 1.9 %shard_map.51 = (bf16[16,2,64,256]{3,2,1,0:T(8,128)(2,1)S(1)}, bf16[2,2,64,256]{3,2,1,0:T(8,128)(2,1)S(1)}, bf16[2,2,64,256]{3,2,1,0:T(8,128)(2,1)S(1)}, bf16[4,...) custom-call(bf16[64,2,16,256]{3,2,1,0:T(8,128)(2,1)S(1)} %copy-done), custom_call_target="tpu_custom_call" | custom-call | tf_op jit(solution)/shard_map/pallas_call | solution.py:499
  3.8 1.8 %collective-permute-start = (bf16[4,2,64,256]{3,2,1,0:T(8,128)(2,1)S(1)}, bf16[4,2,64,256]{3,2,1,0:T(8,128)(2,1)S(1)}, u32[]{:S(2)}, u32[]{:S(2)}) collective-permute-start(bf16[4,2,64,256]{3,2,1,0:T(8,128)(2,1)S(1)} %get-tuple-element.30), channel_id=1, source_target_pairs={{0,31},{1,30},{2,29},{3,28},{4,27},{5,26},{6,25},{7,24},{8,23},{9,... | collective-permute-start | bytes 786440 | tf_op jit(solution)/shard_map/ppermute | solution.py:63
  5.6 2.4 %collective-permute-start.6 = (bf16[2,2,64,256]{3,2,1,0:T(8,128)(2,1)S(1)}, bf16[2,2,64,256]{3,2,1,0:T(8,128)(2,1)S(1)}, u32[]{:S(2)}, u32[]{:S(2)}) collective-permute-start(bf16[2,2,64,256]{3,2,1,0:T(8,128)(2,1)S(1)} %get-tuple-element.36), channel_id=1, source_target_pairs={{0,1},{1,2},{2,3},{4,5},{5,6},{6,7},{8,9},{9,10},{10,11},{12,13},{... | collective-permute-start | bytes 393224 | tf_op jit(solution)/shard_map/ppermute | solution.py:63
  8.1 0.7 collective-permute-start.10
  8.8 0.9 shard_map.55
  9.7 5.2 %collective-permute-start.13 = (bf16[16,64,256]{2,1,0:T(8,128)(2,1)S(1)}, bf16[16,64,256]{2,1,0:T(8,128)(2,1)S(1)}, u32[]{:S(2)}, u32[]{:S(2)}) collective-permute-start(bf16[16,64,256]{2,1,0:T(8,128)(2,1)S(1)} %get-tuple-element.45), channel_id=1, source_target_pairs={{0,4},{1,5},{4,8},{5,9},{6,2},{7,3},{8,12},{9,13},{10,6},{11,7},{1... | collective-permute-start | bytes 1572872 | tf_op jit(solution)/shard_map/ppermute | solution.py:63
  14.9 1.9 %collective-permute-start.14 = (bf16[16,64,256]{2,1,0:T(8,128)(2,1)S(1)}, bf16[16,64,256]{2,1,0:T(8,128)(2,1)S(1)}, u32[]{:S(2)}, u32[]{:S(2)}) collective-permute-start(bf16[16,64,256]{2,1,0:T(8,128)(2,1)S(1)} %get-tuple-element.46), channel_id=1, source_target_pairs={{2,6},{3,7},{4,0},{5,1},{6,10},{7,11},{8,4},{9,5},{10,14},{11,15},... | collective-permute-start | bytes 1572872 | tf_op jit(solution)/shard_map/ppermute | solution.py:63
  16.9 0.0 collective-permute-done.6.refs_0_.top
  16.9 2.0 %collective-permute-start.2 = (bf16[4,2,64,256]{3,2,1,0:T(8,128)(2,1)S(1)}, bf16[4,2,64,256]{3,2,1,0:T(8,128)(2,1)S(1)}, u32[]{:S(2)}, u32[]{:S(2)}) collective-permute-start(bf16[4,2,64,256]{3,2,1,0:T(8,128)(2,1)S(1)} %get-tuple-element.31), channel_id=1, source_target_pairs={{0,31},{1,30},{2,29},{3,28},{4,27},{5,26},{6,25},{7,24},{8,23},{9,... | collective-permute-start | bytes 786440 | tf_op jit(solution)/shard_map/ppermute | solution.py:63
  18.9 12.2 %collective-permute-done.refs_1_.outer.virtual_outer = bf16[4,2,64,256]{3,2,1,0:T(8,128)(2,1)S(1)} collective-permute-done((bf16[4,2,64,256]{3,2,1,0:T(8,128)(2,1)S(1)}, bf16[4,2,64,256]{3,2,1,0:T(8,128)(2,1)S(1)}, u32[]{:S(2)}, u32[]{:S(2)}) %collective-permute-start) | collective-permute-done | bytes 262176 | tf_op jit(solution)/shard_map/ppermute | solution.py:63
  31.1 1.3 %collective-permute-start.7 = (bf16[2,2,64,256]{3,2,1,0:T(8,128)(2,1)S(1)}, bf16[2,2,64,256]{3,2,1,0:T(8,128)(2,1)S(1)}, u32[]{:S(2)}, u32[]{:S(2)}) collective-permute-start(bf16[2,2,64,256]{3,2,1,0:T(8,128)(2,1)S(1)} %get-tuple-element.37), channel_id=1, source_target_pairs={{1,0},{2,1},{3,2},{5,4},{6,5},{7,6},{9,8},{10,9},{11,10},{13,12},{... | collective-permute-start | bytes 393224 | tf_op jit(solution)/shard_map/ppermute | solution.py:63
  32.4 7.4 %collective-permute-done.7.refs_2_.bottom = bf16[2,2,64,256]{3,2,1,0:T(8,128)(2,1)S(1)} collective-permute-done((bf16[2,2,64,256]{3,2,1,0:T(8,128)(2,1)S(1)}, bf16[2,2,64,256]{3,2,1,0:T(8,128)(2,1)S(1)}, u32[]{:S(2)}, u32[]{:S(2)}) %collective-permute-start.7) | collective-permute-done | bytes 131104 | tf_op jit(solution)/shard_map/ppermute | solution.py:63
  39.8 3.0 %collective-permute-start.1 = (bf16[2,2,64,256]{3,2,1,0:T(8,128)(2,1)S(1)}, bf16[2,2,64,256]{3,2,1,0:T(8,128)(2,1)S(1)}, u32[]{:S(2)}, u32[]{:S(2)}) collective-permute-start(bf16[2,2,64,256]{3,2,1,0:T(8,128)(2,1)S(1)} %get-tuple-element.53), channel_id=1, source_target_pairs={{0,1},{1,2},{2,3},{4,5},{5,6},{6,7},{8,9},{9,10},{10,11},{12,13},{... | collective-permute-start | bytes 393224 | tf_op jit(solution)/shard_map/ppermute | solution.py:63
  42.8 0.5 shard_map.53
  43.3 10.3 %collective-permute-done.2.refs_1_.inner.virtual_inner = bf16[4,2,64,256]{3,2,1,0:T(8,128)(2,1)S(1)} collective-permute-done((bf16[4,2,64,256]{3,2,1,0:T(8,128)(2,1)S(1)}, bf16[4,2,64,256]{3,2,1,0:T(8,128)(2,1)S(1)}, u32[]{:S(2)}, u32[]{:S(2)}) %collective-permute-start.2) | collective-permute-done | bytes 262176 | tf_op jit(solution)/shard_map/ppermute | solution.py:63
  53.6 4.4 %collective-permute-start.8 = (bf16[8,64,256]{2,1,0:T(8,128)(2,1)S(1)}, bf16[8,64,256]{2,1,0:T(8,128)(2,1)S(1)}, u32[]{:S(2)}, u32[]{:S(2)}) collective-permute-start(bf16[8,64,256]{2,1,0:T(8,128)(2,1)S(1)} %get-tuple-element.38), channel_id=1, source_target_pairs={{0,4},{1,5},{4,8},{5,9},{6,2},{7,3},{8,12},{9,13},{10,6},{11,7},{1... | collective-permute-start | bytes 786440 | tf_op jit(solution)/shard_map/ppermute | solution.py:63
  58.0 0.0 collective-permute-done.1.refs_0_.virtual_top
  58.0 1.3 %collective-permute-start.3 = (bf16[2,2,64,256]{3,2,1,0:T(8,128)(2,1)S(1)}, bf16[2,2,64,256]{3,2,1,0:T(8,128)(2,1)S(1)}, u32[]{:S(2)}, u32[]{:S(2)}) collective-permute-start(bf16[2,2,64,256]{3,2,1,0:T(8,128)(2,1)S(1)} %get-tuple-element.52), channel_id=1, source_target_pairs={{1,0},{2,1},{3,2},{5,4},{6,5},{7,6},{9,8},{10,9},{11,10},{13,12},{... | collective-permute-start | bytes 393224 | tf_op jit(solution)/shard_map/ppermute | solution.py:63
  59.3 6.4 %collective-permute-done.3.refs_2_.virtual_bottom = bf16[2,2,64,256]{3,2,1,0:T(8,128)(2,1)S(1)} collective-permute-done((bf16[2,2,64,256]{3,2,1,0:T(8,128)(2,1)S(1)}, bf16[2,2,64,256]{3,2,1,0:T(8,128)(2,1)S(1)}, u32[]{:S(2)}, u32[]{:S(2)}) %collective-permute-start.3) | collective-permute-done | bytes 131104 | tf_op jit(solution)/shard_map/ppermute | solution.py:63
  65.7 1.9 %collective-permute-start.9 = (bf16[8,64,256]{2,1,0:T(8,128)(2,1)S(1)}, bf16[8,64,256]{2,1,0:T(8,128)(2,1)S(1)}, u32[]{:S(2)}, u32[]{:S(2)}) collective-permute-start(bf16[8,64,256]{2,1,0:T(8,128)(2,1)S(1)} %get-tuple-element.39), channel_id=1, source_target_pairs={{2,6},{3,7},{4,0},{5,1},{6,10},{7,11},{8,4},{9,5},{10,14},{11,15},... | collective-permute-start | bytes 786440 | tf_op jit(solution)/shard_map/ppermute | solution.py:63
  67.6 0.5 shard_map.52
  68.1 0.0 collective-permute-done.10.refs_0_.middle.virtual_middle
  68.1 0.5 shard_map.54
  68.6 4.8 %collective-permute-start.11 = (bf16[8,64,256]{2,1,0:T(8,128)(2,1)S(1)}, bf16[8,64,256]{2,1,0:T(8,128)(2,1)S(1)}, u32[]{:S(2)}, u32[]{:S(2)}) collective-permute-start(bf16[8,64,256]{2,1,0:T(8,128)(2,1)S(1)} %get-tuple-element.41), channel_id=1, source_target_pairs={{0,4},{1,5},{4,8},{5,9},{6,2},{7,3},{8,12},{9,13},{10,6},{11,7},{1... | collective-permute-start | bytes 786440 | tf_op jit(solution)/shard_map/ppermute | solution.py:63
  73.4 0.0 collective-permute-done.13.first
  73.4 1.9 %collective-permute-start.12 = (bf16[8,64,256]{2,1,0:T(8,128)(2,1)S(1)}, bf16[8,64,256]{2,1,0:T(8,128)(2,1)S(1)}, u32[]{:S(2)}, u32[]{:S(2)}) collective-permute-start(bf16[8,64,256]{2,1,0:T(8,128)(2,1)S(1)} %get-tuple-element.42), channel_id=1, source_target_pairs={{2,6},{3,7},{4,0},{5,1},{6,10},{7,11},{8,4},{9,5},{10,14},{11,15},... | collective-permute-start | bytes 786440 | tf_op jit(solution)/shard_map/ppermute | solution.py:63
  75.4 4.8 %collective-permute-start.4 = (bf16[8,64,256]{2,1,0:T(8,128)(2,1)S(1)}, bf16[8,64,256]{2,1,0:T(8,128)(2,1)S(1)}, u32[]{:S(2)}, u32[]{:S(2)}) collective-permute-start(bf16[8,64,256]{2,1,0:T(8,128)(2,1)S(1)} %get-tuple-element.32), channel_id=1, source_target_pairs={{0,4},{1,5},{4,8},{5,9},{6,2},{7,3},{8,12},{9,13},{10,6},{11,7},{1... | collective-permute-start | bytes 786440 | tf_op jit(solution)/shard_map/ppermute | solution.py:63
  80.2 0.0 collective-permute-done.8.first_outer
  80.2 1.9 %collective-permute-start.5 = (bf16[8,64,256]{2,1,0:T(8,128)(2,1)S(1)}, bf16[8,64,256]{2,1,0:T(8,128)(2,1)S(1)}, u32[]{:S(2)}, u32[]{:S(2)}) collective-permute-start(bf16[8,64,256]{2,1,0:T(8,128)(2,1)S(1)} %get-tuple-element.33), channel_id=1, source_target_pairs={{2,6},{3,7},{4,0},{5,1},{6,10},{7,11},{8,4},{9,5},{10,14},{11,15},... | collective-permute-start | bytes 786440 | tf_op jit(solution)/shard_map/ppermute | solution.py:63
  82.1 0.0 copy-start.1
  82.1 1.0 copy-done.1
  83.1 1.6 %shard_map.50 = (bf16[768,384]{1,0:T(8,128)(2,1)S(1)}, bf16[2,384,192]{2,1,0:T(8,128)(2,1)S(1)}, bf16[768,384]{1,0:T(8,128)(2,1)S(1)}, bf16[2,384,192]{2,1,0:T(8...) custom-call(bf16[3,3,3,64,128]{4,3,2,1,0:T(8,128)(2,1)S(1)} %copy-done.1), custom_call_target="tpu_custom_call" | custom-call | tf_op jit(solution)/shard_map/pallas_call | solution.py:499
  84.7 4.7 %shard_map.56.partial = f32[18,256,256]{2,1,0:T(8,128)S(1)} custom-call(bf16[768,384]{1,0:T(8,128)(2,1)S(1)} %get-tuple-element.43.weights.early, bf16[16,2,64,256]{3,2,1,0:T(8,128)(2,1)S(1)} %get-tuple-element.44.refs_0_.own.given), custom_call_target="tpu_custom_call" | custom-call | tf_op jit(solution)/shard_map/pallas_call | solution.py:499
  89.4 2.9 %shard_map.57.partial = f32[18,256,256]{2,1,0:T(8,128)S(1)} custom-call(bf16[2,384,192]{2,1,0:T(8,128)(2,1)S(1)} %get-tuple-element.35.sides.early_sides, bf16[16,64,256]{2,1,0:T(8,128)(2,1)S(1)} %collective-permute-done.13.first, bf16[16,64,256]{2,1,0:T(8,128)(2,1)S(1)} %collective-permute-done.14.second, ...), custom_call_target="tpu_custom_call", output_to_operand_aliasing={{}: (3, {})} | custom-call | tf_op jit(solution)/shard_map/pallas_call | solution.py:499
  92.3 1.9 %shard_map.58.partial = f32[18,256,256]{2,1,0:T(8,128)S(1)} custom-call(bf16[768,384]{1,0:T(8,128)(2,1)S(1)} %get-tuple-element.43.weights.early, bf16[768,384]{1,0:T(8,128)(2,1)S(1)} %get-tuple-element.34.late, bf16[2,2,64,256]{3,2,1,0:T(8,128)(2,1)S(1)} %collective-permute-done.6.refs_0_.top, ...), custom_call_target="tpu_custom_call", output_to_operand_aliasing={{}: (5, {})} | custom-call | tf_op jit(solution)/shard_map/pallas_call | solution.py:499
  94.2 2.7 %shard_map.59.partial = f32[18,256,256]{2,1,0:T(8,128)S(1)} custom-call(bf16[768,384]{1,0:T(8,128)(2,1)S(1)} %get-tuple-element.34.late, bf16[2,2,64,256]{3,2,1,0:T(8,128)(2,1)S(1)} %collective-permute-done.1.refs_0_.virtual_top, bf16[8,2,64,256]{3,2,1,0:T(8,128)(2,1)S(1)} %collective-permute-done.10.refs_0_.middle.virtual_middle, ...), custom_call_target="tpu_custom_call", output_to_operand_aliasing={{}: (4, {})} | custom-call | tf_op jit(solution)/shard_map/pallas_call | solution.py:499
  96.9 0.0 collective-permute-done.9.second_outer
  96.9 3.6 %shard_map.60.partial = f32[18,256,256]{2,1,0:T(8,128)S(1)} custom-call(bf16[768,384]{1,0:T(8,128)(2,1)S(1)} %get-tuple-element.34.late, bf16[2,384,192]{2,1,0:T(8,128)(2,1)S(1)} %get-tuple-element.35.sides.early_sides, bf16[2,384,192]{2,1,0:T(8,128)(2,1)S(1)} %get-tuple-element.28.late_sides.sides, ...), custom_call_target="tpu_custom_call", output_to_operand_aliasing={{}: (8, {})} | custom-call | tf_op jit(solution)/shard_map/pallas_call | solution.py:499
  100.6 0.0 collective-permute-done.4.first
  100.6 0.0 copy-start.2
  100.6 6.8 %shard_map.61 = (f32[18,256,256]{2,1,0:T(8,128)S(1)}, bf16[18,2,128,256]{3,2,1,0:T(8,128)(2,1)S(1)}, bf16[16,64,256]{2,1,0:T(8,128)(2,1)S(1)}, bf16[16,64,256]{2,1,0:T(8,128)(2,1)S(1)}) custom-call(bf16[2,384,192]{2,1,0:T(8,128)(2,1)S(1)} %get-tuple-element.28.late_sides.sides, ...), custom_call_target="tpu_custom_call", output_to_operand_aliasing={{0}: (4, {})} | custom-call | tf_op jit(solution)/shard_map/pallas_call | solution.py:499
  107.4 4.8 %collective-permute-start.15 = (bf16[16,64,256]{2,1,0:T(8,128)(2,1)S(1)}, bf16[16,64,256]{2,1,0:T(8,128)(2,1)S(1)}, u32[]{:S(2)}, u32[]{:S(2)}) collective-permute-start(bf16[16,64,256]{2,1,0:T(8,128)(2,1)S(1)} %get-tuple-element.49), channel_id=1, source_target_pairs={{0,4},{1,5},{4,8},{5,9},{6,2},{7,3},{8,12},{9,13},{10,6},{11,7},{1... | collective-permute-start | bytes 1572872 | tf_op jit(solution)/shard_map/ppermute | solution.py:63
  112.2 1.9 %collective-permute-start.16 = (bf16[16,64,256]{2,1,0:T(8,128)(2,1)S(1)}, bf16[16,64,256]{2,1,0:T(8,128)(2,1)S(1)}, u32[]{:S(2)}, u32[]{:S(2)}) collective-permute-start(bf16[16,64,256]{2,1,0:T(8,128)(2,1)S(1)} %get-tuple-element.50), channel_id=1, source_target_pairs={{2,6},{3,7},{4,0},{5,1},{6,10},{7,11},{8,4},{9,5},{10,14},{11,15},... | collective-permute-start | bytes 1572872 | tf_op jit(solution)/shard_map/ppermute | solution.py:63
  114.2 6.8 %shard_map.62 = (f32[16,128,256]{2,1,0:T(8,128)S(1)}, bf16[64,2,16,256]{3,2,1,0:T(8,128)(2,1)}) custom-call(bf16[384,768]{1,0:T(8,128)(2,1)S(1)} %get-tuple-element.27.weights, bf16[18,2,128,256]{3,2,1,0:T(8,128)(2,1)S(1)} %get-tuple-element.47.field), custom_call_target="tpu_custom_call" | custom-call | tf_op jit(solution)/shard_map/pallas_call | solution.py:499
  120.9 0.0 collective-permute-done.15.first
  120.9 3.3 %collective-permute-done.16.second = bf16[16,64,256]{2,1,0:T(8,128)(2,1)S(1)} collective-permute-done((bf16[16,64,256]{2,1,0:T(8,128)(2,1)S(1)}, bf16[16,64,256]{2,1,0:T(8,128)(2,1)S(1)}, u32[]{:S(2)}, u32[]{:S(2)}) %collective-permute-start.16) | collective-permute-done | bytes 524320 | tf_op jit(solution)/shard_map/ppermute | solution.py:63
  124.2 2.4 %shard_map.63 = bf16[64,2,16,256]{3,2,1,0:T(8,128)(2,1)} custom-call(f32[16,128,256]{2,1,0:T(8,128)S(1)} %get-tuple-element.48.partial, bf16[16,64,256]{2,1,0:T(8,128)(2,1)S(1)} %collective-permute-done.15.first, bf16[16,64,256]{2,1,0:T(8,128)(2,1)S(1)} %collective-permute-done.16.second, bf16[18,2,128,256]{3,2,1,0:T(8,128)(2,1)S(1)} %get-tuple-element.47.field, ...), custom_call_target="tpu_custom_call" | custom-call | tf_op jit(solution)/shard_map/pallas_call | solution.py:499
  (7 shorter events, 0.0 us)
Async XLA Ops:
  0.6 1.2 copy-start
  3.8 27.3 %collective-permute-start = (bf16[4,2,64,256]{3,2,1,0:T(8,128)(2,1)S(1)}, bf16[4,2,64,256]{3,2,1,0:T(8,128)(2,1)S(1)}, u32[]{:S(2)}, u32[]{:S(2)}) collective-permute-start(bf16[4,2,64,256]{3,2,1,0:T(8,128)(2,1)S(1)} %get-tuple-element.30), channel_id=1, source_target_pairs={{0,31},{1,30},{2,29},{3,28},{4,27},{5,26},{6,25},{7,24},{8,23},{9,... | collective-permute-start | bytes 786440 | tf_op jit(solution)/shard_map/ppermute | solution.py:63
  5.6 11.2 %collective-permute-start.6 = (bf16[2,2,64,256]{3,2,1,0:T(8,128)(2,1)S(1)}, bf16[2,2,64,256]{3,2,1,0:T(8,128)(2,1)S(1)}, u32[]{:S(2)}, u32[]{:S(2)}) collective-permute-start(bf16[2,2,64,256]{3,2,1,0:T(8,128)(2,1)S(1)} %get-tuple-element.36), channel_id=1, source_target_pairs={{0,1},{1,2},{2,3},{4,5},{5,6},{6,7},{8,9},{9,10},{10,11},{12,13},{... | collective-permute-start | bytes 393224 | tf_op jit(solution)/shard_map/ppermute | solution.py:63
  8.1 60.0 %collective-permute-start.10 = (bf16[8,2,64,256]{3,2,1,0:T(8,128)(2,1)S(1)}, bf16[8,2,64,256]{3,2,1,0:T(8,128)(2,1)S(1)}, u32[]{:S(2)}, u32[]{:S(2)}) collective-permute-start(bf16[8,2,64,256]{3,2,1,0:T(8,128)(2,1)S(1)} %get-tuple-element.40), channel_id=1, source_target_pairs={{0,31},{1,30},{2,29},{3,28},{4,27},{5,26},{6,25},{7,24},{8,23},{9,... | collective-permute-start | bytes 1572872 | tf_op jit(solution)/shard_map/ppermute | solution.py:63
  9.7 63.7 %collective-permute-start.13 = (bf16[16,64,256]{2,1,0:T(8,128)(2,1)S(1)}, bf16[16,64,256]{2,1,0:T(8,128)(2,1)S(1)}, u32[]{:S(2)}, u32[]{:S(2)}) collective-permute-start(bf16[16,64,256]{2,1,0:T(8,128)(2,1)S(1)} %get-tuple-element.45), channel_id=1, source_target_pairs={{0,4},{1,5},{4,8},{5,9},{6,2},{7,3},{8,12},{9,13},{10,6},{11,7},{1... | collective-permute-start | bytes 1572872 | tf_op jit(solution)/shard_map/ppermute | solution.py:63
  14.9 60.4 %collective-permute-start.14 = (bf16[16,64,256]{2,1,0:T(8,128)(2,1)S(1)}, bf16[16,64,256]{2,1,0:T(8,128)(2,1)S(1)}, u32[]{:S(2)}, u32[]{:S(2)}) collective-permute-start(bf16[16,64,256]{2,1,0:T(8,128)(2,1)S(1)} %get-tuple-element.46), channel_id=1, source_target_pairs={{2,6},{3,7},{4,0},{5,1},{6,10},{7,11},{8,4},{9,5},{10,14},{11,15},... | collective-permute-start | bytes 1572872 | tf_op jit(solution)/shard_map/ppermute | solution.py:63
  16.9 36.7 %collective-permute-start.2 = (bf16[4,2,64,256]{3,2,1,0:T(8,128)(2,1)S(1)}, bf16[4,2,64,256]{3,2,1,0:T(8,128)(2,1)S(1)}, u32[]{:S(2)}, u32[]{:S(2)}) collective-permute-start(bf16[4,2,64,256]{3,2,1,0:T(8,128)(2,1)S(1)} %get-tuple-element.31), channel_id=1, source_target_pairs={{0,31},{1,30},{2,29},{3,28},{4,27},{5,26},{6,25},{7,24},{8,23},{9,... | collective-permute-start | bytes 786440 | tf_op jit(solution)/shard_map/ppermute | solution.py:63
  31.1 8.7 %collective-permute-start.7 = (bf16[2,2,64,256]{3,2,1,0:T(8,128)(2,1)S(1)}, bf16[2,2,64,256]{3,2,1,0:T(8,128)(2,1)S(1)}, u32[]{:S(2)}, u32[]{:S(2)}) collective-permute-start(bf16[2,2,64,256]{3,2,1,0:T(8,128)(2,1)S(1)} %get-tuple-element.37), channel_id=1, source_target_pairs={{1,0},{2,1},{3,2},{5,4},{6,5},{7,6},{9,8},{10,9},{11,10},{13,12},{... | collective-permute-start | bytes 393224 | tf_op jit(solution)/shard_map/ppermute | solution.py:63
  39.8 18.3 %collective-permute-start.1 = (bf16[2,2,64,256]{3,2,1,0:T(8,128)(2,1)S(1)}, bf16[2,2,64,256]{3,2,1,0:T(8,128)(2,1)S(1)}, u32[]{:S(2)}, u32[]{:S(2)}) collective-permute-start(bf16[2,2,64,256]{3,2,1,0:T(8,128)(2,1)S(1)} %get-tuple-element.53), channel_id=1, source_target_pairs={{0,1},{1,2},{2,3},{4,5},{5,6},{6,7},{8,9},{9,10},{10,11},{12,13},{... | collective-permute-start | bytes 393224 | tf_op jit(solution)/shard_map/ppermute | solution.py:63
  53.6 26.6 %collective-permute-start.8 = (bf16[8,64,256]{2,1,0:T(8,128)(2,1)S(1)}, bf16[8,64,256]{2,1,0:T(8,128)(2,1)S(1)}, u32[]{:S(2)}, u32[]{:S(2)}) collective-permute-start(bf16[8,64,256]{2,1,0:T(8,128)(2,1)S(1)} %get-tuple-element.38), channel_id=1, source_target_pairs={{0,4},{1,5},{4,8},{5,9},{6,2},{7,3},{8,12},{9,13},{10,6},{11,7},{1... | collective-permute-start | bytes 786440 | tf_op jit(solution)/shard_map/ppermute | solution.py:63
  58.0 7.7 %collective-permute-start.3 = (bf16[2,2,64,256]{3,2,1,0:T(8,128)(2,1)S(1)}, bf16[2,2,64,256]{3,2,1,0:T(8,128)(2,1)S(1)}, u32[]{:S(2)}, u32[]{:S(2)}) collective-permute-start(bf16[2,2,64,256]{3,2,1,0:T(8,128)(2,1)S(1)} %get-tuple-element.52), channel_id=1, source_target_pairs={{1,0},{2,1},{3,2},{5,4},{6,5},{7,6},{9,8},{10,9},{11,10},{13,12},{... | collective-permute-start | bytes 393224 | tf_op jit(solution)/shard_map/ppermute | solution.py:63
  65.7 31.2 %collective-permute-start.9 = (bf16[8,64,256]{2,1,0:T(8,128)(2,1)S(1)}, bf16[8,64,256]{2,1,0:T(8,128)(2,1)S(1)}, u32[]{:S(2)}, u32[]{:S(2)}) collective-permute-start(bf16[8,64,256]{2,1,0:T(8,128)(2,1)S(1)} %get-tuple-element.39), channel_id=1, source_target_pairs={{2,6},{3,7},{4,0},{5,1},{6,10},{7,11},{8,4},{9,5},{10,14},{11,15},... | collective-permute-start | bytes 786440 | tf_op jit(solution)/shard_map/ppermute | solution.py:63
  68.6 28.3 %collective-permute-start.11 = (bf16[8,64,256]{2,1,0:T(8,128)(2,1)S(1)}, bf16[8,64,256]{2,1,0:T(8,128)(2,1)S(1)}, u32[]{:S(2)}, u32[]{:S(2)}) collective-permute-start(bf16[8,64,256]{2,1,0:T(8,128)(2,1)S(1)} %get-tuple-element.41), channel_id=1, source_target_pairs={{0,4},{1,5},{4,8},{5,9},{6,2},{7,3},{8,12},{9,13},{10,6},{11,7},{1... | collective-permute-start | bytes 786440 | tf_op jit(solution)/shard_map/ppermute | solution.py:63
  73.4 23.5 %collective-permute-start.12 = (bf16[8,64,256]{2,1,0:T(8,128)(2,1)S(1)}, bf16[8,64,256]{2,1,0:T(8,128)(2,1)S(1)}, u32[]{:S(2)}, u32[]{:S(2)}) collective-permute-start(bf16[8,64,256]{2,1,0:T(8,128)(2,1)S(1)} %get-tuple-element.42), channel_id=1, source_target_pairs={{2,6},{3,7},{4,0},{5,1},{6,10},{7,11},{8,4},{9,5},{10,14},{11,15},... | collective-permute-start | bytes 786440 | tf_op jit(solution)/shard_map/ppermute | solution.py:63
  75.4 25.2 %collective-permute-start.4 = (bf16[8,64,256]{2,1,0:T(8,128)(2,1)S(1)}, bf16[8,64,256]{2,1,0:T(8,128)(2,1)S(1)}, u32[]{:S(2)}, u32[]{:S(2)}) collective-permute-start(bf16[8,64,256]{2,1,0:T(8,128)(2,1)S(1)} %get-tuple-element.32), channel_id=1, source_target_pairs={{0,4},{1,5},{4,8},{5,9},{6,2},{7,3},{8,12},{9,13},{10,6},{11,7},{1... | collective-permute-start | bytes 786440 | tf_op jit(solution)/shard_map/ppermute | solution.py:63
  80.2 20.4 %collective-permute-start.5 = (bf16[8,64,256]{2,1,0:T(8,128)(2,1)S(1)}, bf16[8,64,256]{2,1,0:T(8,128)(2,1)S(1)}, u32[]{:S(2)}, u32[]{:S(2)}) collective-permute-start(bf16[8,64,256]{2,1,0:T(8,128)(2,1)S(1)} %get-tuple-element.33), channel_id=1, source_target_pairs={{2,6},{3,7},{4,0},{5,1},{6,10},{7,11},{8,4},{9,5},{10,14},{11,15},... | collective-permute-start | bytes 786440 | tf_op jit(solution)/shard_map/ppermute | solution.py:63
  82.1 1.0 copy-start.1
  100.6 23.6 %copy-start.2 = (s32[16,256]{1,0:T(8,128)S(1)}, s32[16,256]{1,0:T(8,128)}, u32[]{:S(2)}) copy-start(s32[16,256]{1,0:T(8,128)} %mask.1) | copy-start | bytes 49156
  107.4 13.5 %collective-permute-start.15 = (bf16[16,64,256]{2,1,0:T(8,128)(2,1)S(1)}, bf16[16,64,256]{2,1,0:T(8,128)(2,1)S(1)}, u32[]{:S(2)}, u32[]{:S(2)}) collective-permute-start(bf16[16,64,256]{2,1,0:T(8,128)(2,1)S(1)} %get-tuple-element.49), channel_id=1, source_target_pairs={{0,4},{1,5},{4,8},{5,9},{6,2},{7,3},{8,12},{9,13},{10,6},{11,7},{1... | collective-permute-start | bytes 1572872 | tf_op jit(solution)/shard_map/ppermute | solution.py:63
  112.2 12.0 %collective-permute-start.16 = (bf16[16,64,256]{2,1,0:T(8,128)(2,1)S(1)}, bf16[16,64,256]{2,1,0:T(8,128)(2,1)S(1)}, u32[]{:S(2)}, u32[]{:S(2)}) collective-permute-start(bf16[16,64,256]{2,1,0:T(8,128)(2,1)S(1)} %get-tuple-element.50), channel_id=1, source_target_pairs={{2,6},{3,7},{4,0},{5,1},{6,10},{7,11},{8,4},{9,5},{10,14},{11,15},... | collective-permute-start | bytes 1572872 | tf_op jit(solution)/shard_map/ppermute | solution.py:63

commit v5 on v4

--- a/solution.py
+++ b/solution.py
@@ -180,7 +180,9 @@
     )
 
 
-def prepare_kernel(natural, given, first_rows, last_rows, outer, middle, inner, spread, turned):
+def prepare_kernel(
+    natural, given, first_rows, last_rows, outer, middle, inner, spread, turned, staged, arrived
+):
     chans, layers, rows, depth = natural.shape
     flip = reversal(depth)
     signs = sign_rows(chans, chans)
@@ -188,8 +190,14 @@
     for ref in (outer, middle):
         groups.append((ref, start, ref.shape[0] // 2))
         start += ref.shape[0] // 2
+    copies = [
+        pltpu.make_async_copy(natural.at[:, x], staged.at[x], arrived.at[x]) for x in range(layers)
+    ]
+    for copy in copies:
+        copy.start()
     for x in range(layers):
-        whole = natural[:, x].reshape(chans * rows, depth)
+        copies[x].wait()
+        whole = staged[x].reshape(chans * rows, depth)
         mirrored = dot(whole, flip)
         whole = whole.astype(f32)
         for part in range(spread.shape[0]):
@@ -397,11 +405,8 @@
         field[target] = jnp.where(inside_y(target, span), value, 0.0).astype(bf16)
 
     def loop(count, first_target, k, t):
-        def body(y, carry):
+        for y in range(count):
             finish(first_target + y, k(y), t(y))
-            return carry
-
-        lax.fori_loop(0, count, body, 0, unroll=2)
 
     finish(0, top[1], virtual_top[1])
     y = 0
@@ -462,8 +467,8 @@
             )
 
 
-def own_gradient_kernel(weights, field, total, natural, spread):
-    chans, _, rows, _ = natural.shape
+def own_gradient_kernel(weights, field, given, mask, total, natural, spread):
+    chans, layers, rows, _ = natural.shape
     total[...] = jnp.zeros(total.shape, f32)
     add_own(
         weights,
@@ -478,28 +483,38 @@
     )
     from_rows(lambda y, x: field[y + 1, x, :chans].astype(f32), natural, spread)
 
-
-def update_kernel(partial, first, second, field, given, mask, natural, spread):
+    def body(y, carry):
+        keep = 1.0 - mask[pl.ds(y, 1)].astype(f32)
+        for x in range(layers):
+            part = slice(x * chans, (x + 1) * chans)
+            gradient = total[y, part] - field[y + 1, x, :chans].astype(f32)
+            total[y, part] = given[y, x].astype(f32) - step_size * keep * gradient
+        return carry
+
+    lax.fori_loop(0, rows, body, 0, unroll=2)
+
+
+def update_kernel(partial, first, second, mask, natural, spread):
     chans, layers, _, _ = natural.shape
     direct, _, _ = place_flags()
 
     def value(y, x):
-        gradient = partial[y, x * chans : (x + 1) * chans] - field[y + 1, x, :chans].astype(f32)
+        value = partial[y, x * chans : (x + 1) * chans]
+        keep = step_size * (1.0 - mask[pl.ds(y, 1)].astype(f32))
         if x == 0:
-            gradient += jnp.where(direct, first[y], second[y]).astype(f32)
+            value -= keep * jnp.where(direct, first[y], second[y]).astype(f32)
         if x == layers - 1:
-            gradient += jnp.where(direct, second[y], first[y]).astype(f32)
-        keep = 1.0 - mask[pl.ds(y, 1)].astype(f32)
-        return given[y, x].astype(f32) - step_size * keep * gradient
+            value -= keep * jnp.where(direct, second[y], first[y]).astype(f32)
+        return value
 
     from_rows(value, natural, spread)
 
 
-def call(kernel, shape, scratch, *args, reuse=None):
+def call(kernel, shape, scratch, *args, reuse=None, space=pltpu.VMEM):
     return pl.pallas_call(
         kernel,
         out_shape=shape,
-        in_specs=[IN_VMEM] * len(args),
+        in_specs=[pl.BlockSpec(memory_space=space)] * len(args),
         out_specs=jax.tree.map(lambda _: IN_VMEM, shape),
         input_output_aliases={} if reuse is None else {reuse: 0},
         scratch_shapes=scratch,
@@ -534,8 +549,14 @@
     given, head, tail, outer, middle, inner = call(
         prepare_kernel,
         (block(rows), block(2), block(2), block(2 * edge), block(2 * half), block(count)),
-        [spread, spread],
+        [
+            spread,
+            spread,
+            pltpu.VMEM((layers, chans, rows, depth), bf16),
+            pltpu.SemaphoreType.DMA((layers,)),
+        ],
         kspace,
+        space=pl.ANY,
     )
     outer = send(outer, to_mirror)
     given_sides = around_x(((0, 0, rows),), given)
@@ -591,9 +612,9 @@
         own_gradient_kernel,
         (like(rows, layers * chans, depth, dtype=f32), natural),
         [spread],
-        adjoint, field,
-    )
-    updated = call(update_kernel, natural, [spread], partial, first, second, field, given, mask)
+        adjoint, field, given, mask,
+    )
+    updated = call(update_kernel, natural, [spread], partial, first, second, mask)
     return updated, residual
 
 

time: 127 us -> 127 us (level)
  no operation moved by 1% of the time
where the time goes in v5:
time: 127 us; the launch traced here: 126 us
  starting transfers between devices  46.3 us (36%)
  waiting for transfers between devices  39.1 us (31%)
  Pallas kernels  37.6 us (30%)
  local copies, waits for them, and re-layouts  2.25 us (2%)
    ppermute x17, starting transfers between devices, send(): return lax.ppermute(value, AXES, pairs)  46.3 us
    ppermute x17, waiting for transfers between devices, send(): return lax.ppermute(value, AXES, pairs)  39.1 us
    pallas_call x14, Pallas kernels, call(): pl.pallas_call(kernel, out_shape=shape, in_specs=[pl.BlockSpec(memory_spa...  37.6 us
  transfers between devices with their start and end apart: 17, of which 5 were waited for; matrix products, arithmetic and copies ran while one was open for 0% of the time, Pallas kernels for 21%

profile of v5, /device:TPU:16, one launch (start us, length us, event | category | flops | bytes accessed | tf_op | source)
XLA Modules:
  0.0 126.2 jit_solution(16652334648331654744)
XLA Ops:
  0.6 1.2 copy-done
  1.9 1.7 %shard_map.51 = (bf16[16,2,64,256]{3,2,1,0:T(8,128)(2,1)S(1)}, bf16[2,2,64,256]{3,2,1,0:T(8,128)(2,1)S(1)}, bf16[2,2,64,256]{3,2,1,0:T(8,128)(2,1)S(1)}, bf16[4,...) custom-call(bf16[64,2,16,256]{3,2,1,0:T(8,128)(2,1)S(1)} %copy-done), custom_call_target="tpu_custom_call" | custom-call | tf_op jit(solution)/shard_map/pallas_call | solution.py:514
  3.5 1.8 %collective-permute-start = (bf16[4,2,64,256]{3,2,1,0:T(8,128)(2,1)S(1)}, bf16[4,2,64,256]{3,2,1,0:T(8,128)(2,1)S(1)}, u32[]{:S(2)}, u32[]{:S(2)}) collective-permute-start(bf16[4,2,64,256]{3,2,1,0:T(8,128)(2,1)S(1)} %get-tuple-element.30), channel_id=1, source_target_pairs={{0,31},{1,30},{2,29},{3,28},{4,27},{5,26},{6,25},{7,24},{8,23},{9,... | collective-permute-start | bytes 786440 | tf_op jit(solution)/shard_map/ppermute | solution.py:63
  5.4 2.4 %collective-permute-start.6 = (bf16[2,2,64,256]{3,2,1,0:T(8,128)(2,1)S(1)}, bf16[2,2,64,256]{3,2,1,0:T(8,128)(2,1)S(1)}, u32[]{:S(2)}, u32[]{:S(2)}) collective-permute-start(bf16[2,2,64,256]{3,2,1,0:T(8,128)(2,1)S(1)} %get-tuple-element.36), channel_id=1, source_target_pairs={{0,1},{1,2},{2,3},{4,5},{5,6},{6,7},{8,9},{9,10},{10,11},{12,13},{... | collective-permute-start | bytes 393224 | tf_op jit(solution)/shard_map/ppermute | solution.py:63
  7.8 0.7 collective-permute-start.10
  8.5 0.9 shard_map.55
  9.4 5.2 %collective-permute-start.13 = (bf16[16,64,256]{2,1,0:T(8,128)(2,1)S(1)}, bf16[16,64,256]{2,1,0:T(8,128)(2,1)S(1)}, u32[]{:S(2)}, u32[]{:S(2)}) collective-permute-start(bf16[16,64,256]{2,1,0:T(8,128)(2,1)S(1)} %get-tuple-element.45), channel_id=1, source_target_pairs={{0,4},{1,5},{4,8},{5,9},{6,2},{7,3},{8,12},{9,13},{10,6},{11,7},{1... | collective-permute-start | bytes 1572872 | tf_op jit(solution)/shard_map/ppermute | solution.py:63
  14.6 1.9 %collective-permute-start.14 = (bf16[16,64,256]{2,1,0:T(8,128)(2,1)S(1)}, bf16[16,64,256]{2,1,0:T(8,128)(2,1)S(1)}, u32[]{:S(2)}, u32[]{:S(2)}) collective-permute-start(bf16[16,64,256]{2,1,0:T(8,128)(2,1)S(1)} %get-tuple-element.46), channel_id=1, source_target_pairs={{2,6},{3,7},{4,0},{5,1},{6,10},{7,11},{8,4},{9,5},{10,14},{11,15},... | collective-permute-start | bytes 1572872 | tf_op jit(solution)/shard_map/ppermute | solution.py:63
  16.6 0.0 collective-permute-done.6.refs_0_.top
  16.6 2.0 %collective-permute-start.2 = (bf16[4,2,64,256]{3,2,1,0:T(8,128)(2,1)S(1)}, bf16[4,2,64,256]{3,2,1,0:T(8,128)(2,1)S(1)}, u32[]{:S(2)}, u32[]{:S(2)}) collective-permute-start(bf16[4,2,64,256]{3,2,1,0:T(8,128)(2,1)S(1)} %get-tuple-element.31), channel_id=1, source_target_pairs={{0,31},{1,30},{2,29},{3,28},{4,27},{5,26},{6,25},{7,24},{8,23},{9,... | collective-permute-start | bytes 786440 | tf_op jit(solution)/shard_map/ppermute | solution.py:63
  18.6 12.2 %collective-permute-done.refs_1_.outer.virtual_outer = bf16[4,2,64,256]{3,2,1,0:T(8,128)(2,1)S(1)} collective-permute-done((bf16[4,2,64,256]{3,2,1,0:T(8,128)(2,1)S(1)}, bf16[4,2,64,256]{3,2,1,0:T(8,128)(2,1)S(1)}, u32[]{:S(2)}, u32[]{:S(2)}) %collective-permute-start) | collective-permute-done | bytes 262176 | tf_op jit(solution)/shard_map/ppermute | solution.py:63
  30.8 1.3 %collective-permute-start.7 = (bf16[2,2,64,256]{3,2,1,0:T(8,128)(2,1)S(1)}, bf16[2,2,64,256]{3,2,1,0:T(8,128)(2,1)S(1)}, u32[]{:S(2)}, u32[]{:S(2)}) collective-permute-start(bf16[2,2,64,256]{3,2,1,0:T(8,128)(2,1)S(1)} %get-tuple-element.37), channel_id=1, source_target_pairs={{1,0},{2,1},{3,2},{5,4},{6,5},{7,6},{9,8},{10,9},{11,10},{13,12},{... | collective-permute-start | bytes 393224 | tf_op jit(solution)/shard_map/ppermute | solution.py:63
  32.1 7.4 %collective-permute-done.7.refs_2_.bottom = bf16[2,2,64,256]{3,2,1,0:T(8,128)(2,1)S(1)} collective-permute-done((bf16[2,2,64,256]{3,2,1,0:T(8,128)(2,1)S(1)}, bf16[2,2,64,256]{3,2,1,0:T(8,128)(2,1)S(1)}, u32[]{:S(2)}, u32[]{:S(2)}) %collective-permute-start.7) | collective-permute-done | bytes 131104 | tf_op jit(solution)/shard_map/ppermute | solution.py:63
  39.5 3.0 %collective-permute-start.1 = (bf16[2,2,64,256]{3,2,1,0:T(8,128)(2,1)S(1)}, bf16[2,2,64,256]{3,2,1,0:T(8,128)(2,1)S(1)}, u32[]{:S(2)}, u32[]{:S(2)}) collective-permute-start(bf16[2,2,64,256]{3,2,1,0:T(8,128)(2,1)S(1)} %get-tuple-element.53), channel_id=1, source_target_pairs={{0,1},{1,2},{2,3},{4,5},{5,6},{6,7},{8,9},{9,10},{10,11},{12,13},{... | collective-permute-start | bytes 393224 | tf_op jit(solution)/shard_map/ppermute | solution.py:63
  42.6 0.5 shard_map.53
  43.0 10.3 %collective-permute-done.2.refs_1_.inner.virtual_inner = bf16[4,2,64,256]{3,2,1,0:T(8,128)(2,1)S(1)} collective-permute-done((bf16[4,2,64,256]{3,2,1,0:T(8,128)(2,1)S(1)}, bf16[4,2,64,256]{3,2,1,0:T(8,128)(2,1)S(1)}, u32[]{:S(2)}, u32[]{:S(2)}) %collective-permute-start.2) | collective-permute-done | bytes 262176 | tf_op jit(solution)/shard_map/ppermute | solution.py:63
  53.3 4.4 %collective-permute-start.8 = (bf16[8,64,256]{2,1,0:T(8,128)(2,1)S(1)}, bf16[8,64,256]{2,1,0:T(8,128)(2,1)S(1)}, u32[]{:S(2)}, u32[]{:S(2)}) collective-permute-start(bf16[8,64,256]{2,1,0:T(8,128)(2,1)S(1)} %get-tuple-element.38), channel_id=1, source_target_pairs={{0,4},{1,5},{4,8},{5,9},{6,2},{7,3},{8,12},{9,13},{10,6},{11,7},{1... | collective-permute-start | bytes 786440 | tf_op jit(solution)/shard_map/ppermute | solution.py:63
  57.8 1.3 %collective-permute-start.3 = (bf16[2,2,64,256]{3,2,1,0:T(8,128)(2,1)S(1)}, bf16[2,2,64,256]{3,2,1,0:T(8,128)(2,1)S(1)}, u32[]{:S(2)}, u32[]{:S(2)}) collective-permute-start(bf16[2,2,64,256]{3,2,1,0:T(8,128)(2,1)S(1)} %get-tuple-element.52), channel_id=1, source_target_pairs={{1,0},{2,1},{3,2},{5,4},{6,5},{7,6},{9,8},{10,9},{11,10},{13,12},{... | collective-permute-start | bytes 393224 | tf_op jit(solution)/shard_map/ppermute | solution.py:63
  59.1 6.4 %collective-permute-done.3.refs_2_.virtual_bottom = bf16[2,2,64,256]{3,2,1,0:T(8,128)(2,1)S(1)} collective-permute-done((bf16[2,2,64,256]{3,2,1,0:T(8,128)(2,1)S(1)}, bf16[2,2,64,256]{3,2,1,0:T(8,128)(2,1)S(1)}, u32[]{:S(2)}, u32[]{:S(2)}) %collective-permute-start.3) | collective-permute-done | bytes 131104 | tf_op jit(solution)/shard_map/ppermute | solution.py:63
  65.4 1.9 %collective-permute-start.9 = (bf16[8,64,256]{2,1,0:T(8,128)(2,1)S(1)}, bf16[8,64,256]{2,1,0:T(8,128)(2,1)S(1)}, u32[]{:S(2)}, u32[]{:S(2)}) collective-permute-start(bf16[8,64,256]{2,1,0:T(8,128)(2,1)S(1)} %get-tuple-element.39), channel_id=1, source_target_pairs={{2,6},{3,7},{4,0},{5,1},{6,10},{7,11},{8,4},{9,5},{10,14},{11,15},... | collective-permute-start | bytes 786440 | tf_op jit(solution)/shard_map/ppermute | solution.py:63
  67.3 0.5 shard_map.52
  67.8 0.0 collective-permute-done.10.refs_0_.middle.virtual_middle
  67.8 0.5 shard_map.54
  68.3 4.8 %collective-permute-start.11 = (bf16[8,64,256]{2,1,0:T(8,128)(2,1)S(1)}, bf16[8,64,256]{2,1,0:T(8,128)(2,1)S(1)}, u32[]{:S(2)}, u32[]{:S(2)}) collective-permute-start(bf16[8,64,256]{2,1,0:T(8,128)(2,1)S(1)} %get-tuple-element.41), channel_id=1, source_target_pairs={{0,4},{1,5},{4,8},{5,9},{6,2},{7,3},{8,12},{9,13},{10,6},{11,7},{1... | collective-permute-start | bytes 786440 | tf_op jit(solution)/shard_map/ppermute | solution.py:63
  73.1 0.0 collective-permute-done.13.first
  73.1 1.9 %collective-permute-start.12 = (bf16[8,64,256]{2,1,0:T(8,128)(2,1)S(1)}, bf16[8,64,256]{2,1,0:T(8,128)(2,1)S(1)}, u32[]{:S(2)}, u32[]{:S(2)}) collective-permute-start(bf16[8,64,256]{2,1,0:T(8,128)(2,1)S(1)} %get-tuple-element.42), channel_id=1, source_target_pairs={{2,6},{3,7},{4,0},{5,1},{6,10},{7,11},{8,4},{9,5},{10,14},{11,15},... | collective-permute-start | bytes 786440 | tf_op jit(solution)/shard_map/ppermute | solution.py:63
  75.1 4.8 %collective-permute-start.4 = (bf16[8,64,256]{2,1,0:T(8,128)(2,1)S(1)}, bf16[8,64,256]{2,1,0:T(8,128)(2,1)S(1)}, u32[]{:S(2)}, u32[]{:S(2)}) collective-permute-start(bf16[8,64,256]{2,1,0:T(8,128)(2,1)S(1)} %get-tuple-element.32), channel_id=1, source_target_pairs={{0,4},{1,5},{4,8},{5,9},{6,2},{7,3},{8,12},{9,13},{10,6},{11,7},{1... | collective-permute-start | bytes 786440 | tf_op jit(solution)/shard_map/ppermute | solution.py:63
  79.9 1.9 %collective-permute-start.5 = (bf16[8,64,256]{2,1,0:T(8,128)(2,1)S(1)}, bf16[8,64,256]{2,1,0:T(8,128)(2,1)S(1)}, u32[]{:S(2)}, u32[]{:S(2)}) collective-permute-start(bf16[8,64,256]{2,1,0:T(8,128)(2,1)S(1)} %get-tuple-element.33), channel_id=1, source_target_pairs={{2,6},{3,7},{4,0},{5,1},{6,10},{7,11},{8,4},{9,5},{10,14},{11,15},... | collective-permute-start | bytes 786440 | tf_op jit(solution)/shard_map/ppermute | solution.py:63
  81.8 0.0 copy-start.1
  81.8 1.0 copy-done.1
  82.8 1.6 %shard_map.50 = (bf16[768,384]{1,0:T(8,128)(2,1)S(1)}, bf16[2,384,192]{2,1,0:T(8,128)(2,1)S(1)}, bf16[768,384]{1,0:T(8,128)(2,1)S(1)}, bf16[2,384,192]{2,1,0:T(8...) custom-call(bf16[3,3,3,64,128]{4,3,2,1,0:T(8,128)(2,1)S(1)} %copy-done.1), custom_call_target="tpu_custom_call" | custom-call | tf_op jit(solution)/shard_map/pallas_call | solution.py:514
  84.5 4.7 %shard_map.56.partial = f32[18,256,256]{2,1,0:T(8,128)S(1)} custom-call(bf16[768,384]{1,0:T(8,128)(2,1)S(1)} %get-tuple-element.43.weights.early, bf16[16,2,64,256]{3,2,1,0:T(8,128)(2,1)S(1)} %get-tuple-element.44.refs_0_.own.given), custom_call_target="tpu_custom_call" | custom-call | tf_op jit(solution)/shard_map/pallas_call | solution.py:514
  89.2 2.9 %shard_map.57.partial = f32[18,256,256]{2,1,0:T(8,128)S(1)} custom-call(bf16[2,384,192]{2,1,0:T(8,128)(2,1)S(1)} %get-tuple-element.35.sides.early_sides, bf16[16,64,256]{2,1,0:T(8,128)(2,1)S(1)} %collective-permute-done.13.first, bf16[16,64,256]{2,1,0:T(8,128)(2,1)S(1)} %collective-permute-done.14.second, ...), custom_call_target="tpu_custom_call", output_to_operand_aliasing={{}: (3, {})} | custom-call | tf_op jit(solution)/shard_map/pallas_call | solution.py:514
  92.0 1.9 %shard_map.58.partial = f32[18,256,256]{2,1,0:T(8,128)S(1)} custom-call(bf16[768,384]{1,0:T(8,128)(2,1)S(1)} %get-tuple-element.43.weights.early, bf16[768,384]{1,0:T(8,128)(2,1)S(1)} %get-tuple-element.34.late, bf16[2,2,64,256]{3,2,1,0:T(8,128)(2,1)S(1)} %collective-permute-done.6.refs_0_.top, ...), custom_call_target="tpu_custom_call", output_to_operand_aliasing={{}: (5, {})} | custom-call | tf_op jit(solution)/shard_map/pallas_call | solution.py:514
  93.9 2.7 %shard_map.59.partial = f32[18,256,256]{2,1,0:T(8,128)S(1)} custom-call(bf16[768,384]{1,0:T(8,128)(2,1)S(1)} %get-tuple-element.34.late, bf16[2,2,64,256]{3,2,1,0:T(8,128)(2,1)S(1)} %collective-permute-done.1.refs_0_.virtual_top, bf16[8,2,64,256]{3,2,1,0:T(8,128)(2,1)S(1)} %collective-permute-done.10.refs_0_.middle.virtual_middle, ...), custom_call_target="tpu_custom_call", output_to_operand_aliasing={{}: (4, {})} | custom-call | tf_op jit(solution)/shard_map/pallas_call | solution.py:514
  96.6 0.0 collective-permute-done.9.second_outer
  96.6 0.0 collective-permute-done.12.second_middle
  96.7 3.6 %shard_map.60.partial = f32[18,256,256]{2,1,0:T(8,128)S(1)} custom-call(bf16[768,384]{1,0:T(8,128)(2,1)S(1)} %get-tuple-element.34.late, bf16[2,384,192]{2,1,0:T(8,128)(2,1)S(1)} %get-tuple-element.35.sides.early_sides, bf16[2,384,192]{2,1,0:T(8,128)(2,1)S(1)} %get-tuple-element.28.late_sides.sides, ...), custom_call_target="tpu_custom_call", output_to_operand_aliasing={{}: (8, {})} | custom-call | tf_op jit(solution)/shard_map/pallas_call | solution.py:514
  100.3 0.0 copy-start.2
  100.3 0.0 collective-permute-done.4.first
  100.3 0.0 collective-permute-done.5.second
  100.3 6.8 %shard_map.61 = (f32[18,256,256]{2,1,0:T(8,128)S(1)}, bf16[18,2,128,256]{3,2,1,0:T(8,128)(2,1)S(1)}, bf16[16,64,256]{2,1,0:T(8,128)(2,1)S(1)}, bf16[16,64,256]{2,1,0:T(8,128)(2,1)S(1)}) custom-call(bf16[2,384,192]{2,1,0:T(8,128)(2,1)S(1)} %get-tuple-element.28.late_sides.sides, ...), custom_call_target="tpu_custom_call", output_to_operand_aliasing={{0}: (4, {})} | custom-call | tf_op jit(solution)/shard_map/pallas_call | solution.py:514
  107.1 4.8 %collective-permute-start.15 = (bf16[16,64,256]{2,1,0:T(8,128)(2,1)S(1)}, bf16[16,64,256]{2,1,0:T(8,128)(2,1)S(1)}, u32[]{:S(2)}, u32[]{:S(2)}) collective-permute-start(bf16[16,64,256]{2,1,0:T(8,128)(2,1)S(1)} %get-tuple-element.49), channel_id=1, source_target_pairs={{0,4},{1,5},{4,8},{5,9},{6,2},{7,3},{8,12},{9,13},{10,6},{11,7},{1... | collective-permute-start | bytes 1572872 | tf_op jit(solution)/shard_map/ppermute | solution.py:63
  111.9 1.9 %collective-permute-start.16 = (bf16[16,64,256]{2,1,0:T(8,128)(2,1)S(1)}, bf16[16,64,256]{2,1,0:T(8,128)(2,1)S(1)}, u32[]{:S(2)}, u32[]{:S(2)}) collective-permute-start(bf16[16,64,256]{2,1,0:T(8,128)(2,1)S(1)} %get-tuple-element.50), channel_id=1, source_target_pairs={{2,6},{3,7},{4,0},{5,1},{6,10},{7,11},{8,4},{9,5},{10,14},{11,15},... | collective-permute-start | bytes 1572872 | tf_op jit(solution)/shard_map/ppermute | solution.py:63
  113.8 7.2 %shard_map.62 = (f32[16,128,256]{2,1,0:T(8,128)S(1)}, bf16[64,2,16,256]{3,2,1,0:T(8,128)(2,1)}) custom-call(bf16[384,768]{1,0:T(8,128)(2,1)S(1)} %get-tuple-element.27.weights, bf16[18,2,128,256]{3,2,1,0:T(8,128)(2,1)S(1)} %get-tuple-element.47.field, bf16[16,2,64,256]{3,2,1,0:T(8,128)(2,1)S(1)} %get-tuple-element.44.refs_0_.own.given, s32[16,256]{1,0:T(8,128)S(1)} %copy-done.2), custom_call_target="tpu_custom_call" | custom-call | tf_op jit(solution)/shard_map/pallas_call | solution.py:514
  121.0 0.0 collective-permute-done.15.first
  121.0 2.9 %collective-permute-done.16.second = bf16[16,64,256]{2,1,0:T(8,128)(2,1)S(1)} collective-permute-done((bf16[16,64,256]{2,1,0:T(8,128)(2,1)S(1)}, bf16[16,64,256]{2,1,0:T(8,128)(2,1)S(1)}, u32[]{:S(2)}, u32[]{:S(2)}) %collective-permute-start.16) | collective-permute-done | bytes 524320 | tf_op jit(solution)/shard_map/ppermute | solution.py:63
  123.9 2.3 %shard_map.63 = bf16[64,2,16,256]{3,2,1,0:T(8,128)(2,1)} custom-call(f32[16,128,256]{2,1,0:T(8,128)S(1)} %get-tuple-element.48.partial, bf16[16,64,256]{2,1,0:T(8,128)(2,1)S(1)} %collective-permute-done.15.first, bf16[16,64,256]{2,1,0:T(8,128)(2,1)S(1)} %collective-permute-done.16.second, s32[16,256]{1,0:T(8,128)S(1)} %copy-done.2), custom_call_target="tpu_custom_call" | custom-call | tf_op jit(solution)/shard_map/pallas_call | solution.py:514
  (7 shorter events, 0.0 us)
Async XLA Ops:
  0.6 1.2 copy-start
  3.5 27.3 %collective-permute-start = (bf16[4,2,64,256]{3,2,1,0:T(8,128)(2,1)S(1)}, bf16[4,2,64,256]{3,2,1,0:T(8,128)(2,1)S(1)}, u32[]{:S(2)}, u32[]{:S(2)}) collective-permute-start(bf16[4,2,64,256]{3,2,1,0:T(8,128)(2,1)S(1)} %get-tuple-element.30), channel_id=1, source_target_pairs={{0,31},{1,30},{2,29},{3,28},{4,27},{5,26},{6,25},{7,24},{8,23},{9,... | collective-permute-start | bytes 786440 | tf_op jit(solution)/shard_map/ppermute | solution.py:63
  5.4 11.2 %collective-permute-start.6 = (bf16[2,2,64,256]{3,2,1,0:T(8,128)(2,1)S(1)}, bf16[2,2,64,256]{3,2,1,0:T(8,128)(2,1)S(1)}, u32[]{:S(2)}, u32[]{:S(2)}) collective-permute-start(bf16[2,2,64,256]{3,2,1,0:T(8,128)(2,1)S(1)} %get-tuple-element.36), channel_id=1, source_target_pairs={{0,1},{1,2},{2,3},{4,5},{5,6},{6,7},{8,9},{9,10},{10,11},{12,13},{... | collective-permute-start | bytes 393224 | tf_op jit(solution)/shard_map/ppermute | solution.py:63
  7.8 60.0 %collective-permute-start.10 = (bf16[8,2,64,256]{3,2,1,0:T(8,128)(2,1)S(1)}, bf16[8,2,64,256]{3,2,1,0:T(8,128)(2,1)S(1)}, u32[]{:S(2)}, u32[]{:S(2)}) collective-permute-start(bf16[8,2,64,256]{3,2,1,0:T(8,128)(2,1)S(1)} %get-tuple-element.40), channel_id=1, source_target_pairs={{0,31},{1,30},{2,29},{3,28},{4,27},{5,26},{6,25},{7,24},{8,23},{9,... | collective-permute-start | bytes 1572872 | tf_op jit(solution)/shard_map/ppermute | solution.py:63
  9.4 63.7 %collective-permute-start.13 = (bf16[16,64,256]{2,1,0:T(8,128)(2,1)S(1)}, bf16[16,64,256]{2,1,0:T(8,128)(2,1)S(1)}, u32[]{:S(2)}, u32[]{:S(2)}) collective-permute-start(bf16[16,64,256]{2,1,0:T(8,128)(2,1)S(1)} %get-tuple-element.45), channel_id=1, source_target_pairs={{0,4},{1,5},{4,8},{5,9},{6,2},{7,3},{8,12},{9,13},{10,6},{11,7},{1... | collective-permute-start | bytes 1572872 | tf_op jit(solution)/shard_map/ppermute | solution.py:63
  14.6 60.4 %collective-permute-start.14 = (bf16[16,64,256]{2,1,0:T(8,128)(2,1)S(1)}, bf16[16,64,256]{2,1,0:T(8,128)(2,1)S(1)}, u32[]{:S(2)}, u32[]{:S(2)}) collective-permute-start(bf16[16,64,256]{2,1,0:T(8,128)(2,1)S(1)} %get-tuple-element.46), channel_id=1, source_target_pairs={{2,6},{3,7},{4,0},{5,1},{6,10},{7,11},{8,4},{9,5},{10,14},{11,15},... | collective-permute-start | bytes 1572872 | tf_op jit(solution)/shard_map/ppermute | solution.py:63
  16.6 36.7 %collective-permute-start.2 = (bf16[4,2,64,256]{3,2,1,0:T(8,128)(2,1)S(1)}, bf16[4,2,64,256]{3,2,1,0:T(8,128)(2,1)S(1)}, u32[]{:S(2)}, u32[]{:S(2)}) collective-permute-start(bf16[4,2,64,256]{3,2,1,0:T(8,128)(2,1)S(1)} %get-tuple-element.31), channel_id=1, source_target_pairs={{0,31},{1,30},{2,29},{3,28},{4,27},{5,26},{6,25},{7,24},{8,23},{9,... | collective-permute-start | bytes 786440 | tf_op jit(solution)/shard_map/ppermute | solution.py:63
  30.8 8.7 %collective-permute-start.7 = (bf16[2,2,64,256]{3,2,1,0:T(8,128)(2,1)S(1)}, bf16[2,2,64,256]{3,2,1,0:T(8,128)(2,1)S(1)}, u32[]{:S(2)}, u32[]{:S(2)}) collective-permute-start(bf16[2,2,64,256]{3,2,1,0:T(8,128)(2,1)S(1)} %get-tuple-element.37), channel_id=1, source_target_pairs={{1,0},{2,1},{3,2},{5,4},{6,5},{7,6},{9,8},{10,9},{11,10},{13,12},{... | collective-permute-start | bytes 393224 | tf_op jit(solution)/shard_map/ppermute | solution.py:63
  39.5 18.3 %collective-permute-start.1 = (bf16[2,2,64,256]{3,2,1,0:T(8,128)(2,1)S(1)}, bf16[2,2,64,256]{3,2,1,0:T(8,128)(2,1)S(1)}, u32[]{:S(2)}, u32[]{:S(2)}) collective-permute-start(bf16[2,2,64,256]{3,2,1,0:T(8,128)(2,1)S(1)} %get-tuple-element.53), channel_id=1, source_target_pairs={{0,1},{1,2},{2,3},{4,5},{5,6},{6,7},{8,9},{9,10},{10,11},{12,13},{... | collective-permute-start | bytes 393224 | tf_op jit(solution)/shard_map/ppermute | solution.py:63
  53.3 26.6 %collective-permute-start.8 = (bf16[8,64,256]{2,1,0:T(8,128)(2,1)S(1)}, bf16[8,64,256]{2,1,0:T(8,128)(2,1)S(1)}, u32[]{:S(2)}, u32[]{:S(2)}) collective-permute-start(bf16[8,64,256]{2,1,0:T(8,128)(2,1)S(1)} %get-tuple-element.38), channel_id=1, source_target_pairs={{0,4},{1,5},{4,8},{5,9},{6,2},{7,3},{8,12},{9,13},{10,6},{11,7},{1... | collective-permute-start | bytes 786440 | tf_op jit(solution)/shard_map/ppermute | solution.py:63
  57.8 7.7 %collective-permute-start.3 = (bf16[2,2,64,256]{3,2,1,0:T(8,128)(2,1)S(1)}, bf16[2,2,64,256]{3,2,1,0:T(8,128)(2,1)S(1)}, u32[]{:S(2)}, u32[]{:S(2)}) collective-permute-start(bf16[2,2,64,256]{3,2,1,0:T(8,128)(2,1)S(1)} %get-tuple-element.52), channel_id=1, source_target_pairs={{1,0},{2,1},{3,2},{5,4},{6,5},{7,6},{9,8},{10,9},{11,10},{13,12},{... | collective-permute-start | bytes 393224 | tf_op jit(solution)/shard_map/ppermute | solution.py:63
  65.4 31.2 %collective-permute-start.9 = (bf16[8,64,256]{2,1,0:T(8,128)(2,1)S(1)}, bf16[8,64,256]{2,1,0:T(8,128)(2,1)S(1)}, u32[]{:S(2)}, u32[]{:S(2)}) collective-permute-start(bf16[8,64,256]{2,1,0:T(8,128)(2,1)S(1)} %get-tuple-element.39), channel_id=1, source_target_pairs={{2,6},{3,7},{4,0},{5,1},{6,10},{7,11},{8,4},{9,5},{10,14},{11,15},... | collective-permute-start | bytes 786440 | tf_op jit(solution)/shard_map/ppermute | solution.py:63
  68.3 28.3 %collective-permute-start.11 = (bf16[8,64,256]{2,1,0:T(8,128)(2,1)S(1)}, bf16[8,64,256]{2,1,0:T(8,128)(2,1)S(1)}, u32[]{:S(2)}, u32[]{:S(2)}) collective-permute-start(bf16[8,64,256]{2,1,0:T(8,128)(2,1)S(1)} %get-tuple-element.41), channel_id=1, source_target_pairs={{0,4},{1,5},{4,8},{5,9},{6,2},{7,3},{8,12},{9,13},{10,6},{11,7},{1... | collective-permute-start | bytes 786440 | tf_op jit(solution)/shard_map/ppermute | solution.py:63
  73.1 23.5 %collective-permute-start.12 = (bf16[8,64,256]{2,1,0:T(8,128)(2,1)S(1)}, bf16[8,64,256]{2,1,0:T(8,128)(2,1)S(1)}, u32[]{:S(2)}, u32[]{:S(2)}) collective-permute-start(bf16[8,64,256]{2,1,0:T(8,128)(2,1)S(1)} %get-tuple-element.42), channel_id=1, source_target_pairs={{2,6},{3,7},{4,0},{5,1},{6,10},{7,11},{8,4},{9,5},{10,14},{11,15},... | collective-permute-start | bytes 786440 | tf_op jit(solution)/shard_map/ppermute | solution.py:63
  75.1 25.2 %collective-permute-start.4 = (bf16[8,64,256]{2,1,0:T(8,128)(2,1)S(1)}, bf16[8,64,256]{2,1,0:T(8,128)(2,1)S(1)}, u32[]{:S(2)}, u32[]{:S(2)}) collective-permute-start(bf16[8,64,256]{2,1,0:T(8,128)(2,1)S(1)} %get-tuple-element.32), channel_id=1, source_target_pairs={{0,4},{1,5},{4,8},{5,9},{6,2},{7,3},{8,12},{9,13},{10,6},{11,7},{1... | collective-permute-start | bytes 786440 | tf_op jit(solution)/shard_map/ppermute | solution.py:63
  79.9 20.4 %collective-permute-start.5 = (bf16[8,64,256]{2,1,0:T(8,128)(2,1)S(1)}, bf16[8,64,256]{2,1,0:T(8,128)(2,1)S(1)}, u32[]{:S(2)}, u32[]{:S(2)}) collective-permute-start(bf16[8,64,256]{2,1,0:T(8,128)(2,1)S(1)} %get-tuple-element.33), channel_id=1, source_target_pairs={{2,6},{3,7},{4,0},{5,1},{6,10},{7,11},{8,4},{9,5},{10,14},{11,15},... | collective-permute-start | bytes 786440 | tf_op jit(solution)/shard_map/ppermute | solution.py:63
  81.8 1.0 copy-start.1
  100.3 13.6 %copy-start.2 = (s32[16,256]{1,0:T(8,128)S(1)}, s32[16,256]{1,0:T(8,128)}, u32[]{:S(2)}) copy-start(s32[16,256]{1,0:T(8,128)} %mask.3) | copy-start | bytes 49156
  107.1 13.9 %collective-permute-start.15 = (bf16[16,64,256]{2,1,0:T(8,128)(2,1)S(1)}, bf16[16,64,256]{2,1,0:T(8,128)(2,1)S(1)}, u32[]{:S(2)}, u32[]{:S(2)}) collective-permute-start(bf16[16,64,256]{2,1,0:T(8,128)(2,1)S(1)} %get-tuple-element.49), channel_id=1, source_target_pairs={{0,4},{1,5},{4,8},{5,9},{6,2},{7,3},{8,12},{9,13},{10,6},{11,7},{1... | collective-permute-start | bytes 1572872 | tf_op jit(solution)/shard_map/ppermute | solution.py:63
  111.9 12.0 %collective-permute-start.16 = (bf16[16,64,256]{2,1,0:T(8,128)(2,1)S(1)}, bf16[16,64,256]{2,1,0:T(8,128)(2,1)S(1)}, u32[]{:S(2)}, u32[]{:S(2)}) collective-permute-start(bf16[16,64,256]{2,1,0:T(8,128)(2,1)S(1)} %get-tuple-element.50), channel_id=1, source_target_pairs={{2,6},{3,7},{4,0},{5,1},{6,10},{7,11},{8,4},{9,5},{10,14},{11,15},... | collective-permute-start | bytes 1572872 | tf_op jit(solution)/shard_map/ppermute | solution.py:63
